TPU v7x, 128 devices: a whole 4x4x4 slice. The times are simulated.
128 devices in a mesh: cube: 8 (over x_lo, z), row: 4 (over x_hi, core), col: 4 (over y).
Axes of the slice: x: 4 (x_hi: 2, x_lo: 2; x = x_hi * 2 + x_lo), y: 4, z: 4, core: 2. Of those that a mesh axis runs over, the one named last changes fastest.
Arguments:
- child_update: float32 [32, 2, 4, 128, 128, 128], P(('cube', 'row'), None, None, None, 'col'), may hold values from -13 to 13
- child_map: int32 [2, 16384], replicated, may hold values from -1 to 16383, as said below
- parent_diag: float32 [16384], replicated, may hold values from 0.5 to 2
Outputs:
- updated: float32 [32, 4, 128, 128, 128], P(('cube', 'row'), None, None, 'col')
Inputs may be any that keep to these rules, and one draw needn't show every extreme that they name: `child_map`: for each child and each aligned block of 128 child rows, the live rows (entries other than -1) come first and map, strictly increasing, into the same aligned block of 128 parent rows; every block has at least one -1 entry and uses the last parent row of its block.
All inputs are finite; a program needn't handle non-finite values.
Results may differ from a plain program's by a relative error of at most 0.0001.
Values sent between devices are 32-bit elements; how exact they have to be, the bound alone decides.
A program may use at most 192 MiB of HBM per device.

v0:
```python
import jax
import jax.numpy as jnp
from jax import lax
from jax.sharding import PartitionSpec as P

K = 1024


def swapped(value, axis, distance):
    mask = 2**distance
    pairs = [(source, source ^ mask) for source in range(lax.axis_size(axis))]
    return lax.ppermute(value, axis, pairs)


def broadcast(value, axis, root):
    mine = lax.axis_index(axis) == root
    return lax.psum(jnp.where(mine, value, jnp.zeros_like(value)), axis)


def tile_onehot(values, targets):
    offsets = jnp.arange(values.shape[-1], dtype=jnp.int32)
    return (values[..., None, :] == targets[..., None, None] + offsets[:, None]).astype(jnp.float32)


def on_device(child_update, child_map, parent_diag):
    grid_size = lax.axis_size(("cube", "row"))
    half_grid = grid_size // 2
    columns = lax.axis_size("col")
    position = lax.axis_index(("cube", "row"))
    column_index = lax.axis_index("col")
    sibling = position // half_grid
    within = position % half_grid
    block = child_update[0]
    tile = block.shape[2]
    local_tiles = block.shape[1]
    local_cols = block.shape[3]
    own_map = lax.dynamic_index_in_dim(child_map, sibling, 0, keepdims=False)
    row_map = lax.dynamic_index_in_dim(
        own_map.reshape(local_tiles, 2, half_grid, tile), within, 2, keepdims=False
    )
    row_map = jnp.swapaxes(row_map, 0, 1)
    tile_rows = (
        grid_size * jnp.arange(local_tiles, dtype=jnp.int32)[None, :]
        + half_grid * jnp.arange(2, dtype=jnp.int32)[:, None]
        + within
    )
    row_onehot = tile_onehot(row_map, tile * tile_rows)
    col_map = lax.dynamic_index_in_dim(
        own_map.reshape(local_cols, columns, tile), column_index, 1, keepdims=False
    )
    tile_cols = columns * jnp.arange(local_cols, dtype=jnp.int32) + column_index
    col_onehot = tile_onehot(col_map, tile * tile_cols)
    placed = jnp.einsum("wjos,wjsmv->wjomv", row_onehot, block, precision=lax.Precision.HIGHEST)
    placed = jnp.einsum("wjomv,mpv->wjomp", placed, col_onehot, precision=lax.Precision.HIGHEST)
    kept = lax.dynamic_index_in_dim(placed, sibling, 0, keepdims=False)
    sent = lax.dynamic_index_in_dim(placed, 1 - sibling, 0, keepdims=False)
    arrived = swapped(sent, ("cube", "row"), half_grid.bit_length() - 1)
    global_rows = (
        tile * (grid_size * jnp.arange(local_tiles, dtype=jnp.int32)[:, None] + position)
        + jnp.arange(tile, dtype=jnp.int32)[None, :]
    )
    global_cols = tile * tile_cols[:, None] + jnp.arange(tile, dtype=jnp.int32)[None, :]
    diag_values = lax.dynamic_index_in_dim(
        parent_diag.reshape(local_tiles, grid_size, tile), position, 1, keepdims=False
    )
    on_diagonal = global_rows[:, :, None, None] == global_cols[None, None, :, :]
    front = kept + arrived + jnp.where(on_diagonal, diag_values[:, :, None, None], 0.0)
    panel_local = K // (tile * columns)
    panel_piece = front[:, :, :panel_local, :][:, :, :, None, :]
    panel_rows = lax.all_gather(panel_piece, "col", axis=3, tiled=True).reshape(
        local_tiles, tile, K
    )
    first_tile = panel_rows[0]
    pivot_count = K // tile
    pieces = [
        broadcast(first_tile, ("cube", "row"), root_index) for root_index in range(pivot_count)
    ]
    pivot_block = jnp.concatenate(pieces, axis=0)
    factor = jnp.linalg.cholesky(pivot_block)
    count = panel_rows.shape[0]
    flat = panel_rows.reshape(count * tile, K)
    solved_flat = jax.scipy.linalg.solve_triangular(factor, flat.T, lower=True).T
    solved = solved_flat.reshape(count, tile, K)
    diagonal = broadcast(solved, "row", column_index)
    gathered = lax.all_gather(diagonal[None], "cube", axis=0, tiled=True)
    update = jnp.einsum("rsk,cjvk->rsjcv", solved, gathered, precision=lax.Precision.HIGHEST)
    update = update.reshape(local_tiles, tile, local_cols, tile)
    trailing = front - update
    panel_cols = lax.dynamic_index_in_dim(
        solved.reshape(local_tiles, tile, panel_local, columns, tile),
        column_index,
        3,
        keepdims=False,
    )
    result = jnp.concatenate([panel_cols, trailing[:, :, panel_local:]], axis=2)
    return result[None]


def solution(mesh):
    return jax.shard_map(
        on_device,
        mesh=mesh,
        in_specs=(P(("cube", "row"), None, None, None, "col", None), P(), P()),
        out_specs=P(("cube", "row"), None, None, "col", None),
        check_vma=False,
    )
```

profile of v0, /device:TPU:1, one launch (start us, length us, event | category | flops | bytes accessed | tf_op | source)
XLA Modules:
  0.0 1053.8 jit_solution(11002890170687136967)
XLA Ops:
  7.6 26.4 %fusion.2 = f32[2,4,128,32,128]{4,2,1,0,3:T(8,128)} fusion(f32[2,4,128,32,128]{4,3,2,1,0:T(8,128)} %bitcast.172, s32[2,4,128]{2,1,0:T(4,128)S(1)} %iota_add_fusion.1, s32[2,4,128]{2,1,0:T(4,128)S(1)} %copy.31), kind=kOutput, calls=%fused_computation.4 | convolution fusion | flops 6442582016 | bytes 33562624 | tf_op jit(solution)/shard_map/wjos,wjsmv->wjomv/dot_general | solution.py:53
  34.0 15.8 %fusion.10 = f32[32,128,2,4,128]{4,1,3,2,0:T(8,128)} fusion(f32[2,4,128,32,128]{4,2,1,0,3:T(8,128)} %fusion.2, s32[32,128]{1,0:T(8,128)S(1)} %iota_add_fusion, s32[32,128]{1,0:T(8,128)S(1)} %bitcast.197), kind=kOutput, calls=%fused_computation.19 | convolution fusion | flops 6442975232 | bytes 33587200 | tf_op jit(solution)/shard_map/wjomv,mpv->wjomp/dot_general | solution.py:54
  49.8 7.9 dynamic-slice_bitcast_fusion
  57.7 2.0 collective-permute-start
  60.6 179.3 %collective-permute-done = f32[4,128,32,128]{1,3,0,2:T(8,128)} collective-permute-done((f32[4,128,32,128]{1,3,0,2:T(8,128)}, f32[4,128,32,128]{1,3,0,2:T(8,128)}, u32[]{:S(2)}, u32[]{:S(2)}) %collective-permute-start) | collective-permute-done | bytes 8388640 | tf_op jit(solution)/shard_map/ppermute | solution.py:12
  239.8 7.0 fusion.4
  246.8 3.4 copy-done.2
  251.1 34.3 %all-gather.6.cloned.1.call-done = f32[4,128,2,512]{1,3,0,2:T(8,128)} async-done(((f32[4,128,2,128]{1,3,0,2:T(8,128)}), f32[4,128,2,512]{1,3,0,2:T(8,128)}) %all-gather.6.cloned.1.call-update) | async-done | bytes 2097168 | tf_op jit(solution)/shard_map/all_gather | solution.py:70
  285.5 3.2 slice_select_fusion.7
  291.7 111.1 %all-reduce.7.cloned.1.call-done = (f32[128,1024]{0,1:T(8,128)}, f32[128,1024]{0,1:T(8,128)}, f32[128,1024]{0,1:T(8,128)}, f32[128,1024]{0,1:T(8,128)}, f32[128,...) async-done(((f32[128,1024]{0,1:T(8,128)}, f32[128,1024]{0,1:T(8,128)}, f32[128,1024]{0,1:T(8,128)}, f32[128,1024]{0,1:T(8,128)}, ...) | async-done | bytes 4194320 | tf_op jit(solution)/shard_map/psum | solution.py:17
  402.8 2.1 constant_dynamic-update-slice_fusion.7
  404.9 1.9 constant_dynamic-update-slice_fusion.6
  406.9 1.9 constant_dynamic-update-slice_fusion.5
  408.8 1.9 constant_dynamic-update-slice_fusion.4
  414.2 5.7 copy.34
  419.9 4.4 fusion.5
  424.3 1.9 copy-done.3
  426.3 11.7 %cholesky.223 = f32[128,128]{1,0:T(8,128)S(1)} custom-call(f32[128,128]{1,0:T(8,128)S(1)} %cholesky.580), custom_call_target="Cholesky" | custom-call | tf_op jit(solution)/shard_map/jit(cholesky)/cholesky | solution.py:79
  438.0 9.8 custom-call.63
  447.8 2.5 cholesky.255
  450.3 2.4 constant_dynamic-update-slice_fusion.33
  454.3 11.9 %cholesky.244 = f32[128,128]{1,0:T(8,128)S(1)} custom-call(f32[128,128]{1,0:T(8,128)S(1)} %cholesky.584), custom_call_target="Cholesky" | custom-call | tf_op jit(solution)/shard_map/jit(cholesky)/cholesky | solution.py:79
  466.8 9.8 custom-call.64
  477.8 2.1 convolution_subtract_fusion.1
  479.9 11.7 %cholesky.468 = f32[128,128]{1,0:T(8,128)S(1)} custom-call(f32[128,128]{1,0:T(8,128)S(1)} %cholesky.589), custom_call_target="Cholesky" | custom-call | tf_op jit(solution)/shard_map/jit(cholesky)/cholesky | solution.py:79
  493.0 9.8 custom-call.65
  504.0 2.3 convolution_subtract_fusion.2
  506.3 11.9 %cholesky.487 = f32[128,128]{1,0:T(8,128)S(1)} custom-call(f32[128,128]{1,0:T(8,128)S(1)} %cholesky.594), custom_call_target="Cholesky" | custom-call | tf_op jit(solution)/shard_map/jit(cholesky)/cholesky | solution.py:79
  519.5 9.8 custom-call.66
  530.4 2.3 convolution_subtract_fusion.10
  532.7 11.7 %cholesky.506 = f32[128,128]{1,0:T(8,128)S(1)} custom-call(f32[128,128]{1,0:T(8,128)S(1)} %cholesky.599), custom_call_target="Cholesky" | custom-call | tf_op jit(solution)/shard_map/jit(cholesky)/cholesky | solution.py:79
  545.8 10.2 custom-call.67
  557.0 2.3 convolution_subtract_fusion.11
  559.3 11.7 %cholesky.526 = f32[128,128]{1,0:T(8,128)S(1)} custom-call(f32[128,128]{1,0:T(8,128)S(1)} %cholesky.604), custom_call_target="Cholesky" | custom-call | tf_op jit(solution)/shard_map/jit(cholesky)/cholesky | solution.py:79
  572.3 9.8 custom-call.68
  583.1 2.0 convolution_subtract_fusion.12
  585.1 11.9 %cholesky.546 = f32[128,128]{1,0:T(8,128)S(1)} custom-call(f32[128,128]{1,0:T(8,128)S(1)} %cholesky.609), custom_call_target="Cholesky" | custom-call | tf_op jit(solution)/shard_map/jit(cholesky)/cholesky | solution.py:79
  598.3 9.8 custom-call.69
  608.9 1.8 convolution_subtract_fusion.13
  610.7 11.7 %cholesky.564 = f32[128,128]{1,0:T(8,128)S(1)} custom-call(f32[128,128]{1,0:T(8,128)S(1)} %convolution_subtract_fusion.13), custom_call_target="Cholesky" | custom-call | tf_op jit(solution)/shard_map/jit(cholesky)/cholesky | solution.py:79
  629.5 4.8 select_select_fusion
  634.3 22.8 %while.1 = (s32[]{:T(128)}, f32[1024,1024]{1,0:T(8,128)}, s32[8,2]{0,1:T(2,128)S(1)}, f32[8,128,128]{2,1,0:T(8,128)S(1)}, s32[]{:T(128)}) while((s32[]{:T(128)}, f32[1024,1024]{1,0:T(8,128)}, s32[8,2]{0,1:T(2,128)S(1)}, f32[8,128,128]{2,1,0:T(8,128)S(1)}, s32[]{:T(128)}) %tuple.64), condition=%wide.while_cond, body=%wide.while_body.sunk | while | flops 2 | bytes 131189 | solution.py:82
  634.9 2.2 bitcast_dynamic-update-slice_fusion.2
  637.7 2.2 bitcast_dynamic-update-slice_fusion.2
  640.6 2.2 bitcast_dynamic-update-slice_fusion.2
  643.5 2.2 bitcast_dynamic-update-slice_fusion.2
  646.3 2.2 bitcast_dynamic-update-slice_fusion.2
  649.2 2.2 bitcast_dynamic-update-slice_fusion.2
  652.1 2.2 bitcast_dynamic-update-slice_fusion.2
  654.9 2.2 bitcast_dynamic-update-slice_fusion.2
  657.1 78.8 %custom-call.70 = f32[8,128,128]{1,2,0:T(8,128)S(1)} custom-call(f32[8,128,128]{2,1,0:T(8,128)S(1)} %get-tuple-element.12), custom_call_target="InvertDiagBlocksLowerTriangular" | custom-call | tf_op jit(solution)/shard_map/jit(_solve_triangular)/triangular_solve | solution.py:82
  741.3 1.7 convolution_subtract_fusion.8
  745.6 1.9 convolution_subtract_fusion.4
  747.9 2.0 convolution_subtract_fusion.7
  750.4 2.2 convolution_subtract_fusion.3
  753.0 1.8 reshape.256
  754.8 2.9 copy.38
  759.5 60.0 %all-reduce.5.cloned.1.call-done = f32[1,4,128,1024]{3,2,1,0:T(8,128)} async-done(((f32[1,4,128,1024]{3,2,1,0:T(8,128)}), f32[1,4,128,1024]{3,2,1,0:T(8,128)}) %all-reduce.5.cloned.1.call-update) | async-done | bytes 2097168 | tf_op jit(solution)/shard_map/psum | solution.py:17
  819.5 2.0 reshape_reshape.7
  822.6 167.9 %all-gather.4.cloned.1.call-done = f32[8,4,128,1024]{3,2,1,0:T(8,128)} async-done(((f32[1,4,128,1024]{3,2,1,0:T(8,128)}), f32[8,4,128,1024]{3,2,1,0:T(8,128)}) %all-gather.4.cloned.1.call-update) | async-done | bytes 16777232 | tf_op jit(solution)/shard_map/all_gather | solution.py:85
  990.5 29.7 %fusion.6 = f32[4,128,4,8,128]{1,4,0,2,3:T(8,128)S(1)} fusion(f32[8,4,128,1024]{3,2,1,0:T(8,128)} %all-gather.4.cloned.1.call-done, f32[4,128,1024,1,1]{1,0,2,4,3:T(4,128)} %bitcast.176), kind=kOutput, calls=%fused_computation.15 | convolution fusion | flops 25769803776 | bytes 27262976 | tf_op jit(solution)/shard_map/rsk,cjvk->rsjcv/dot_general | solution.py:86
  1020.8 8.2 slice_subtract_fusion
  1028.9 7.6 maximum_bitcast_fusion
  1036.5 10.3 copy.41
  (109 shorter events, 43.9 us)
Async XLA Ops:
  6.5 0.9 copy-start
  6.5 278.9 %all-gather.6.cloned.1.call-start = ((), (), s32[]{:S(2)}) async-start(), calls=%async_computation.2 | async-start | bytes 2621440 | tf_op jit(solution)/shard_map/all_gather | solution.py:70
  57.7 182.1 %collective-permute-start = (f32[4,128,32,128]{1,3,0,2:T(8,128)}, f32[4,128,32,128]{1,3,0,2:T(8,128)}, u32[]{:S(2)}, u32[]{:S(2)}) collective-permute-start(f32[4,128,32,128]{1,3,0,2:T(8,128)} %dynamic-slice_bitcast_fusion), channel_id=1, source_target_pairs={{0,64},{4,68},{8,72},{12,76},{16,80},{20,84},{24,88},{28,92},{32,9... | collective-permute-start | bytes 25165832 | tf_op jit(solution)/shard_map/ppermute | solution.py:12
  246.8 3.4 copy-start.2
  251.0 151.8 %all-reduce.7.cloned.1.call-start = ((), (), s32[]{:S(2)}) async-start(), calls=%async_computation.3 | async-start | bytes 8388608 | tf_op jit(solution)/shard_map/psum | solution.py:17
  285.5 3.3 copy-start.5
  288.7 530.8 %all-reduce.5.cloned.1.call-start = ((), (), s32[]{:S(2)}) async-start(), calls=%async_computation | async-start | bytes 4194304 | tf_op jit(solution)/shard_map/psum | solution.py:17
  402.8 7.9 copy-start.9
  402.8 8.7 copy-start.8
  402.8 9.6 copy-start.7
  402.8 10.5 copy-start.6
  424.3 1.9 copy-start.3
  737.3 6.1 copy-start.4
  759.4 231.0 %all-gather.4.cloned.1.call-start = ((), (), s32[]{:S(2)}) async-start(), calls=%async_computation.1 | async-start | bytes 18874368 | tf_op jit(solution)/shard_map/all_gather | solution.py:85
  1036.5 10.3 copy-start.1
Sparse Core Ops, SparseCore 0:
  251.2 34.2 all-gather.5
  289.7 113.0 all-reduce.6
  759.5 59.8 all-reduce.4
  820.9 169.4 all-gather.3
where the time goes:
time: 1060 us; the launch traced here: 1050 us
  waiting for transfers between devices  553 us (52%)
  other arithmetic  288 us (27%)
  matrix products  112 us (11%)
  local copies, waits for them, and re-layouts  79.4 us (7%)
  between operations  19.1 us (2%)
    ppermute x1, waiting for transfers between devices, swapped(): return lax.ppermute(value, axis, pairs)  179 us
    another operation x30, other arithmetic, on_device(): factor = jnp.linalg.cholesky(pivot_block)  172 us
    psum x2, waiting for transfers between devices, broadcast(): return lax.psum(jnp.where(mine, value, jnp.zeros_like(value)), axis)  171 us
    all_gather x1, waiting for transfers between devices, on_device(): gathered = lax.all_gather(diagonal[None], 'cube', axis=0, tiled=True)  168 us
    another operation x3, other arithmetic, on_device(): jax.scipy.linalg.solve_triangular(factor, flat.T, lower=True)  83.6 us
    all_gather x1, waiting for transfers between devices, on_device(): lax.all_gather(panel_piece, 'col', axis=3, tiled=True)  34.3 us
    dot_general x1, matrix products, on_device(): jnp.einsum('rsk,cjvk->rsjcv', solved, gathered, precision=lax.Precision.H...  29.7 us
    dot_general x1, matrix products, on_device(): jnp.einsum('wjos,wjsmv->wjomv', row_onehot, block, precision=lax.Precisio...  26.4 us
  transfers between devices with their start and end apart: 5, of which 5 were waited for; matrix products, arithmetic and copies ran while one was open for 1% of the time, Pallas kernels for 0%

commit v1 on v0

v1 whole, which is shorter than its diff:
```python
import functools

import jax
import jax.numpy as jnp
from jax import lax
from jax.experimental import pallas as pl
from jax.experimental.pallas import tpu as pltpu
from jax.sharding import PartitionSpec as P

K = 1024
TB = 128
HI = lax.Precision.HIGHEST
F32 = jnp.float32
MESH = pl.DeviceIdType.MESH
VMEM = pl.BlockSpec(memory_space=pltpu.VMEM)
SMEM = pl.BlockSpec(memory_space=pltpu.SMEM)


def nt(a, b):
    return lax.dot_general(
        a, b, (((1,), (1,)), ((), ())), precision=HI, preferred_element_type=F32
    )


def nn(a, b):
    return lax.dot_general(
        a, b, (((1,), (0,)), ((), ())), precision=HI, preferred_element_type=F32
    )


def place_kernel(raw_ref, got_ref, rmap_ref, cmap_ref, diag_ref, out_ref):
    sub = lax.broadcasted_iota(jnp.int32, (TB, TB), 0)
    lane = lax.broadcasted_iota(jnp.int32, (TB, TB), 1)
    tiles = rmap_ref.shape[1]
    for v in range(2):
        cols = [
            nt(ref[v], (sub == cmap_ref[t, v : v + 1, :]).astype(F32))
            for t, ref in enumerate((raw_ref, got_ref))
        ]
        for j in range(tiles):
            rows = slice(j * TB, (j + 1) * TB)
            total = jnp.where(sub == lane, diag_ref[v * tiles + j : v * tiles + j + 1, :], 0.0)
            for t in range(2):
                hot = (sub == rmap_ref[t, j : j + 1, :]).astype(F32)
                total += nn(hot, cols[t][rows, :])
            out_ref[v, rows, :] = total


def pivot_kernel(piece_ref, out_ref, send, recv, local):
    cube, row, col = lax.axis_index("cube"), lax.axis_index("row"), lax.axis_index("col")
    z, near = lax.rem(cube, 4), cube < 4
    core = lax.rem(row, 2)
    at = lambda cu, ro, co: {"cube": cu, "row": ro, "col": co}
    mates = [at((cube - z) + lax.rem(z + d, 4), row, col) for d in (1, 2, 3)]
    across = [
        at(lax.rem(cube + 4, 8), row, col),
        at(cube, lax.rem(row + 2, 4), col),
        at(lax.rem(cube + 4, 8), lax.rem(row + 2, 4), col),
    ]
    up, down = lax.rem(col + 1, 4), lax.rem(col + 3, 4)
    sides = [at(cube, row, up), at(cube, row, down)]
    other = at(cube, row + 1 - 2 * core, col)
    barrier = pltpu.get_barrier_semaphore()
    for peer in mates + across + sides + [other]:
        pl.semaphore_signal(barrier, inc=1, device_id=peer, device_id_type=MESH)
    pl.semaphore_wait(barrier, 9)

    def copy(c, p, slot, peer):
        return pltpu.make_async_remote_copy(
            src_ref=out_ref.at[c, p],
            dst_ref=out_ref.at[c, p],
            send_sem=send.at[slot],
            recv_sem=recv.at[c, p],
            device_id=peer,
            device_id_type=MESH,
        )

    mine = lax.rem(cube, 2) * 4 + row
    source = cube < 2

    @pl.when(source)
    def _():
        own = pltpu.make_async_copy(piece_ref, out_ref.at[col, mine], local)
        own.start()
        own.wait()
        for i, peer in enumerate(mates):
            copy(col, mine, i, peer).start()

    for zz in range(2):
        p = zz * 4 + row

        @pl.when(near)
        def _():
            @pl.when(z != zz)
            def _():
                copy(col, p, 0, other).wait_recv()

            for i, peer in enumerate(across):
                copy(col, p, 3 + 3 * zz + i, peer).start()

    half = row // 2
    for zz in range(2):
        for hh in range(2):
            p = zz * 4 + hh * 2 + core
            n = zz * 2 + hh

            @pl.when(jnp.logical_or(jnp.logical_not(near), half != hh))
            def _():
                copy(col, p, 0, other).wait_recv()

            copy(col, p, 9 + n, sides[0]).start()
            copy(col, p, 13 + n, sides[1]).start()
            copy(col, p, 17 + n, other).start()
    for zz in range(2):
        for hh in range(2):
            p = zz * 4 + hh * 2 + core
            n = zz * 2 + hh
            copy(down, p, 0, other).wait_recv()
            copy(down, p, 21 + n, other).start()

            @pl.when(core == 0)
            def _():
                copy(down, p, 25 + n, sides[0]).start()

            copy(up, p, 0, other).wait_recv()
            copy(up, p, 29 + n, other).start()

            @pl.when(core == 1)
            def _():
                copy(up, p, 25 + n, sides[1]).start()

    far = lax.rem(col + 2, 4)
    for zz in range(2):
        for hh in range(2):
            p = zz * 4 + hh * 2 + core
            copy(far, p, 0, other).wait_recv()
            copy(far, p, 33 + zz * 2 + hh, other).start()
    for c in range(4):
        for zz in range(2):
            for hh in range(2):
                copy(c, zz * 4 + hh * 2 + 1 - core, 0, other).wait_recv()

    @pl.when(source)
    def _():
        for i in range(3):
            copy(col, mine, i, other).wait_send()

    @pl.when(near)
    def _():
        for i in range(3, 9):
            copy(col, mine, i, other).wait_send()

    for i in range(9, 37):
        copy(col, mine, i, other).wait_send()


def leaf(d_ref, li_ref):
    a_rows = [d_ref[8 * g : 8 * g + 8, :] for g in range(16)]
    lane = lax.broadcasted_iota(jnp.int32, (8, TB), 1)
    sub = lax.broadcasted_iota(jnp.int32, (8, TB), 0)
    b_rows = [(lane == sub + 8 * g).astype(F32) for g in range(16)]
    wide = lambda x: jnp.broadcast_to(x, (8, TB))
    for g0 in range(16):
        j = 8 * g0
        c = [wide(a_rows[g0][:, j + q : j + q + 1]) for q in range(8)]
        e = [[wide(c[q][i : i + 1, :]) if i >= q else None for q in range(8)] for i in range(8)]
        a = [wide(a_rows[g0][q : q + 1, :]) for q in range(8)]
        b = [wide(b_rows[g0][q : q + 1, :]) for q in range(8)]
        more = g0 + 1 < 16
        if more:
            m = [wide(a_rows[g0 + 1][:, j + q : j + q + 1]) for q in range(8)]
        s, t = [None] * 8, [None] * 8
        low = [[None] * 8 for _ in range(8)]
        for q in range(8):
            inv = 1.0 / e[q][q]
            s[q], t[q] = a[q] * inv, b[q] * inv
            for i in range(q + 1, 8):
                low[i][q] = e[i][q] * inv
            for i in range(q + 1, 8):
                for p in range(q + 1, i + 1):
                    e[i][p] = e[i][p] - low[i][q] * e[p][q]
            for i in range(q + 1, 8):
                a[i] = a[i] - low[i][q] * a[q]
                b[i] = b[i] - low[i][q] * b[q]
                if more:
                    m[i] = m[i] - low[i][q] * m[q]
            if more:
                a_rows[g0 + 1] = a_rows[g0 + 1] - m[q] * s[q]
                b_rows[g0 + 1] = b_rows[g0 + 1] - m[q] * t[q]
            li_ref[j + q : j + q + 1, :] = (b[q] * lax.rsqrt(e[q][q]))[0:1, :]
        if g0 + 2 < 16:
            for q in range(7, -1, -1):
                for i in range(q + 1, 8):
                    s[q] = s[q] - low[i][q] * s[i]
                    t[q] = t[q] - low[i][q] * t[i]
            for g in range(g0 + 2, 16):
                m = [wide(a_rows[g][:, j + q : j + q + 1]) for q in range(8)]
                da, db = m[0] * s[0], m[0] * t[0]
                for q in range(1, 8):
                    da, db = da + m[q] * s[q], db + m[q] * t[q]
                a_rows[g] = a_rows[g] - da
                b_rows[g] = b_rows[g] - db


def factor_kernel(col_ref, s_ref, a_ref, y_ref, x_ref, m_ref, li_ref, d_ref):
    blocks = K // TB
    for c in range(4):
        for v in range(2):
            u = 4 * v + c
            for p in range(blocks):
                if p >= u:
                    m_ref[p * TB : (p + 1) * TB, u * TB : (u + 1) * TB] = s_ref[c, p, v]
                else:
                    m_ref[p * TB : (p + 1) * TB, u * TB : (u + 1) * TB] = jnp.zeros((TB, TB), F32)
            m_ref[K:, u * TB : (u + 1) * TB] = a_ref[c, v]

    def step(k, _):
        o = pl.multiple_of(k * TB, TB)
        here = pl.ds(o, TB)
        d_ref[...] = m_ref[here, here]
        leaf(d_ref, li_ref.at[k])
        m_ref[:, here] = nt(m_ref[:, here], li_ref[k])

        def update(j, _):
            q = pl.multiple_of(j * TB, TB)
            there = pl.ds(q, TB)
            m_ref[:, there] = m_ref[:, there] - nt(m_ref[:, here], m_ref[there, here])
            return 0

        lax.fori_loop(k + 1, blocks, update, 0)
        return 0

    lax.fori_loop(0, blocks, step, 0)
    col = col_ref[0]
    for v in range(2):
        y_ref[v] = m_ref[K:, pl.ds(pl.multiple_of((4 * v + col) * TB, TB), TB)]

    def back(i, _):
        k = blocks - 1 - i
        o = pl.multiple_of(k * TB, TB)
        here = pl.ds(o, TB)
        x = nn(m_ref[K:, here], li_ref[k])
        x_ref[:, here] = x

        def update(j, _):
            there = pl.ds(pl.multiple_of(j * TB, TB), TB)
            m_ref[K:, there] = m_ref[K:, there] - nn(x, m_ref[here, there])
            return 0

        lax.fori_loop(0, k, update, 0)
        return 0

    lax.fori_loop(0, blocks, back, 0)


def split(x):
    high = x.astype(jnp.bfloat16)
    return high, (x - high.astype(F32)).astype(jnp.bfloat16)


def finish_kernel(
    at_ref, rinv_ref, kept_ref, got_ref, cinv_ref, g_ref, x_ref, y_ref, diag_ref, out_ref,
    r_ref, wh_ref, wl_ref, xh_ref, xl_ref,
):
    step = pl.program_id(0)
    rows = x_ref.shape[0]

    @pl.when(step == 0)
    def _():
        xh_ref[...], xl_ref[...] = split(x_ref[...])

    for n in range(8):
        for c in range(4):
            for v in range(2):
                u = 4 * v + c
                high, low = split(g_ref[n, c, v])
                wh_ref[n * TB : (n + 1) * TB, u * TB : (u + 1) * TB] = high
                wl_ref[n * TB : (n + 1) * TB, u * TB : (u + 1) * TB] = low
    dims = (((1,), (1,)), ((), ()))
    dot = lambda a, b: lax.dot_general(a, b, dims, preferred_element_type=F32)
    for n in range(8):
        part = slice(n * TB, (n + 1) * TB)
        wh, wl = wh_ref[part, :], wl_ref[part, :]
        r_ref[n * rows : (n + 1) * rows, :] = (
            dot(xl_ref[...], wh) + dot(xh_ref[...], wl)
        ) + dot(xh_ref[...], wh)

    @pl.when(step == 0)
    def _():
        for v in range(2):
            r_ref[v * rows : (v + 1) * rows, :] = -y_ref[v]

    sub = lax.broadcasted_iota(jnp.int32, (TB, TB), 0)
    lane = lax.broadcasted_iota(jnp.int32, (TB, TB), 1)
    base = pl.multiple_of(at_ref[1] * rows + step * TB, TB)
    r_ref[pl.ds(base, TB), :] = r_ref[pl.ds(base, TB), :] - jnp.where(
        sub == lane, diag_ref[pl.ds(step, 1), :], 0.0
    )
    index = [jnp.maximum(cinv_ref[t], 0) for t in range(2)]
    live = [(cinv_ref[t] >= 0).astype(F32) for t in range(2)]
    for j in range(rows // TB):

        def body(o, _):
            value = -r_ref[pl.ds(j * TB + o, 8, stride=rows), :]
            for t, ref in enumerate((kept_ref.at[0, 0], got_ref)):
                s = rinv_ref[t, j * TB + o]
                x = ref[j, jnp.maximum(s, 0)]
                x = jnp.take_along_axis(x, index[t], axis=1)
                value += x * (live[t] * jnp.where(s >= 0, 1.0, 0.0))
            out_ref[0, j, o] = value
            return 0

        lax.fori_loop(0, TB, body, 0, unroll=8)


def inverse(relative):
    offsets = jnp.arange(TB, dtype=jnp.int32)
    hit = relative[..., None, :] == offsets[:, None]
    return jnp.max(jnp.where(hit, offsets, -1), axis=-1)


def on_device(child_update, child_map, parent_diag):
    cube, row, col = lax.axis_index("cube"), lax.axis_index("row"), lax.axis_index("col")
    grid, columns = 32, 4
    position = cube * 4 + row
    sibling = position // (grid // 2)
    block = child_update[0]
    tiles, cols = block.shape[1], block.shape[3]
    rows = tiles * TB
    trade = [(i, i ^ 16) for i in range(grid)]

    panel = jnp.transpose(block[:, :, :, :2, :], (0, 3, 1, 2, 4)).reshape(2, 2, rows, TB)
    raw = lax.dynamic_index_in_dim(panel, sibling, 0, keepdims=False)
    give = lax.dynamic_index_in_dim(panel, 1 - sibling, 0, keepdims=False)
    got = lax.ppermute(give, ("cube", "row"), trade)
    bulk = lax.dynamic_index_in_dim(block, 1 - sibling, 0, keepdims=False)
    bulk, got = lax.optimization_barrier((bulk, got))
    arrived = lax.ppermute(bulk, ("cube", "row"), trade)

    maps = jnp.stack(
        [
            lax.dynamic_index_in_dim(child_map, sibling, 0, keepdims=False),
            lax.dynamic_index_in_dim(child_map, 1 - sibling, 0, keepdims=False),
        ]
    )
    row_maps = lax.dynamic_index_in_dim(
        maps.reshape(2, tiles, grid, TB), position, 2, keepdims=False
    )
    row_tiles = grid * jnp.arange(tiles, dtype=jnp.int32) + position
    row_maps = row_maps - TB * row_tiles[None, :, None]
    col_maps = lax.dynamic_index_in_dim(
        maps.reshape(2, cols, columns, TB), col, 2, keepdims=False
    )
    col_tiles = columns * jnp.arange(cols, dtype=jnp.int32) + col
    col_maps = col_maps - TB * col_tiles[None, :, None]
    diag = lax.dynamic_index_in_dim(
        parent_diag.reshape(tiles, grid, TB), position, 1, keepdims=False
    )
    meets = row_tiles[None, :] == col_tiles[:2, None]
    panel_diag = jnp.where(meets[:, :, None], diag[None], 0.0).reshape(2 * tiles, TB)

    piece = pl.pallas_call(
        place_kernel,
        out_shape=jax.ShapeDtypeStruct((2, rows, TB), F32),
        in_specs=[VMEM] * 5,
        out_specs=VMEM,
    )(raw, got, row_maps, col_maps[:, :2], panel_diag)

    own_rows = lax.all_gather(piece, "col", axis=0)
    pivot = pl.pallas_call(
        pivot_kernel,
        out_shape=jax.ShapeDtypeStruct((4, 8, 2, TB, TB), F32),
        in_specs=[VMEM],
        out_specs=VMEM,
        scratch_shapes=[
            pltpu.SemaphoreType.DMA((37,)),
            pltpu.SemaphoreType.DMA((4, 8)),
            pltpu.SemaphoreType.DMA,
        ],
        compiler_params=pltpu.CompilerParams(collective_id=0, has_side_effects=True),
    )(piece[:, :TB])

    turned = lax.ppermute(
        own_rows, ("row", "col"), [(r * 4 + c, c * 4 + r) for r in range(4) for c in range(4)]
    )
    others = lax.all_gather(turned, "cube", axis=0)

    y, x = pl.pallas_call(
        factor_kernel,
        out_shape=[
            jax.ShapeDtypeStruct((2, rows, TB), F32),
            jax.ShapeDtypeStruct((rows, K), F32),
        ],
        in_specs=[SMEM, VMEM, VMEM],
        out_specs=[VMEM, VMEM],
        scratch_shapes=[
            pltpu.VMEM((K + rows, K), F32),
            pltpu.VMEM((K // TB, TB, TB), F32),
            pltpu.VMEM((TB, TB), F32),
        ],
        cost_estimate=pl.CostEstimate(flops=40_000_000_000, bytes_accessed=8 << 20, transcendentals=0),
    )(col.reshape(1), pivot, own_rows)

    row_inverse = inverse(row_maps).reshape(2, rows)
    solved = jnp.arange(cols) < 2
    col_inverse = jnp.where(solved[None, :, None], -1, inverse(col_maps))
    here = jnp.logical_and(row == col, jnp.logical_or(jnp.arange(tiles) > 0, cube >= 2))
    trailing_diag = jnp.where(here[:, None], diag, 0.0)
    at = jnp.stack([sibling, cube]).astype(jnp.int32)
    return pl.pallas_call(
        finish_kernel,
        out_shape=jax.ShapeDtypeStruct((1, tiles, TB, cols, TB), F32),
        grid_spec=pltpu.PrefetchScalarGridSpec(
            num_scalar_prefetch=2,
            grid=(cols // 8,),
            in_specs=[
                pl.BlockSpec((1, 1, tiles, TB, 8, TB), lambda i, at, _: (0, at[0], 0, 0, i, 0)),
                pl.BlockSpec((tiles, TB, 8, TB), lambda i, *_: (0, 0, i, 0)),
                pl.BlockSpec((2, 8, TB), lambda i, *_: (0, i, 0)),
                pl.BlockSpec((8, 4, 2, TB, TB), lambda i, *_: (0, 0, 0, i, 0)),
                VMEM,
                VMEM,
                VMEM,
            ],
            out_specs=pl.BlockSpec((1, tiles, TB, 8, TB), lambda i, *_: (0, 0, 0, i, 0)),
            scratch_shapes=[
                pltpu.VMEM((8 * rows, TB), F32),
                pltpu.VMEM((8 * TB, K), jnp.bfloat16),
                pltpu.VMEM((8 * TB, K), jnp.bfloat16),
                pltpu.VMEM((rows, K), jnp.bfloat16),
                pltpu.VMEM((rows, K), jnp.bfloat16),
            ],
        ),
    )(at, row_inverse, child_update, arrived, col_inverse, others, x, y, trailing_diag)


def solution(mesh):
    return jax.shard_map(
        on_device,
        mesh=mesh,
        in_specs=(P(("cube", "row"), None, None, None, "col", None), P(), P()),
        out_specs=P(("cube", "row"), None, None, "col", None),
        check_vma=False,
    )
```

time: 1060 us -> 639 us (0.60)
  Pallas kernels: 0 us -> 515 us
  waiting for transfers between devices: 553 us -> 80.9 us
  other arithmetic: 288 us -> 5.64 us
  matrix products: 112 us -> 0 us
  local copies, waits for them, and re-layouts: 79.4 us -> 16.1 us
    pallas_call x0 -> x4, Pallas kernels: none -> 515 us  [the longest x1 363 us: on_device(): pl.pallas_call(pivot_kernel, out_shape=jax.ShapeDtypeStruct((4, 8, 2, TB,...]
    another operation x33 -> x2, other arithmetic: 256 us -> 0.8 us  [the longest x1 0.66 us: on_device(): at = jnp.stack([sibling, cube]).astype(jnp.int32)]
    psum x2 -> x0, waiting for transfers between devices: 171 us -> none  [broadcast(): return lax.psum(jnp.where(mine, value, jnp.zeros_like(value)), axis)]
    all_gather x2, waiting for transfers between devices: 202 us -> 34.2 us  [the longest x1 34.2 us: on_device(): own_rows = lax.all_gather(piece, 'col', axis=0)]
    ppermute x1 -> x3, waiting for transfers between devices: 179 us -> 46.6 us  [the longest x1 46.6 us: on_device(): lax.ppermute(own_rows, ('row', 'col'), [(r * 4 + c, c * 4 + r) for r in r...]
    dot_general x3 -> x0, matrix products: 72 us -> none  [the longest x1 29.7 us: on_device(): jnp.einsum('rsk,cjvk->rsjcv', solved, gathered, precision=lax.Precision.H...]
    another operation x29 -> x0, matrix products: 40.1 us -> none  [the longest x14 23.1 us: on_device(): factor = jnp.linalg.cholesky(pivot_block)]
    another operation x35 -> x0, local copies, waits for them, and re-layouts: 28.6 us -> none
  transfers between devices with their start and end apart: 5 -> 5, of which waited for: 5 -> 2; matrix products, arithmetic and copies ran while one was open for 1% -> 3% of each run, Pallas kernels for 0% -> 70%
where the time goes in v1:
time: 639 us; the launch traced here: 638 us
  Pallas kernels  515 us (81%)
  waiting for transfers between devices  80.9 us (13%)
  local copies, waits for them, and re-layouts  16.1 us (3%)
  between operations  13.6 us (2%)
    pallas_call x1, Pallas kernels, on_device(): pl.pallas_call(pivot_kernel, out_shape=jax.ShapeDtypeStruct((4, 8, 2, TB,...  363 us
    pallas_call x1, Pallas kernels, on_device(): pl.pallas_call(factor_kernel, out_shape=[jax.ShapeDtypeStruct((2, rows, T...  85.1 us
    pallas_call x1, Pallas kernels, on_device(): pl.pallas_call(finish_kernel, out_shape=jax.ShapeDtypeStruct((1, tiles, T...  63.4 us
    ppermute x1, waiting for transfers between devices, on_device(): lax.ppermute(own_rows, ('row', 'col'), [(r * 4 + c, c * 4 + r) for r in r...  46.6 us
    all_gather x1, waiting for transfers between devices, on_device(): own_rows = lax.all_gather(piece, 'col', axis=0)  34.2 us
  transfers between devices with their start and end apart: 5, of which 2 were waited for; matrix products, arithmetic and copies ran while one was open for 3% of the time, Pallas kernels for 70%

profile of v1, /device:TPU:1, one launch (start us, length us, event | category | flops | bytes accessed | tf_op | source)
XLA Modules:
  0.0 637.9 jit_solution(3434080757500416732)
XLA Ops:
  6.5 0.0 copy-start
  6.5 0.0 copy-start.4
  6.5 0.0 all-gather.5.cloned.1.call-start
  6.5 2.5 slice.16
  9.1 0.1 constant_dynamic-slice_fusion.1
  9.2 2.1 collective-permute-start
  11.3 0.8 copy.29
  12.2 0.0 copy-done.4
  12.2 0.1 constant_dynamic-slice_fusion.6
  12.3 0.1 pad_add_fusion
  12.4 0.1 reshape.82
  12.6 0.0 copy-done
  12.7 0.1 eq.63
  12.8 0.1 eq.64
  12.8 0.1 eq.65
  12.9 0.6 slice_subtract_fusion.cmap_ref
  13.6 0.7 broadcast_subtract_fusion.rmap_ref
  14.3 0.7 broadcast_select_fusion.1.diag_ref
  14.9 7.8 %dynamic-slice_bitcast_fusion = f32[4,128,32,128]{3,2,1,0:T(8,128)} fusion(f32[1,2,4,128,32,128]{5,4,3,2,1,0:T(8,128)} %kept_ref.1, s32[]{:T(128)S(6)} %select_n.50), kind=kLoop, calls=%fused_computation | loop fusion | bytes 16777220 | tf_op jit(solution)/shard_map/jit(dynamic_index_in_dim)/squeeze | solution.py:336
  22.7 0.0 collective-permute-done.got_ref
  22.7 0.0 copy-start.3
  22.7 0.8 copy-done.3
  23.5 4.2 shard_map.37
  27.7 0.0 all-gather.5.cloned.1.call-update
  27.7 0.0 all-gather.7.cloned.1.call-start
  27.8 34.2 %all-gather.5.cloned.1.call-done = f32[8,512,128]{2,1,0:T(8,128)} async-done(((f32[2,512,128]{2,1,0:T(8,128)}), f32[8,512,128]{2,1,0:T(8,128)}) %all-gather.5.cloned.1.call-update) | async-done | bytes 2097168 | tf_op jit(solution)/shard_map/all_gather | solution.py:369
  62.0 2.9 collective-permute-start.2
  64.8 46.6 %collective-permute-done.2 = f32[4,2,512,128]{3,2,1,0:T(8,128)S(1)} collective-permute-done((f32[4,2,512,128]{3,2,1,0:T(8,128)}, f32[4,2,512,128]{3,2,1,0:T(8,128)S(1)}, u32[]{:S(2)}, u32[]{:S(2)}) %collective-permute-start.2) | collective-permute-done | bytes 2097184 | tf_op jit(solution)/shard_map/ppermute | solution.py:383
  111.5 0.0 copy-start.2
  111.5 1.3 copy-done.2
  112.8 0.0 all-gather.7.cloned.1.call-update
  112.8 1.3 collective-permute-start.1
  114.1 0.1 subtract_bitcast_fusion.1
  114.2 0.2 select_reduce_fusion.1
  114.4 0.6 copy.31
  115.0 0.7 pad_add_fusion.1.at_ref
  115.7 0.1 subtract_bitcast_fusion
  115.8 1.2 select_reduce_fusion
  116.9 0.7 broadcast_select_fusion.2.diag_ref
  117.6 0.7 broadcast_select_fusion.cinv_ref
  118.2 1.6 slice.19.piece_ref
  119.8 362.7 %shard_map.38.s_ref = f32[4,8,2,128,128]{4,3,2,1,0:T(8,128)} custom-call(f32[2,128,128]{2,1,0:T(8,128)} %slice.19.piece_ref), custom_call_target="tpu_custom_call" | custom-call | tf_op jit(solution)/shard_map/pallas_call | solution.py:370
  482.5 85.1 %shard_map.39 = (f32[2,512,128]{2,1,0:T(8,128)}, f32[512,1024]{1,0:T(8,128)}) custom-call(s32[1]{0:T(128)} %bitcast.17.col_ref, f32[4,8,2,128,128]{4,3,2,1,0:T(8,128)} %shard_map.38.s_ref, f32[4,2,512,128]{3,2,1,0:T(8,128)} %bitcast.60), custom_call_target="tpu_custom_call" | custom-call | flops 40000000000 | bytes 8388608 | tf_op jit(solution)/shard_map/pallas_call | solution.py:388
  567.6 0.0 collective-permute-done.1.got_ref
  567.6 0.0 all-gather.7.cloned.1.call-done
  567.6 0.0 copy-start.1
  567.6 63.4 %shard_map.40 = f32[1,4,128,32,128]{4,3,2,1,0:T(8,128)} custom-call(s32[2]{0:T(128)} %pad_add_fusion.1.at_ref, s32[2,512]{1,0:T(2,128)} %bitcast.55, f32[1,2,4,128,32,128]{5,4,3,2,1,0:T(8,128)} %kept_ref.1, f32[4,128,32,128]{3,2,1,0:T(8,128)} %collective-permute-done.1.got_ref, s32[2,32,128]{2,1,0:T(8,128)} %broadcast_select_fusion.cinv_ref, ...), custom_call_target="tpu_custom_call" | custom-call | tf_op jit(solution)/shard_map/pallas_call | solution.py:410
  631.0 0.0 copy-done.1
  (13 shorter events, 0.1 us)
Async XLA Ops:
  6.5 6.1 copy-start
  6.5 5.6 copy-start.4
  6.5 55.4 %all-gather.5.cloned.1.call-start = ((), (), s32[]{:S(2)}) async-start(), calls=%async_computation | async-start | bytes 2621440 | tf_op jit(solution)/shard_map/all_gather | solution.py:369
  9.2 13.5 %collective-permute-start = (f32[2,512,128]{2,1,0:T(8,128)S(1)}, f32[2,512,128]{2,1,0:T(8,128)S(1)}, u32[]{:S(2)}, u32[]{:S(2)}) collective-permute-start(f32[2,512,128]{2,1,0:T(8,128)S(1)} %bitcast.47), channel_id=1, source_target_pairs={{0,64},{4,68},{8,72},{12,76},{16,80},{20,84},{24,88},{28,92},{32,9... | collective-permute-start | bytes 1572872 | tf_op jit(solution)/shard_map/ppermute | solution.py:335
  22.7 0.8 copy-start.3
  27.7 539.9 %all-gather.7.cloned.1.call-start = ((), (), s32[]{:S(2)}) async-start(), calls=%async_computation.1 | async-start | bytes 18874368 | tf_op jit(solution)/shard_map/all_gather | solution.py:386
  62.0 49.5 %collective-permute-start.2 = (f32[4,2,512,128]{3,2,1,0:T(8,128)}, f32[4,2,512,128]{3,2,1,0:T(8,128)S(1)}, u32[]{:S(2)}, u32[]{:S(2)}) collective-permute-start(f32[4,2,512,128]{3,2,1,0:T(8,128)} %bitcast.59), channel_id=1, source_target_pairs={{0,0},{1,4},{2,8},{3,12},{4,1},{5,5},{6,9},{7,13},{8,2},{9,6},{10,... | collective-permute-start | bytes 6291464 | tf_op jit(solution)/shard_map/ppermute | solution.py:383
  111.5 1.3 copy-start.2
  112.8 454.8 %collective-permute-start.1 = (f32[4,128,32,128]{3,2,1,0:T(8,128)}, f32[4,128,32,128]{3,2,1,0:T(8,128)}, u32[]{:S(2)}, u32[]{:S(2)}) collective-permute-start(f32[4,128,32,128]{3,2,1,0:T(8,128)} %dynamic-slice_bitcast_fusion), channel_id=1, source_target_pairs={{0,64},{4,68},{8,72},{12,76},{16,80},{20,84},{24,88},{28,92},{32,9... | collective-permute-start | bytes 25165832 | tf_op jit(solution)/shard_map/ppermute | solution.py:338
  567.6 63.4 %copy-start.1 = (f32[16384]{0:T(1024)S(1)}, f32[16384]{0:T(1024)}, u32[]{:S(2)}) copy-start(f32[16384]{0:T(1024)} %param.5) | copy-start | bytes 196612
Sparse Core Ops, SparseCore 0:
  27.8 34.0 all-gather.4
  113.0 292.3 all-gather.6

commit v2 on v1

--- a/solution.py
+++ b/solution.py
@@ -1,11 +1,10 @@
-import functools
-
 import jax
 import jax.numpy as jnp
 from jax import lax
 from jax.experimental import pallas as pl
 from jax.experimental.pallas import tpu as pltpu
 from jax.sharding import PartitionSpec as P
+
 
 K = 1024
 TB = 128
@@ -31,127 +30,118 @@
 def place_kernel(raw_ref, got_ref, rmap_ref, cmap_ref, diag_ref, out_ref):
     sub = lax.broadcasted_iota(jnp.int32, (TB, TB), 0)
     lane = lax.broadcasted_iota(jnp.int32, (TB, TB), 1)
-    tiles = rmap_ref.shape[1]
+    tiles = rmap_ref.shape[2]
     for v in range(2):
-        cols = [
-            nt(ref[v], (sub == cmap_ref[t, v : v + 1, :]).astype(F32))
-            for t, ref in enumerate((raw_ref, got_ref))
-        ]
-        for j in range(tiles):
-            rows = slice(j * TB, (j + 1) * TB)
-            total = jnp.where(sub == lane, diag_ref[v * tiles + j : v * tiles + j + 1, :], 0.0)
-            for t in range(2):
-                hot = (sub == rmap_ref[t, j : j + 1, :]).astype(F32)
-                total += nn(hot, cols[t][rows, :])
-            out_ref[v, rows, :] = total
+        for half in range(2):
+            cols = [
+                nt(ref[half, v], (sub == cmap_ref[t, v : v + 1, :]).astype(F32))
+                for t, ref in enumerate((raw_ref, got_ref))
+            ]
+            for j in range(tiles):
+                rows = slice(j * TB, (j + 1) * TB)
+                total = jnp.where(sub == lane, diag_ref[half, v, j : j + 1, :], 0.0)
+                for t in range(2):
+                    hot = (sub == rmap_ref[t, half, j : j + 1, :]).astype(F32)
+                    total += nn(hot, cols[t][rows, :])
+                out_ref[half, v, rows, :] = total
 
 
 def pivot_kernel(piece_ref, out_ref, send, recv, local):
     cube, row, col = lax.axis_index("cube"), lax.axis_index("row"), lax.axis_index("col")
-    z, near = lax.rem(cube, 4), cube < 4
+    z = lax.rem(cube, 4)
     core = lax.rem(row, 2)
     at = lambda cu, ro, co: {"cube": cu, "row": ro, "col": co}
     mates = [at((cube - z) + lax.rem(z + d, 4), row, col) for d in (1, 2, 3)]
-    across = [
-        at(lax.rem(cube + 4, 8), row, col),
-        at(cube, lax.rem(row + 2, 4), col),
-        at(lax.rem(cube + 4, 8), lax.rem(row + 2, 4), col),
-    ]
+    across = at(lax.rem(cube + 4, 8), lax.rem(row + 2, 4), col)
     up, down = lax.rem(col + 1, 4), lax.rem(col + 3, 4)
     sides = [at(cube, row, up), at(cube, row, down)]
     other = at(cube, row + 1 - 2 * core, col)
     barrier = pltpu.get_barrier_semaphore()
-    for peer in mates + across + sides + [other]:
+    for peer in mates + [across] + sides + [other]:
         pl.semaphore_signal(barrier, inc=1, device_id=peer, device_id_type=MESH)
-    pl.semaphore_wait(barrier, 9)
-
-    def copy(c, p, slot, peer):
+    pl.semaphore_wait(barrier, 7)
+
+    def copy(c, p, slot, peer, width):
+        part = out_ref.at[c, p, pl.ds(0, width)]
         return pltpu.make_async_remote_copy(
-            src_ref=out_ref.at[c, p],
-            dst_ref=out_ref.at[c, p],
+            src_ref=part,
+            dst_ref=part,
             send_sem=send.at[slot],
             recv_sem=recv.at[c, p],
             device_id=peer,
             device_id_type=MESH,
         )
 
-    mine = lax.rem(cube, 2) * 4 + row
-    source = cube < 2
-
-    @pl.when(source)
-    def _():
-        own = pltpu.make_async_copy(piece_ref, out_ref.at[col, mine], local)
-        own.start()
-        own.wait()
-        for i, peer in enumerate(mates):
-            copy(col, mine, i, peer).start()
+    for zz in range(2):
+        mine = zz * 4 + row
+
+        @pl.when(z == zz)
+        def _():
+            part = pl.ds(0, zz + 1)
+            own = pltpu.make_async_copy(piece_ref.at[part], out_ref.at[col, mine, part], local)
+            own.start()
+            own.wait()
+            for i, peer in enumerate(mates):
+                copy(col, mine, i, peer, zz + 1).start()
 
     for zz in range(2):
         p = zz * 4 + row
-
-        @pl.when(near)
+        n = zz
+
+        @pl.when(z != zz)
         def _():
-            @pl.when(z != zz)
-            def _():
-                copy(col, p, 0, other).wait_recv()
-
-            for i, peer in enumerate(across):
-                copy(col, p, 3 + 3 * zz + i, peer).start()
-
-    half = row // 2
+            copy(col, p, 0, other, zz + 1).wait_recv()
+
+        copy(col, p, 3 + zz, across, zz + 1).start()
+        copy(col, p, 5 + n, sides[0], zz + 1).start()
+        copy(col, p, 7 + n, sides[1], zz + 1).start()
+        copy(col, p, 9 + n, other, zz + 1).start()
+    opposite = lax.rem(row + 2, 4)
     for zz in range(2):
-        for hh in range(2):
-            p = zz * 4 + hh * 2 + core
-            n = zz * 2 + hh
-
-            @pl.when(jnp.logical_or(jnp.logical_not(near), half != hh))
-            def _():
-                copy(col, p, 0, other).wait_recv()
-
-            copy(col, p, 9 + n, sides[0]).start()
-            copy(col, p, 13 + n, sides[1]).start()
-            copy(col, p, 17 + n, other).start()
-    for zz in range(2):
-        for hh in range(2):
-            p = zz * 4 + hh * 2 + core
-            n = zz * 2 + hh
-            copy(down, p, 0, other).wait_recv()
-            copy(down, p, 21 + n, other).start()
+        p = zz * 4 + opposite
+        n = zz
+        copy(col, p, 0, other, zz + 1).wait_recv()
+        copy(col, p, 11 + n, sides[0], zz + 1).start()
+        copy(col, p, 13 + n, sides[1], zz + 1).start()
+        copy(col, p, 15 + n, other, zz + 1).start()
+    for i, who in enumerate((row, opposite)):
+        for zz in range(2):
+            p = zz * 4 + who
+            n = i * 2 + zz
+            copy(down, p, 0, other, zz + 1).wait_recv()
+            copy(down, p, 17 + n, other, zz + 1).start()
 
             @pl.when(core == 0)
             def _():
-                copy(down, p, 25 + n, sides[0]).start()
-
-            copy(up, p, 0, other).wait_recv()
-            copy(up, p, 29 + n, other).start()
+                copy(down, p, 21 + n, sides[0], zz + 1).start()
+
+            copy(up, p, 0, other, zz + 1).wait_recv()
+            copy(up, p, 25 + n, other, zz + 1).start()
 
             @pl.when(core == 1)
             def _():
-                copy(up, p, 25 + n, sides[1]).start()
+                copy(up, p, 21 + n, sides[1], zz + 1).start()
 
     far = lax.rem(col + 2, 4)
-    for zz in range(2):
-        for hh in range(2):
-            p = zz * 4 + hh * 2 + core
-            copy(far, p, 0, other).wait_recv()
-            copy(far, p, 33 + zz * 2 + hh, other).start()
+    for i, who in enumerate((row, opposite)):
+        for zz in range(2):
+            p = zz * 4 + who
+            copy(far, p, 0, other, zz + 1).wait_recv()
+            copy(far, p, 29 + i * 2 + zz, other, zz + 1).start()
     for c in range(4):
         for zz in range(2):
             for hh in range(2):
-                copy(c, zz * 4 + hh * 2 + 1 - core, 0, other).wait_recv()
-
-    @pl.when(source)
-    def _():
-        for i in range(3):
-            copy(col, mine, i, other).wait_send()
-
-    @pl.when(near)
-    def _():
-        for i in range(3, 9):
-            copy(col, mine, i, other).wait_send()
-
-    for i in range(9, 37):
-        copy(col, mine, i, other).wait_send()
+                copy(c, zz * 4 + hh * 2 + 1 - core, 0, other, zz + 1).wait_recv()
+
+    for zz in range(2):
+
+        @pl.when(z == zz)
+        def _():
+            for i in range(3):
+                copy(col, row, i, other, zz + 1).wait_send()
+
+        for i in (3, 5, 7, 9, 11, 13, 15, 17, 19, 21, 23, 25, 27, 29, 31):
+            copy(col, row, i + zz, other, zz + 1).wait_send()
 
 
 def leaf(d_ref, li_ref):
@@ -258,8 +248,14 @@
     return high, (x - high.astype(F32)).astype(jnp.bfloat16)
 
 
-def finish_kernel(
-    at_ref, rinv_ref, kept_ref, got_ref, cinv_ref, g_ref, x_ref, y_ref, diag_ref, out_ref,
+def place_rows(ref, j, t, rinv_ref, index, live, o):
+    s = rinv_ref[t, j * TB + o]
+    x = jnp.take_along_axis(ref[j, jnp.maximum(s, 0)], index, axis=1)
+    return x * (live * jnp.where(s >= 0, 1.0, 0.0))
+
+
+def update_kernel(
+    at_ref, rinv_ref, kept_ref, cinv_ref, g_ref, x_ref, y_ref, diag_ref, out_ref,
     r_ref, wh_ref, wl_ref, xh_ref, xl_ref,
 ):
     step = pl.program_id(0)
@@ -270,12 +266,14 @@
         xh_ref[...], xl_ref[...] = split(x_ref[...])
 
     for n in range(8):
-        for c in range(4):
+        part = slice(n * TB, (n + 1) * TB)
+        for m in range(4):
+            q = lax.rem(at_ref[2] + n // 4 + 4 - m, 4)
             for v in range(2):
-                u = 4 * v + c
-                high, low = split(g_ref[n, c, v])
-                wh_ref[n * TB : (n + 1) * TB, u * TB : (u + 1) * TB] = high
-                wl_ref[n * TB : (n + 1) * TB, u * TB : (u + 1) * TB] = low
+                high, low = split(g_ref[(n % 4) * 2 + n // 4, m, v])
+                there = pl.ds(pl.multiple_of((4 * v + q) * TB, TB), TB)
+                wh_ref[part, there] = high
+                wl_ref[part, there] = low
     dims = (((1,), (1,)), ((), ()))
     dot = lambda a, b: lax.dot_general(a, b, dims, preferred_element_type=F32)
     for n in range(8):
@@ -296,18 +294,24 @@
     r_ref[pl.ds(base, TB), :] = r_ref[pl.ds(base, TB), :] - jnp.where(
         sub == lane, diag_ref[pl.ds(step, 1), :], 0.0
     )
-    index = [jnp.maximum(cinv_ref[t], 0) for t in range(2)]
-    live = [(cinv_ref[t] >= 0).astype(F32) for t in range(2)]
+    index, live = jnp.maximum(cinv_ref[0], 0), (cinv_ref[0] >= 0).astype(F32)
     for j in range(rows // TB):
 
         def body(o, _):
-            value = -r_ref[pl.ds(j * TB + o, 8, stride=rows), :]
-            for t, ref in enumerate((kept_ref.at[0, 0], got_ref)):
-                s = rinv_ref[t, j * TB + o]
-                x = ref[j, jnp.maximum(s, 0)]
-                x = jnp.take_along_axis(x, index[t], axis=1)
-                value += x * (live[t] * jnp.where(s >= 0, 1.0, 0.0))
-            out_ref[0, j, o] = value
+            value = place_rows(kept_ref.at[0, 0], j, 0, rinv_ref, index, live, o)
+            out_ref[j, o] = value - r_ref[pl.ds(j * TB + o, 8, stride=rows), :]
+            return 0
+
+        lax.fori_loop(0, TB, body, 0, unroll=8)
+
+
+def finish_kernel(rinv_ref, got_ref, cinv_ref, part_ref, out_ref):
+    index, live = jnp.maximum(cinv_ref[1], 0), (cinv_ref[1] >= 0).astype(F32)
+    for j in range(got_ref.shape[0]):
+
+        def body(o, _):
+            value = place_rows(got_ref, j, 1, rinv_ref, index, live, o)
+            out_ref[0, j, o] = value + part_ref[j, o]
             return 0
 
         lax.fori_loop(0, TB, body, 0, unroll=8)
@@ -329,10 +333,8 @@
     rows = tiles * TB
     trade = [(i, i ^ 16) for i in range(grid)]
 
-    panel = jnp.transpose(block[:, :, :, :2, :], (0, 3, 1, 2, 4)).reshape(2, 2, rows, TB)
-    raw = lax.dynamic_index_in_dim(panel, sibling, 0, keepdims=False)
-    give = lax.dynamic_index_in_dim(panel, 1 - sibling, 0, keepdims=False)
-    got = lax.ppermute(give, ("cube", "row"), trade)
+    raw = jnp.transpose(block[:, :, :, :2, :], (0, 3, 1, 2, 4)).reshape(2, 2, rows, TB)
+    got = lax.ppermute(raw, ("cube", "row"), trade)
     bulk = lax.dynamic_index_in_dim(block, 1 - sibling, 0, keepdims=False)
     bulk, got = lax.optimization_barrier((bulk, got))
     arrived = lax.ppermute(bulk, ("cube", "row"), trade)
@@ -343,47 +345,83 @@
             lax.dynamic_index_in_dim(child_map, 1 - sibling, 0, keepdims=False),
         ]
     )
-    row_maps = lax.dynamic_index_in_dim(
-        maps.reshape(2, tiles, grid, TB), position, 2, keepdims=False
-    )
-    row_tiles = grid * jnp.arange(tiles, dtype=jnp.int32) + position
-    row_maps = row_maps - TB * row_tiles[None, :, None]
+    within = position % 16
+    pair_tiles = (
+        grid * jnp.arange(tiles, dtype=jnp.int32)[None, :]
+        + 16 * jnp.arange(2, dtype=jnp.int32)[:, None]
+        + within
+    )
+    pair_maps = jnp.swapaxes(
+        lax.dynamic_index_in_dim(
+            maps.reshape(2, tiles, 2, 16, TB), within, 3, keepdims=False
+        ),
+        1,
+        2,
+    )
+    pair_maps = pair_maps - TB * pair_tiles[None, :, :, None]
+    row_maps = lax.dynamic_index_in_dim(pair_maps, sibling, 1, keepdims=False)
     col_maps = lax.dynamic_index_in_dim(
         maps.reshape(2, cols, columns, TB), col, 2, keepdims=False
     )
     col_tiles = columns * jnp.arange(cols, dtype=jnp.int32) + col
     col_maps = col_maps - TB * col_tiles[None, :, None]
-    diag = lax.dynamic_index_in_dim(
-        parent_diag.reshape(tiles, grid, TB), position, 1, keepdims=False
-    )
-    meets = row_tiles[None, :] == col_tiles[:2, None]
-    panel_diag = jnp.where(meets[:, :, None], diag[None], 0.0).reshape(2 * tiles, TB)
-
-    piece = pl.pallas_call(
+    pair_diag = jnp.swapaxes(
+        lax.dynamic_index_in_dim(
+            parent_diag.reshape(tiles, 2, 16, TB), within, 2, keepdims=False
+        ),
+        0,
+        1,
+    )
+    diag = lax.dynamic_index_in_dim(pair_diag, sibling, 0, keepdims=False)
+    meets = pair_tiles[:, None, :] == col_tiles[None, :2, None]
+    panel_diag = jnp.where(meets[..., None], pair_diag[:, None], 0.0)
+
+    pieces = pl.pallas_call(
         place_kernel,
-        out_shape=jax.ShapeDtypeStruct((2, rows, TB), F32),
+        out_shape=jax.ShapeDtypeStruct((2, 2, rows, TB), F32),
         in_specs=[VMEM] * 5,
         out_specs=VMEM,
-    )(raw, got, row_maps, col_maps[:, :2], panel_diag)
-
-    own_rows = lax.all_gather(piece, "col", axis=0)
+    )(raw, got, pair_maps, col_maps[:, :2], panel_diag)
+
+    even = lax.dynamic_index_in_dim(pieces, col % 2, 0, keepdims=False)
+    odd = lax.dynamic_index_in_dim(pieces, 1 - col % 2, 0, keepdims=False)
+    quarters = []
+    for m in range(4):
+        pairs = []
+        for s in range(2):
+            for z in range(4):
+                for half in range(2):
+                    for core in range(2):
+                        for y in range(4):
+                            kind = (m + y) % 4
+                            far, h = kind // 2, kind % 2
+                            source = ((s * 4 + z) * 4 + half * 2 + core) * 4 + y
+                            target = ((s ^ far) * 4 + z) * 4 + (half ^ far) * 2 + h
+                            pairs.append((source, target * 4 + half * 2 + core))
+        quarters.append(lax.ppermute(even if m % 2 == 0 else odd, ("cube", "row", "col"), pairs))
+    turned = jnp.stack(quarters)
+    groups = [
+        [(s * 4 + z) * 4 + half * 2 + core for z in range(4) for core in range(2)]
+        for s in range(2)
+        for half in range(2)
+    ]
+    others = lax.all_gather(turned, ("cube", "row"), axis=0, axis_index_groups=groups)
+
+    own_rows = lax.all_gather(
+        lax.dynamic_index_in_dim(pieces, sibling, 0, keepdims=False), "col", axis=0
+    )
     pivot = pl.pallas_call(
         pivot_kernel,
         out_shape=jax.ShapeDtypeStruct((4, 8, 2, TB, TB), F32),
         in_specs=[VMEM],
         out_specs=VMEM,
         scratch_shapes=[
-            pltpu.SemaphoreType.DMA((37,)),
+            pltpu.SemaphoreType.DMA((33,)),
             pltpu.SemaphoreType.DMA((4, 8)),
             pltpu.SemaphoreType.DMA,
         ],
         compiler_params=pltpu.CompilerParams(collective_id=0, has_side_effects=True),
-    )(piece[:, :TB])
-
-    turned = lax.ppermute(
-        own_rows, ("row", "col"), [(r * 4 + c, c * 4 + r) for r in range(4) for c in range(4)]
-    )
-    others = lax.all_gather(turned, "cube", axis=0)
+    )(pieces[0, :, :TB])
 
     y, x = pl.pallas_call(
         factor_kernel,
@@ -406,23 +444,23 @@
     col_inverse = jnp.where(solved[None, :, None], -1, inverse(col_maps))
     here = jnp.logical_and(row == col, jnp.logical_or(jnp.arange(tiles) > 0, cube >= 2))
     trailing_diag = jnp.where(here[:, None], diag, 0.0)
-    at = jnp.stack([sibling, cube]).astype(jnp.int32)
-    return pl.pallas_call(
-        finish_kernel,
-        out_shape=jax.ShapeDtypeStruct((1, tiles, TB, cols, TB), F32),
+    crossed = (row // 2 != col // 2).astype(jnp.int32)
+    at = jnp.stack([sibling, cube, 2 * crossed]).astype(jnp.int32)
+    part = pl.pallas_call(
+        update_kernel,
+        out_shape=jax.ShapeDtypeStruct((tiles, TB, cols, TB), F32),
         grid_spec=pltpu.PrefetchScalarGridSpec(
             num_scalar_prefetch=2,
             grid=(cols // 8,),
             in_specs=[
                 pl.BlockSpec((1, 1, tiles, TB, 8, TB), lambda i, at, _: (0, at[0], 0, 0, i, 0)),
-                pl.BlockSpec((tiles, TB, 8, TB), lambda i, *_: (0, 0, i, 0)),
                 pl.BlockSpec((2, 8, TB), lambda i, *_: (0, i, 0)),
                 pl.BlockSpec((8, 4, 2, TB, TB), lambda i, *_: (0, 0, 0, i, 0)),
                 VMEM,
                 VMEM,
                 VMEM,
             ],
-            out_specs=pl.BlockSpec((1, tiles, TB, 8, TB), lambda i, *_: (0, 0, 0, i, 0)),
+            out_specs=pl.BlockSpec((tiles, TB, 8, TB), lambda i, *_: (0, 0, i, 0)),
             scratch_shapes=[
                 pltpu.VMEM((8 * rows, TB), F32),
                 pltpu.VMEM((8 * TB, K), jnp.bfloat16),
@@ -431,7 +469,22 @@
                 pltpu.VMEM((rows, K), jnp.bfloat16),
             ],
         ),
-    )(at, row_inverse, child_update, arrived, col_inverse, others, x, y, trailing_diag)
+        cost_estimate=pl.CostEstimate(flops=26_000_000_000, bytes_accessed=32 << 20, transcendentals=0),
+    )(at, row_inverse, child_update, col_inverse, others, x, y, trailing_diag)
+    return pl.pallas_call(
+        finish_kernel,
+        out_shape=jax.ShapeDtypeStruct((1, tiles, TB, cols, TB), F32),
+        grid_spec=pltpu.PrefetchScalarGridSpec(
+            num_scalar_prefetch=1,
+            grid=(cols // 8,),
+            in_specs=[
+                pl.BlockSpec((tiles, TB, 8, TB), lambda i, *_: (0, 0, i, 0)),
+                pl.BlockSpec((2, 8, TB), lambda i, *_: (0, i, 0)),
+                pl.BlockSpec((tiles, TB, 8, TB), lambda i, *_: (0, 0, i, 0)),
+            ],
+            out_specs=pl.BlockSpec((1, tiles, TB, 8, TB), lambda i, *_: (0, 0, 0, i, 0)),
+        ),
+    )(row_inverse, arrived, col_inverse, part)
 
 
 def solution(mesh):

time: 639 us -> 300 us (0.47)
  Pallas kernels: 515 us -> 208 us
  waiting for transfers between devices: 80.9 us -> 37.6 us
  starting transfers between devices: 6.28 us -> 16.1 us
    pallas_call x1, Pallas kernels: 363 us -> 30.4 us  [on_device(): pl.pallas_call(pivot_kernel, out_shape=jax.ShapeDtypeStruct((4, 8, 2, TB,...]
    pallas_call x1 -> x2, Pallas kernels: 4.22 us -> 63.8 us  [the longest x1 57 us: on_device(): pl.pallas_call(update_kernel, out_shape=jax.ShapeDtypeStruct((tiles, TB,...]
    pallas_call x1, Pallas kernels: 63.4 us -> 28.4 us  [on_device(): pl.pallas_call(finish_kernel, out_shape=jax.ShapeDtypeStruct((1, tiles, T...]
    all_gather x2, waiting for transfers between devices: 34.2 us -> 0.02 us  [the longest x1 0.02 us: on_device(): lax.all_gather(lax.dynamic_index_in_dim(pieces, sibling, 0, keepdims=Fals...]
    ppermute x2 -> x5, starting transfers between devices: 4.97 us -> 14.7 us  [the longest x4 12.6 us: on_device(): lax.ppermute(even if m % 2 == 0 else odd, ('cube', 'row', 'col'), pairs)]
    ppermute x2 -> x5, waiting for transfers between devices: 46.6 us -> 37.5 us  [the longest x4 25.6 us: on_device(): lax.ppermute(even if m % 2 == 0 else odd, ('cube', 'row', 'col'), pairs)]
  transfers between devices with their start and end apart: 5 -> 8, of which waited for: 2 -> 4; matrix products, arithmetic and copies ran while one was open for 3% -> 6% of each run, Pallas kernels for 70% -> 58%
where the time goes in v2:
time: 300 us; the launch traced here: 299 us
  Pallas kernels  208 us (69%)
  waiting for transfers between devices  37.6 us (13%)
  local copies, waits for them, and re-layouts  16.2 us (5%)
  starting transfers between devices  16.1 us (5%)
  between operations  13.6 us (5%)
  other arithmetic  7.09 us (2%)
    pallas_call x1, Pallas kernels, on_device(): pl.pallas_call(factor_kernel, out_shape=[jax.ShapeDtypeStruct((2, rows, T...  85.3 us
    pallas_call x1, Pallas kernels, on_device(): pl.pallas_call(update_kernel, out_shape=jax.ShapeDtypeStruct((tiles, TB,...  57 us
    pallas_call x1, Pallas kernels, on_device(): pl.pallas_call(pivot_kernel, out_shape=jax.ShapeDtypeStruct((4, 8, 2, TB,...  30.4 us
    pallas_call x1, Pallas kernels, on_device(): pl.pallas_call(finish_kernel, out_shape=jax.ShapeDtypeStruct((1, tiles, T...  28.4 us
    ppermute x4, waiting for transfers between devices, on_device(): lax.ppermute(even if m % 2 == 0 else odd, ('cube', 'row', 'col'), pairs)  25.6 us
    ppermute x4, starting transfers between devices, on_device(): lax.ppermute(even if m % 2 == 0 else odd, ('cube', 'row', 'col'), pairs)  12.6 us
    ppermute x1, waiting for transfers between devices, on_device(): got = lax.ppermute(raw, ('cube', 'row'), trade)  11.9 us
    squeeze x1, local copies, waits for them, and re-layouts, on_device(): bulk = lax.dynamic_index_in_dim(block, 1 - sibling, 0, keepdims=False)  7.78 us
  transfers between devices with their start and end apart: 8, of which 4 were waited for; matrix products, arithmetic and copies ran while one was open for 6% of the time, Pallas kernels for 58%

profile of v2, /device:TPU:1, one launch (start us, length us, event | category | flops | bytes accessed | tf_op | source)
XLA Modules:
  0.0 298.5 jit_solution(15079607022890439143)
XLA Ops:
  6.5 0.0 copy-start
  6.5 0.0 copy-start.4
  6.5 0.0 all-gather.4.cloned.1.call-start
  6.5 2.5 slice_bitcast_fusion
  9.1 0.1 copy.19
  9.2 0.0 copy-start.2
  9.2 2.1 collective-permute-start
  11.3 0.0 copy-done.4
  11.3 0.1 constant_dynamic-slice_fusion.6
  11.5 0.1 pad_add_fusion
  11.6 0.1 reshape.117
  11.8 0.1 broadcast_multiply_fusion
  11.9 0.1 broadcast_compare_fusion
  12.0 0.0 copy-done
  12.1 0.7 slice_subtract_fusion.cmap_ref
  12.7 0.7 broadcast_select_fusion.1.diag_ref
  13.4 0.7 fusion.rmap_ref
  14.1 7.8 %dynamic-slice_bitcast_fusion = f32[4,128,32,128]{3,2,1,0:T(8,128)} fusion(f32[1,2,4,128,32,128]{5,4,3,2,1,0:T(8,128)} %kept_ref.1, s32[]{:T(128)S(6)} %select_n.80), kind=kLoop, calls=%fused_computation | loop fusion | bytes 16777220 | tf_op jit(solution)/shard_map/jit(dynamic_index_in_dim)/squeeze | solution.py:338
  21.8 0.0 copy-done.2
  21.8 11.9 %collective-permute-done.got_ref = f32[2,2,512,128]{3,2,1,0:T(8,128)S(1)} collective-permute-done((f32[2,2,512,128]{3,2,1,0:T(8,128)S(1)}, f32[2,2,512,128]{3,2,1,0:T(8,128)S(1)}, u32[]{:S(2)}, u32[]{:S(2)}) %collective-permute-start) | collective-permute-done | bytes 1048608 | tf_op jit(solution)/shard_map/ppermute | solution.py:337
  33.8 0.0 copy-start.3
  33.8 1.0 copy-done.3
  34.8 6.8 %shard_map.37 = f32[2,2,512,128]{3,2,1,0:T(8,128)} custom-call(f32[2,2,512,128]{3,2,1,0:T(8,128)} %bitcast.53, f32[2,2,512,128]{3,2,1,0:T(8,128)} %copy-done.3, s32[2,2,4,128]{3,2,1,0:T(4,128)} %fusion.rmap_ref, s32[2,2,128]{2,1,0:T(2,128)} %slice_subtract_fusion.cmap_ref, f32[2,2,4,128]{3,2,1,0:T(4,128)} %broadcast_select_fusion.1.diag_ref), custom_call_target="tpu_custom_call" | custom-call | tf_op jit(solution)/shard_map/pallas_call | solution.py:379
  41.5 2.3 constant_dynamic-slice_fusion.1
  43.8 0.0 copy-start.5
  43.8 0.0 all-gather.4.cloned.1.call-update
  43.8 0.0 all-gather.6.cloned.1.call-start
  43.9 3.9 %collective-permute-start.5 = (f32[2,512,128]{2,1,0:T(8,128)S(1)}, f32[2,512,128]{2,1,0:T(8,128)S(1)}, u32[]{:S(2)}, u32[]{:S(2)}) collective-permute-start(f32[2,512,128]{2,1,0:T(8,128)S(1)} %get-tuple-element.16), channel_id=1, source_target_pairs={{0,76},{1,0},{2,4},{3,72},{4,77},{5,1},{6,5},{7,73},{8,70},{9,10},... | collective-permute-start | bytes 1572872 | tf_op jit(solution)/shard_map/ppermute | solution.py:401
  47.8 0.0 collective-permute-start.3
  47.8 4.9 %collective-permute-start.4 = (f32[2,512,128]{2,1,0:T(8,128)S(1)}, f32[2,512,128]{2,1,0:T(8,128)S(1)}, u32[]{:S(2)}, u32[]{:S(2)}) collective-permute-start(f32[2,512,128]{2,1,0:T(8,128)S(1)} %get-tuple-element.17), channel_id=1, source_target_pairs={{0,72},{1,76},{2,0},{3,4},{4,73},{5,77},{6,1},{7,5},{8,66},{9,70},... | collective-permute-start | bytes 1572872 | tf_op jit(solution)/shard_map/ppermute | solution.py:401
  52.7 3.7 %collective-permute-start.2 = (f32[2,512,128]{2,1,0:T(8,128)S(1)}, f32[2,512,128]{2,1,0:T(8,128)S(1)}, u32[]{:S(2)}, u32[]{:S(2)}) collective-permute-start(f32[2,512,128]{2,1,0:T(8,128)S(1)} %get-tuple-element.17), channel_id=1, source_target_pairs={{0,0},{1,4},{2,72},{3,76},{4,1},{5,5},{6,73},{7,77},{8,10},{9,14},... | collective-permute-start | bytes 1572872 | tf_op jit(solution)/shard_map/ppermute | solution.py:401
  56.4 3.1 %collective-permute-done.5 = f32[2,512,128]{2,1,0:T(8,128)S(1)} collective-permute-done((f32[2,512,128]{2,1,0:T(8,128)S(1)}, f32[2,512,128]{2,1,0:T(8,128)S(1)}, u32[]{:S(2)}, u32[]{:S(2)}) %collective-permute-start.5) | collective-permute-done | bytes 524320 | tf_op jit(solution)/shard_map/ppermute | solution.py:401
  59.5 0.0 collective-permute-done.3
  59.5 19.9 %collective-permute-done.4 = f32[2,512,128]{2,1,0:T(8,128)S(1)} collective-permute-done((f32[2,512,128]{2,1,0:T(8,128)S(1)}, f32[2,512,128]{2,1,0:T(8,128)S(1)}, u32[]{:S(2)}, u32[]{:S(2)}) %collective-permute-start.4) | collective-permute-done | bytes 524320 | tf_op jit(solution)/shard_map/ppermute | solution.py:401
  79.4 2.6 collective-permute-done.2
  82.0 1.5 pad_maximum_fusion
  83.5 0.0 all-gather.6.cloned.1.call-update
  83.5 1.4 collective-permute-start.1
  84.9 0.0 copy-done.5
  84.9 0.2 select_reduce_fusion.1
  85.1 0.6 copy.30
  85.7 0.6 pad_add_fusion.1.at_ref
  86.3 0.1 subtract_bitcast_fusion
  86.4 1.2 select_reduce_fusion
  87.5 0.6 broadcast_select_fusion.2.diag_ref
  88.2 0.7 broadcast_select_fusion.cinv_ref
  88.9 1.6 slice_bitcast_fusion.1.piece_ref
  90.4 30.4 %shard_map.38.s_ref = f32[4,8,2,128,128]{4,3,2,1,0:T(8,128)} custom-call(f32[2,128,128]{2,1,0:T(8,128)} %slice_bitcast_fusion.1.piece_ref), custom_call_target="tpu_custom_call" | custom-call | tf_op jit(solution)/shard_map/pallas_call | solution.py:413
  120.9 0.0 all-gather.4.cloned.1.call-done.a_ref
  120.9 85.3 %shard_map.39 = (f32[2,512,128]{2,1,0:T(8,128)}, f32[512,1024]{1,0:T(8,128)}) custom-call(s32[1]{0:T(128)} %bitcast.22.col_ref, f32[4,8,2,128,128]{4,3,2,1,0:T(8,128)} %shard_map.38.s_ref, f32[4,2,512,128]{3,2,1,0:T(8,128)} %all-gather.4.cloned.1.call-done.a_ref), custom_call_target="tpu_custom_call" | custom-call | flops 40000000000 | bytes 8388608 | tf_op jit(solution)/shard_map/pallas_call | solution.py:426
  206.2 0.0 all-gather.6.cloned.1.call-done
  206.2 57.0 %shard_map.40.part_ref = f32[4,128,32,128]{3,2,1,0:T(8,128)} custom-call(s32[3]{0:T(128)} %pad_add_fusion.1.at_ref, s32[2,512]{1,0:T(2,128)} %bitcast.63, f32[1,2,4,128,32,128]{5,4,3,2,1,0:T(8,128)} %kept_ref.1, s32[2,32,128]{2,1,0:T(8,128)} %broadcast_select_fusion.cinv_ref, f32[8,4,2,512,128]{4,3,2,1,0:T(8,128)} %bitcast.68, ...), custom_call_target="tpu_custom_call" | custom-call | flops 25999998976 | bytes 33554432 | tf_op jit(solution)/shard_map/pallas_call | solution.py:449
  263.3 0.0 collective-permute-done.1.got_ref
  263.3 0.0 copy-start.1
  263.3 28.4 %shard_map.41 = f32[1,4,128,32,128]{4,3,2,1,0:T(8,128)} custom-call(s32[2,512]{1,0:T(2,128)} %bitcast.64, f32[4,128,32,128]{3,2,1,0:T(8,128)} %collective-permute-done.1.got_ref, s32[2,32,128]{2,1,0:T(8,128)} %broadcast_select_fusion.cinv_ref, f32[4,128,32,128]{3,2,1,0:T(8,128)} %shard_map.40.part_ref), custom_call_target="tpu_custom_call" | custom-call | tf_op jit(solution)/shard_map/pallas_call | solution.py:474
  291.7 0.0 copy-done.1
  (12 shorter events, 0.1 us)
Async XLA Ops:
  6.5 5.5 %copy-start = (f32[16384]{0:T(1024)S(1)}, f32[16384]{0:T(1024)}, u32[]{:S(2)}) copy-start(f32[16384]{0:T(1024)} %param.5) | copy-start | bytes 196612
  6.5 4.8 %copy-start.4 = (s32[2,16384]{1,0:T(2,128)S(1)}, s32[2,16384]{1,0:T(2,128)}, u32[]{:S(2)}) copy-start(s32[2,16384]{1,0:T(2,128)} %param.4) | copy-start | bytes 393220
  6.5 114.3 %all-gather.4.cloned.1.call-start = ((), (), s32[]{:S(2)}) async-start(), calls=%async_computation | async-start | bytes 2621440 | tf_op jit(solution)/shard_map/all_gather | solution.py:410
  9.2 12.6 %copy-start.2 = (f32[2,2,4,128,128]{4,3,2,1,0:T(8,128)}, f32[2,2,4,128,128]{4,3,2,1,0:T(8,128)S(1)}, u32[]{:S(2)}) copy-start(f32[2,2,4,128,128]{4,3,2,1,0:T(8,128)S(1)} %copy.19) | copy-start | bytes 3145732
  9.2 24.6 %collective-permute-start = (f32[2,2,512,128]{3,2,1,0:T(8,128)S(1)}, f32[2,2,512,128]{3,2,1,0:T(8,128)S(1)}, u32[]{:S(2)}, u32[]{:S(2)}) collective-permute-start(f32[2,2,512,128]{3,2,1,0:T(8,128)S(1)} %bitcast.52), channel_id=1, source_target_pairs={{0,64},{4,68},{8,72},{12,76},{16,80},{20,84},{24,88},{28,92},{32,9... | collective-permute-start | bytes 3145736 | tf_op jit(solution)/shard_map/ppermute | solution.py:337
  33.8 1.0 copy-start.3
  43.8 41.1 %copy-start.5 = (s32[2,2,4,128]{3,2,1,0:T(4,128)S(1)}, s32[2,2,4,128]{3,2,1,0:T(4,128)}, u32[]{:S(2)}) copy-start(s32[2,2,4,128]{3,2,1,0:T(4,128)} %fusion.rmap_ref) | copy-start | bytes 24580
  43.8 162.4 %all-gather.6.cloned.1.call-start = ((), (), s32[]{:S(2)}) async-start(), calls=%async_computation.1 | async-start | bytes 18874368 | tf_op jit(solution)/shard_map/all_gather | solution.py:408
  43.9 15.7 %collective-permute-start.5 = (f32[2,512,128]{2,1,0:T(8,128)S(1)}, f32[2,512,128]{2,1,0:T(8,128)S(1)}, u32[]{:S(2)}, u32[]{:S(2)}) collective-permute-start(f32[2,512,128]{2,1,0:T(8,128)S(1)} %get-tuple-element.16), channel_id=1, source_target_pairs={{0,76},{1,0},{2,4},{3,72},{4,77},{5,1},{6,5},{7,73},{8,70},{9,10},... | collective-permute-start | bytes 1572872 | tf_op jit(solution)/shard_map/ppermute | solution.py:401
  47.8 11.7 %collective-permute-start.3 = (f32[2,512,128]{2,1,0:T(8,128)S(1)}, f32[2,512,128]{2,1,0:T(8,128)S(1)}, u32[]{:S(2)}, u32[]{:S(2)}) collective-permute-start(f32[2,512,128]{2,1,0:T(8,128)S(1)} %get-tuple-element.16), channel_id=1, source_target_pairs={{0,4},{1,72},{2,76},{3,0},{4,5},{5,73},{6,77},{7,1},{8,14},{9,66},... | collective-permute-start | bytes 1572872 | tf_op jit(solution)/shard_map/ppermute | solution.py:401
  47.8 31.6 %collective-permute-start.4 = (f32[2,512,128]{2,1,0:T(8,128)S(1)}, f32[2,512,128]{2,1,0:T(8,128)S(1)}, u32[]{:S(2)}, u32[]{:S(2)}) collective-permute-start(f32[2,512,128]{2,1,0:T(8,128)S(1)} %get-tuple-element.17), channel_id=1, source_target_pairs={{0,72},{1,76},{2,0},{3,4},{4,73},{5,77},{6,1},{7,5},{8,66},{9,70},... | collective-permute-start | bytes 1572872 | tf_op jit(solution)/shard_map/ppermute | solution.py:401
  52.7 29.3 %collective-permute-start.2 = (f32[2,512,128]{2,1,0:T(8,128)S(1)}, f32[2,512,128]{2,1,0:T(8,128)S(1)}, u32[]{:S(2)}, u32[]{:S(2)}) collective-permute-start(f32[2,512,128]{2,1,0:T(8,128)S(1)} %get-tuple-element.17), channel_id=1, source_target_pairs={{0,0},{1,4},{2,72},{3,76},{4,1},{5,5},{6,73},{7,77},{8,10},{9,14},... | collective-permute-start | bytes 1572872 | tf_op jit(solution)/shard_map/ppermute | solution.py:401
  83.5 179.8 %collective-permute-start.1 = (f32[4,128,32,128]{3,2,1,0:T(8,128)}, f32[4,128,32,128]{3,2,1,0:T(8,128)}, u32[]{:S(2)}, u32[]{:S(2)}) collective-permute-start(f32[4,128,32,128]{3,2,1,0:T(8,128)} %dynamic-slice_bitcast_fusion), channel_id=1, source_target_pairs={{0,64},{4,68},{8,72},{12,76},{16,80},{20,84},{24,88},{28,92},{32,9... | collective-permute-start | bytes 25165832 | tf_op jit(solution)/shard_map/ppermute | solution.py:340
  263.3 28.4 %copy-start.1 = (f32[16384]{0:T(1024)S(1)}, f32[16384]{0:T(1024)}, u32[]{:S(2)}) copy-start(f32[16384]{0:T(1024)} %param.5) | copy-start | bytes 196612
Sparse Core Ops, SparseCore 0:
  43.9 46.7 all-gather.3
  92.5 86.9 all-gather.5

commit v3 on v2

--- a/solution.py
+++ b/solution.py
@@ -197,27 +197,34 @@
     for c in range(4):
         for v in range(2):
             u = 4 * v + c
-            for p in range(blocks):
-                if p >= u:
-                    m_ref[p * TB : (p + 1) * TB, u * TB : (u + 1) * TB] = s_ref[c, p, v]
-                else:
-                    m_ref[p * TB : (p + 1) * TB, u * TB : (u + 1) * TB] = jnp.zeros((TB, TB), F32)
+            for p in range(u, blocks):
+                m_ref[p * TB : (p + 1) * TB, u * TB : (u + 1) * TB] = s_ref[c, p, v]
             m_ref[K:, u * TB : (u + 1) * TB] = a_ref[c, v]
 
+    pair_width = 2 * TB
+
     def step(k, _):
-        o = pl.multiple_of(k * TB, TB)
-        here = pl.ds(o, TB)
+        here = pl.ds(pl.multiple_of(k * TB, TB), TB)
         d_ref[...] = m_ref[here, here]
         leaf(d_ref, li_ref.at[k])
         m_ref[:, here] = nt(m_ref[:, here], li_ref[k])
 
-        def update(j, _):
-            q = pl.multiple_of(j * TB, TB)
-            there = pl.ds(q, TB)
-            m_ref[:, there] = m_ref[:, there] - nt(m_ref[:, here], m_ref[there, here])
-            return 0
-
-        lax.fori_loop(k + 1, blocks, update, 0)
+        @pl.when(lax.rem(k, 2) == 0)
+        def _():
+            after = pl.ds(pl.multiple_of((k + 1) * TB, TB), TB)
+            m_ref[:, after] = m_ref[:, after] - nt(m_ref[:, here], m_ref[after, here])
+
+        @pl.when(lax.rem(k, 2) == 1)
+        def _():
+            pair = pl.ds(pl.multiple_of((k - 1) * TB, TB), pair_width)
+
+            def trail(i, _):
+                part = pl.ds(pl.multiple_of(i * pair_width, pair_width), pair_width)
+                m_ref[:, part] = m_ref[:, part] - nt(m_ref[:, pair], m_ref[part, pair])
+                return 0
+
+            lax.fori_loop((k + 1) // 2, blocks // 2, trail, 0)
+
         return 0
 
     lax.fori_loop(0, blocks, step, 0)
@@ -226,21 +233,23 @@
         y_ref[v] = m_ref[K:, pl.ds(pl.multiple_of((4 * v + col) * TB, TB), TB)]
 
     def back(i, _):
-        k = blocks - 1 - i
-        o = pl.multiple_of(k * TB, TB)
-        here = pl.ds(o, TB)
-        x = nn(m_ref[K:, here], li_ref[k])
-        x_ref[:, here] = x
-
-        def update(j, _):
-            there = pl.ds(pl.multiple_of(j * TB, TB), TB)
-            m_ref[K:, there] = m_ref[K:, there] - nn(x, m_ref[here, there])
+        n = blocks // 2 - 1 - i
+        first = pl.ds(pl.multiple_of(n * pair_width, TB), TB)
+        last = pl.ds(pl.multiple_of(n * pair_width + TB, TB), TB)
+        pair = pl.ds(pl.multiple_of(n * pair_width, pair_width), pair_width)
+        x_ref[:, last] = nn(m_ref[K:, last], li_ref[2 * n + 1])
+        rest = m_ref[K:, first] - nn(x_ref[:, last], m_ref[last, first])
+        x_ref[:, first] = nn(rest, li_ref[2 * n])
+
+        def lead(j, _):
+            part = pl.ds(pl.multiple_of(j * pair_width, pair_width), pair_width)
+            m_ref[K:, part] = m_ref[K:, part] - nn(x_ref[:, pair], m_ref[pair, part])
             return 0
 
-        lax.fori_loop(0, k, update, 0)
+        lax.fori_loop(0, n, lead, 0)
         return 0
 
-    lax.fori_loop(0, blocks, back, 0)
+    lax.fori_loop(0, blocks // 2, back, 0)
 
 
 def split(x):
@@ -248,18 +257,39 @@
     return high, (x - high.astype(F32)).astype(jnp.bfloat16)
 
 
-def place_rows(ref, j, t, rinv_ref, index, live, o):
-    s = rinv_ref[t, j * TB + o]
-    x = jnp.take_along_axis(ref[j, jnp.maximum(s, 0)], index, axis=1)
-    return x * (live * jnp.where(s >= 0, 1.0, 0.0))
+def place_rows(t, rinv_ref, cinv_ref, from_ref, part_ref, out_ref):
+    groups = range(0, from_ref.shape[-2], 8)
+    index = [jnp.maximum(cinv_ref[t, g : g + 8], 0) for g in groups]
+    live = [(cinv_ref[t, g : g + 8] >= 0).astype(F32) for g in groups]
+    base = pl.program_id(0) * TB
+
+    def body(o, _):
+        s = rinv_ref[t, base + o]
+        weight = jnp.where(s >= 0, 1.0, 0.0)
+        s = jnp.maximum(s, 0)
+        for g, at, keep in zip(groups, index, live):
+            x = jnp.take_along_axis(from_ref[s, g : g + 8], at, axis=1) * (keep * weight)
+            if part_ref is not None:
+                x += part_ref[o, g : g + 8]
+            out_ref[o, g : g + 8] = x
+        return 0
+
+    lax.fori_loop(0, TB, body, 0, unroll=16)
+
+
+def keep_kernel(at_ref, rinv_ref, kept_ref, cinv_ref, out_ref):
+    place_rows(0, rinv_ref, cinv_ref, kept_ref.at[0, 0, 0], None, out_ref.at[0])
+
+
+def finish_kernel(rinv_ref, got_ref, cinv_ref, part_ref, out_ref):
+    place_rows(1, rinv_ref, cinv_ref, got_ref.at[0], part_ref.at[0], out_ref.at[0, 0])
 
 
 def update_kernel(
-    at_ref, rinv_ref, kept_ref, cinv_ref, g_ref, x_ref, y_ref, diag_ref, out_ref,
-    r_ref, wh_ref, wl_ref, xh_ref, xl_ref,
+    at_ref, kept_ref, g_ref, x_ref, y_ref, diag_ref, out_ref, wh_ref, wl_ref, xh_ref, xl_ref
 ):
     step = pl.program_id(0)
-    rows = x_ref.shape[0]
+    tiles = kept_ref.shape[0]
 
     @pl.when(step == 0)
     def _():
@@ -276,45 +306,24 @@
                 wl_ref[part, there] = low
     dims = (((1,), (1,)), ((), ()))
     dot = lambda a, b: lax.dot_general(a, b, dims, preferred_element_type=F32)
-    for n in range(8):
-        part = slice(n * TB, (n + 1) * TB)
+    sub = lax.broadcasted_iota(jnp.int32, (TB, TB), 0)
+    lane = lax.broadcasted_iota(jnp.int32, (TB, TB), 1)
+    diag = jnp.where(sub == lane, diag_ref[pl.ds(step, 1), :], 0.0)
+    for n in range(0, 8, 2):
+        part = slice(n * TB, (n + 2) * TB)
         wh, wl = wh_ref[part, :], wl_ref[part, :]
-        r_ref[n * rows : (n + 1) * rows, :] = (
-            dot(xl_ref[...], wh) + dot(xh_ref[...], wl)
-        ) + dot(xh_ref[...], wh)
+        r = (dot(xl_ref[...], wh) + dot(xh_ref[...], wl)) + dot(xh_ref[...], wh)
+        for i in range(2):
+            for j in range(tiles):
+                meets = jnp.logical_and(at_ref[1] == n + i, step == j)
+                value = kept_ref[j, :, n + i, :] - r[j * TB : (j + 1) * TB, i * TB : (i + 1) * TB]
+                out_ref[j, :, n + i, :] = value + diag * jnp.where(meets, 1.0, 0.0)
 
     @pl.when(step == 0)
     def _():
         for v in range(2):
-            r_ref[v * rows : (v + 1) * rows, :] = -y_ref[v]
-
-    sub = lax.broadcasted_iota(jnp.int32, (TB, TB), 0)
-    lane = lax.broadcasted_iota(jnp.int32, (TB, TB), 1)
-    base = pl.multiple_of(at_ref[1] * rows + step * TB, TB)
-    r_ref[pl.ds(base, TB), :] = r_ref[pl.ds(base, TB), :] - jnp.where(
-        sub == lane, diag_ref[pl.ds(step, 1), :], 0.0
-    )
-    index, live = jnp.maximum(cinv_ref[0], 0), (cinv_ref[0] >= 0).astype(F32)
-    for j in range(rows // TB):
-
-        def body(o, _):
-            value = place_rows(kept_ref.at[0, 0], j, 0, rinv_ref, index, live, o)
-            out_ref[j, o] = value - r_ref[pl.ds(j * TB + o, 8, stride=rows), :]
-            return 0
-
-        lax.fori_loop(0, TB, body, 0, unroll=8)
-
-
-def finish_kernel(rinv_ref, got_ref, cinv_ref, part_ref, out_ref):
-    index, live = jnp.maximum(cinv_ref[1], 0), (cinv_ref[1] >= 0).astype(F32)
-    for j in range(got_ref.shape[0]):
-
-        def body(o, _):
-            value = place_rows(got_ref, j, 1, rinv_ref, index, live, o)
-            out_ref[0, j, o] = value + part_ref[j, o]
-            return 0
-
-        lax.fori_loop(0, TB, body, 0, unroll=8)
+            for j in range(tiles):
+                out_ref[j, :, v, :] = y_ref[v, j * TB : (j + 1) * TB, :]
 
 
 def inverse(relative):
@@ -446,23 +455,39 @@
     trailing_diag = jnp.where(here[:, None], diag, 0.0)
     crossed = (row // 2 != col // 2).astype(jnp.int32)
     at = jnp.stack([sibling, cube, 2 * crossed]).astype(jnp.int32)
+    by_row = pl.BlockSpec((1, TB, cols, TB), lambda i, *_: (i, 0, 0, 0))
+    all_maps = pl.BlockSpec((2, cols, TB), lambda i, *_: (0, 0, 0))
+    kept = pl.pallas_call(
+        keep_kernel,
+        out_shape=jax.ShapeDtypeStruct((tiles, TB, cols, TB), F32),
+        grid_spec=pltpu.PrefetchScalarGridSpec(
+            num_scalar_prefetch=2,
+            grid=(tiles,),
+            in_specs=[
+                pl.BlockSpec(
+                    (1, 1, 1, TB, cols, TB), lambda i, at, _: (0, at[0], i, 0, 0, 0)
+                ),
+                all_maps,
+            ],
+            out_specs=by_row,
+        ),
+    )(at, row_inverse, child_update, col_inverse)
+    by_col = pl.BlockSpec((tiles, TB, 8, TB), lambda i, *_: (0, 0, i, 0))
     part = pl.pallas_call(
         update_kernel,
         out_shape=jax.ShapeDtypeStruct((tiles, TB, cols, TB), F32),
         grid_spec=pltpu.PrefetchScalarGridSpec(
-            num_scalar_prefetch=2,
+            num_scalar_prefetch=1,
             grid=(cols // 8,),
             in_specs=[
-                pl.BlockSpec((1, 1, tiles, TB, 8, TB), lambda i, at, _: (0, at[0], 0, 0, i, 0)),
-                pl.BlockSpec((2, 8, TB), lambda i, *_: (0, i, 0)),
+                by_col,
                 pl.BlockSpec((8, 4, 2, TB, TB), lambda i, *_: (0, 0, 0, i, 0)),
                 VMEM,
                 VMEM,
                 VMEM,
             ],
-            out_specs=pl.BlockSpec((tiles, TB, 8, TB), lambda i, *_: (0, 0, i, 0)),
+            out_specs=by_col,
             scratch_shapes=[
-                pltpu.VMEM((8 * rows, TB), F32),
                 pltpu.VMEM((8 * TB, K), jnp.bfloat16),
                 pltpu.VMEM((8 * TB, K), jnp.bfloat16),
                 pltpu.VMEM((rows, K), jnp.bfloat16),
@@ -470,19 +495,15 @@
             ],
         ),
         cost_estimate=pl.CostEstimate(flops=26_000_000_000, bytes_accessed=32 << 20, transcendentals=0),
-    )(at, row_inverse, child_update, col_inverse, others, x, y, trailing_diag)
+    )(at, kept, others, x, y, trailing_diag)
     return pl.pallas_call(
         finish_kernel,
         out_shape=jax.ShapeDtypeStruct((1, tiles, TB, cols, TB), F32),
         grid_spec=pltpu.PrefetchScalarGridSpec(
             num_scalar_prefetch=1,
-            grid=(cols // 8,),
-            in_specs=[
-                pl.BlockSpec((tiles, TB, 8, TB), lambda i, *_: (0, 0, i, 0)),
-                pl.BlockSpec((2, 8, TB), lambda i, *_: (0, i, 0)),
-                pl.BlockSpec((tiles, TB, 8, TB), lambda i, *_: (0, 0, i, 0)),
-            ],
-            out_specs=pl.BlockSpec((1, tiles, TB, 8, TB), lambda i, *_: (0, 0, 0, i, 0)),
+            grid=(tiles,),
+            in_specs=[by_row, all_maps, by_row],
+            out_specs=pl.BlockSpec((1, 1, TB, cols, TB), lambda i, *_: (0, i, 0, 0, 0)),
         ),
     )(row_inverse, arrived, col_inverse, part)
 

time: 300 us -> 285 us (0.950)
  Pallas kernels: 208 us -> 168 us
  waiting for transfers between devices: 37.6 us -> 62.1 us
    pallas_call x1, Pallas kernels: 57 us -> 30.5 us  [on_device(): pl.pallas_call(update_kernel, out_shape=jax.ShapeDtypeStruct((tiles, TB,...]
    ppermute x1, waiting for transfers between devices: 0.01 us -> 24.5 us  [on_device(): arrived = lax.ppermute(bulk, ('cube', 'row'), trade)]
    pallas_call x1, Pallas kernels: 85.3 us -> 69.9 us  [on_device(): pl.pallas_call(factor_kernel, out_shape=[jax.ShapeDtypeStruct((2, rows, T...]
    pallas_call x1, Pallas kernels: 28.4 us -> 13.6 us  [on_device(): pl.pallas_call(finish_kernel, out_shape=jax.ShapeDtypeStruct((1, tiles, T...]
    pallas_call x0 -> x1, Pallas kernels: none -> 12 us  [on_device(): pl.pallas_call(keep_kernel, out_shape=jax.ShapeDtypeStruct((tiles, TB, co...]
    pallas_call x1, Pallas kernels: 30.4 us -> 35.5 us  [on_device(): pl.pallas_call(pivot_kernel, out_shape=jax.ShapeDtypeStruct((4, 8, 2, TB,...]
  transfers between devices with their start and end apart: 8 -> 8, of which waited for: 4 -> 5; matrix products, arithmetic and copies ran while one was open for 6% -> 6% of each run, Pallas kernels for 58% -> 52%
where the time goes in v3:
time: 285 us; the launch traced here: 283 us
  Pallas kernels  168 us (59%)
  waiting for transfers between devices  62.1 us (22%)
  local copies, waits for them, and re-layouts  16.2 us (6%)
  starting transfers between devices  16.1 us (6%)
  between operations  13.6 us (5%)
  other arithmetic  7.11 us (2%)
    pallas_call x1, Pallas kernels, on_device(): pl.pallas_call(factor_kernel, out_shape=[jax.ShapeDtypeStruct((2, rows, T...  69.9 us
    pallas_call x1, Pallas kernels, on_device(): pl.pallas_call(pivot_kernel, out_shape=jax.ShapeDtypeStruct((4, 8, 2, TB,...  35.5 us
    pallas_call x1, Pallas kernels, on_device(): pl.pallas_call(update_kernel, out_shape=jax.ShapeDtypeStruct((tiles, TB,...  30.5 us
    ppermute x4, waiting for transfers between devices, on_device(): lax.ppermute(even if m % 2 == 0 else odd, ('cube', 'row', 'col'), pairs)  25.6 us
    ppermute x1, waiting for transfers between devices, on_device(): arrived = lax.ppermute(bulk, ('cube', 'row'), trade)  24.5 us
    pallas_call x1, Pallas kernels, on_device(): pl.pallas_call(finish_kernel, out_shape=jax.ShapeDtypeStruct((1, tiles, T...  13.6 us
    ppermute x4, starting transfers between devices, on_device(): lax.ppermute(even if m % 2 == 0 else odd, ('cube', 'row', 'col'), pairs)  12.6 us
    pallas_call x1, Pallas kernels, on_device(): pl.pallas_call(keep_kernel, out_shape=jax.ShapeDtypeStruct((tiles, TB, co...  12 us
  transfers between devices with their start and end apart: 8, of which 5 were waited for; matrix products, arithmetic and copies ran while one was open for 6% of the time, Pallas kernels for 52%

profile of v3, /device:TPU:1, one launch (start us, length us, event | category | flops | bytes accessed | tf_op | source)
XLA Modules:
  0.0 283.4 jit_solution(3282012674391531677)
XLA Ops:
  6.5 0.0 copy-start
  6.5 0.0 copy-start.4
  6.5 0.0 all-gather.4.cloned.1.call-start
  6.5 2.5 slice_bitcast_fusion
  9.1 0.1 copy.19
  9.2 0.0 copy-start.2
  9.2 2.1 collective-permute-start
  11.3 0.0 copy-done.4
  11.3 0.1 constant_dynamic-slice_fusion.6
  11.5 0.1 pad_add_fusion
  11.6 0.1 reshape.117
  11.8 0.1 broadcast_multiply_fusion
  11.9 0.1 broadcast_compare_fusion
  12.0 0.0 copy-done
  12.1 0.7 slice_subtract_fusion.cmap_ref
  12.7 0.7 broadcast_select_fusion.1.diag_ref
  13.4 0.7 fusion.rmap_ref
  14.0 7.8 %dynamic-slice_bitcast_fusion = f32[4,128,32,128]{3,2,1,0:T(8,128)} fusion(f32[1,2,4,128,32,128]{5,4,3,2,1,0:T(8,128)} %kept_ref.1, s32[]{:T(128)S(6)} %select_n.80), kind=kLoop, calls=%fused_computation | loop fusion | bytes 16777220 | tf_op jit(solution)/shard_map/jit(dynamic_index_in_dim)/squeeze | solution.py:347
  21.8 0.0 copy-done.2
  21.8 11.9 %collective-permute-done.got_ref = f32[2,2,512,128]{3,2,1,0:T(8,128)S(1)} collective-permute-done((f32[2,2,512,128]{3,2,1,0:T(8,128)S(1)}, f32[2,2,512,128]{3,2,1,0:T(8,128)S(1)}, u32[]{:S(2)}, u32[]{:S(2)}) %collective-permute-start) | collective-permute-done | bytes 1048608 | tf_op jit(solution)/shard_map/ppermute | solution.py:346
  33.8 0.0 copy-start.3
  33.8 1.0 copy-done.3
  34.8 6.7 %shard_map.38 = f32[2,2,512,128]{3,2,1,0:T(8,128)} custom-call(f32[2,2,512,128]{3,2,1,0:T(8,128)} %bitcast.53, f32[2,2,512,128]{3,2,1,0:T(8,128)} %copy-done.3, s32[2,2,4,128]{3,2,1,0:T(4,128)} %fusion.rmap_ref, s32[2,2,128]{2,1,0:T(2,128)} %slice_subtract_fusion.cmap_ref, f32[2,2,4,128]{3,2,1,0:T(4,128)} %broadcast_select_fusion.1.diag_ref), custom_call_target="tpu_custom_call" | custom-call | tf_op jit(solution)/shard_map/pallas_call | solution.py:388
  41.5 2.3 constant_dynamic-slice_fusion.1
  43.7 0.0 copy-start.5
  43.7 0.0 all-gather.4.cloned.1.call-update
  43.8 0.0 all-gather.6.cloned.1.call-start
  43.8 4.0 %collective-permute-start.5 = (f32[2,512,128]{2,1,0:T(8,128)S(1)}, f32[2,512,128]{2,1,0:T(8,128)S(1)}, u32[]{:S(2)}, u32[]{:S(2)}) collective-permute-start(f32[2,512,128]{2,1,0:T(8,128)S(1)} %get-tuple-element.16), channel_id=1, source_target_pairs={{0,76},{1,0},{2,4},{3,72},{4,77},{5,1},{6,5},{7,73},{8,70},{9,10},... | collective-permute-start | bytes 1572872 | tf_op jit(solution)/shard_map/ppermute | solution.py:410
  47.8 0.0 collective-permute-start.3
  47.8 4.9 %collective-permute-start.4 = (f32[2,512,128]{2,1,0:T(8,128)S(1)}, f32[2,512,128]{2,1,0:T(8,128)S(1)}, u32[]{:S(2)}, u32[]{:S(2)}) collective-permute-start(f32[2,512,128]{2,1,0:T(8,128)S(1)} %get-tuple-element.17), channel_id=1, source_target_pairs={{0,72},{1,76},{2,0},{3,4},{4,73},{5,77},{6,1},{7,5},{8,66},{9,70},... | collective-permute-start | bytes 1572872 | tf_op jit(solution)/shard_map/ppermute | solution.py:410
  52.7 3.7 %collective-permute-start.2 = (f32[2,512,128]{2,1,0:T(8,128)S(1)}, f32[2,512,128]{2,1,0:T(8,128)S(1)}, u32[]{:S(2)}, u32[]{:S(2)}) collective-permute-start(f32[2,512,128]{2,1,0:T(8,128)S(1)} %get-tuple-element.17), channel_id=1, source_target_pairs={{0,0},{1,4},{2,72},{3,76},{4,1},{5,5},{6,73},{7,77},{8,10},{9,14},... | collective-permute-start | bytes 1572872 | tf_op jit(solution)/shard_map/ppermute | solution.py:410
  56.4 3.1 %collective-permute-done.5 = f32[2,512,128]{2,1,0:T(8,128)S(1)} collective-permute-done((f32[2,512,128]{2,1,0:T(8,128)S(1)}, f32[2,512,128]{2,1,0:T(8,128)S(1)}, u32[]{:S(2)}, u32[]{:S(2)}) %collective-permute-start.5) | collective-permute-done | bytes 524320 | tf_op jit(solution)/shard_map/ppermute | solution.py:410
  59.5 0.0 collective-permute-done.3
  59.5 19.8 %collective-permute-done.4 = f32[2,512,128]{2,1,0:T(8,128)S(1)} collective-permute-done((f32[2,512,128]{2,1,0:T(8,128)S(1)}, f32[2,512,128]{2,1,0:T(8,128)S(1)}, u32[]{:S(2)}, u32[]{:S(2)}) %collective-permute-start.4) | collective-permute-done | bytes 524320 | tf_op jit(solution)/shard_map/ppermute | solution.py:410
  79.3 2.6 collective-permute-done.2
  82.0 1.4 pad_maximum_fusion
  83.4 0.0 all-gather.6.cloned.1.call-update
  83.5 1.4 collective-permute-start.1
  84.9 0.0 copy-done.5
  84.9 0.2 select_reduce_fusion.1
  85.1 0.6 copy.30
  85.7 0.6 pad_add_fusion.1.at_ref
  86.3 0.1 subtract_bitcast_fusion
  86.4 1.2 select_reduce_fusion
  87.6 0.7 broadcast_select_fusion.cinv_ref
  88.2 12.0 %shard_map.37.kept_ref = f32[4,128,32,128]{3,2,1,0:T(8,128)} custom-call(s32[3]{0:T(128)} %pad_add_fusion.1.at_ref, s32[2,512]{1,0:T(2,128)} %bitcast.61, f32[1,2,4,128,32,128]{5,4,3,2,1,0:T(8,128)} %kept_ref.1, s32[2,32,128]{2,1,0:T(8,128)} %broadcast_select_fusion.cinv_ref), custom_call_target="tpu_custom_call" | custom-call | tf_op jit(solution)/shard_map/pallas_call | solution.py:460
  100.3 0.7 broadcast_select_fusion.2.diag_ref
  101.0 1.6 slice_bitcast_fusion.1.piece_ref
  102.5 35.5 %shard_map.39.s_ref = f32[4,8,2,128,128]{4,3,2,1,0:T(8,128)} custom-call(f32[2,128,128]{2,1,0:T(8,128)} %slice_bitcast_fusion.1.piece_ref), custom_call_target="tpu_custom_call" | custom-call | tf_op jit(solution)/shard_map/pallas_call | solution.py:422
  138.0 0.0 all-gather.4.cloned.1.call-done.a_ref
  138.0 69.9 %shard_map.40 = (f32[2,512,128]{2,1,0:T(8,128)}, f32[512,1024]{1,0:T(8,128)}) custom-call(s32[1]{0:T(128)} %bitcast.22.col_ref, f32[4,8,2,128,128]{4,3,2,1,0:T(8,128)} %shard_map.39.s_ref, f32[4,2,512,128]{3,2,1,0:T(8,128)} %all-gather.4.cloned.1.call-done.a_ref), custom_call_target="tpu_custom_call" | custom-call | flops 40000000000 | bytes 8388608 | tf_op jit(solution)/shard_map/pallas_call | solution.py:435
  207.9 0.0 all-gather.6.cloned.1.call-done
  207.9 30.5 %shard_map.41.part_ref = f32[4,128,32,128]{3,2,1,0:T(8,128)} custom-call(s32[3]{0:T(128)} %pad_add_fusion.1.at_ref, f32[4,128,32,128]{3,2,1,0:T(8,128)} %shard_map.37.kept_ref, f32[8,4,2,512,128]{4,3,2,1,0:T(8,128)} %bitcast.68, f32[512,1024]{1,0:T(8,128)} %get-tuple-element.11.x_ref, f32[2,512,128]{2,1,0:T(8,128)} %get-tuple-element.12.y_ref, ...), custom_call_target="tpu_custom_call" | custom-call | flops 25999998976 | bytes 33554432 | tf_op jit(solution)/shard_map/pallas_call | solution.py:476
  238.5 24.5 %collective-permute-done.1.got_ref = f32[4,128,32,128]{3,2,1,0:T(8,128)} collective-permute-done((f32[4,128,32,128]{3,2,1,0:T(8,128)}, f32[4,128,32,128]{3,2,1,0:T(8,128)}, u32[]{:S(2)}, u32[]{:S(2)}) %collective-permute-start.1) | collective-permute-done | bytes 8388640 | tf_op jit(solution)/shard_map/ppermute | solution.py:349
  263.0 0.0 copy-start.1
  263.0 13.6 %shard_map.42 = f32[1,4,128,32,128]{4,3,2,1,0:T(8,128)} custom-call(s32[2,512]{1,0:T(2,128)} %bitcast.62, f32[4,128,32,128]{3,2,1,0:T(8,128)} %collective-permute-done.1.got_ref, s32[2,32,128]{2,1,0:T(8,128)} %broadcast_select_fusion.cinv_ref, f32[4,128,32,128]{3,2,1,0:T(8,128)} %shard_map.41.part_ref), custom_call_target="tpu_custom_call" | custom-call | tf_op jit(solution)/shard_map/pallas_call | solution.py:499
  276.5 0.0 copy-done.1
  (12 shorter events, 0.1 us)
Async XLA Ops:
  6.5 5.5 %copy-start = (f32[16384]{0:T(1024)S(1)}, f32[16384]{0:T(1024)}, u32[]{:S(2)}) copy-start(f32[16384]{0:T(1024)} %param.5) | copy-start | bytes 196612
  6.5 4.8 %copy-start.4 = (s32[2,16384]{1,0:T(2,128)S(1)}, s32[2,16384]{1,0:T(2,128)}, u32[]{:S(2)}) copy-start(s32[2,16384]{1,0:T(2,128)} %param.4) | copy-start | bytes 393220
  6.5 131.5 %all-gather.4.cloned.1.call-start = ((), (), s32[]{:S(2)}) async-start(), calls=%async_computation | async-start | bytes 2621440 | tf_op jit(solution)/shard_map/all_gather | solution.py:419
  9.2 12.6 %copy-start.2 = (f32[2,2,4,128,128]{4,3,2,1,0:T(8,128)}, f32[2,2,4,128,128]{4,3,2,1,0:T(8,128)S(1)}, u32[]{:S(2)}) copy-start(f32[2,2,4,128,128]{4,3,2,1,0:T(8,128)S(1)} %copy.19) | copy-start | bytes 3145732
  9.2 24.6 %collective-permute-start = (f32[2,2,512,128]{3,2,1,0:T(8,128)S(1)}, f32[2,2,512,128]{3,2,1,0:T(8,128)S(1)}, u32[]{:S(2)}, u32[]{:S(2)}) collective-permute-start(f32[2,2,512,128]{3,2,1,0:T(8,128)S(1)} %bitcast.52), channel_id=1, source_target_pairs={{0,64},{4,68},{8,72},{12,76},{16,80},{20,84},{24,88},{28,92},{32,9... | collective-permute-start | bytes 3145736 | tf_op jit(solution)/shard_map/ppermute | solution.py:346
  33.8 1.0 copy-start.3
  43.7 41.2 %copy-start.5 = (s32[2,2,4,128]{3,2,1,0:T(4,128)S(1)}, s32[2,2,4,128]{3,2,1,0:T(4,128)}, u32[]{:S(2)}) copy-start(s32[2,2,4,128]{3,2,1,0:T(4,128)} %fusion.rmap_ref) | copy-start | bytes 24580
  43.8 164.2 %all-gather.6.cloned.1.call-start = ((), (), s32[]{:S(2)}) async-start(), calls=%async_computation.1 | async-start | bytes 18874368 | tf_op jit(solution)/shard_map/all_gather | solution.py:417
  43.8 15.7 %collective-permute-start.5 = (f32[2,512,128]{2,1,0:T(8,128)S(1)}, f32[2,512,128]{2,1,0:T(8,128)S(1)}, u32[]{:S(2)}, u32[]{:S(2)}) collective-permute-start(f32[2,512,128]{2,1,0:T(8,128)S(1)} %get-tuple-element.16), channel_id=1, source_target_pairs={{0,76},{1,0},{2,4},{3,72},{4,77},{5,1},{6,5},{7,73},{8,70},{9,10},... | collective-permute-start | bytes 1572872 | tf_op jit(solution)/shard_map/ppermute | solution.py:410
  47.8 11.7 %collective-permute-start.3 = (f32[2,512,128]{2,1,0:T(8,128)S(1)}, f32[2,512,128]{2,1,0:T(8,128)S(1)}, u32[]{:S(2)}, u32[]{:S(2)}) collective-permute-start(f32[2,512,128]{2,1,0:T(8,128)S(1)} %get-tuple-element.16), channel_id=1, source_target_pairs={{0,4},{1,72},{2,76},{3,0},{4,5},{5,73},{6,77},{7,1},{8,14},{9,66},... | collective-permute-start | bytes 1572872 | tf_op jit(solution)/shard_map/ppermute | solution.py:410
  47.8 31.6 %collective-permute-start.4 = (f32[2,512,128]{2,1,0:T(8,128)S(1)}, f32[2,512,128]{2,1,0:T(8,128)S(1)}, u32[]{:S(2)}, u32[]{:S(2)}) collective-permute-start(f32[2,512,128]{2,1,0:T(8,128)S(1)} %get-tuple-element.17), channel_id=1, source_target_pairs={{0,72},{1,76},{2,0},{3,4},{4,73},{5,77},{6,1},{7,5},{8,66},{9,70},... | collective-permute-start | bytes 1572872 | tf_op jit(solution)/shard_map/ppermute | solution.py:410
  52.7 29.3 %collective-permute-start.2 = (f32[2,512,128]{2,1,0:T(8,128)S(1)}, f32[2,512,128]{2,1,0:T(8,128)S(1)}, u32[]{:S(2)}, u32[]{:S(2)}) collective-permute-start(f32[2,512,128]{2,1,0:T(8,128)S(1)} %get-tuple-element.17), channel_id=1, source_target_pairs={{0,0},{1,4},{2,72},{3,76},{4,1},{5,5},{6,73},{7,77},{8,10},{9,14},... | collective-permute-start | bytes 1572872 | tf_op jit(solution)/shard_map/ppermute | solution.py:410
  83.5 179.5 %collective-permute-start.1 = (f32[4,128,32,128]{3,2,1,0:T(8,128)}, f32[4,128,32,128]{3,2,1,0:T(8,128)}, u32[]{:S(2)}, u32[]{:S(2)}) collective-permute-start(f32[4,128,32,128]{3,2,1,0:T(8,128)} %dynamic-slice_bitcast_fusion), channel_id=1, source_target_pairs={{0,64},{4,68},{8,72},{12,76},{16,80},{20,84},{24,88},{28,92},{32,9... | collective-permute-start | bytes 25165832 | tf_op jit(solution)/shard_map/ppermute | solution.py:349
  263.0 13.6 %copy-start.1 = (f32[16384]{0:T(1024)S(1)}, f32[16384]{0:T(1024)}, u32[]{:S(2)}) copy-start(f32[16384]{0:T(1024)} %param.5) | copy-start | bytes 196612
Sparse Core Ops, SparseCore 0:
  43.9 46.8 all-gather.3
  92.4 90.9 all-gather.5

commit v4 on v3

--- a/solution.py
+++ b/solution.py
@@ -1,3 +1,5 @@
+import functools
+
 import jax
 import jax.numpy as jnp
 from jax import lax
@@ -257,11 +259,11 @@
     return high, (x - high.astype(F32)).astype(jnp.bfloat16)
 
 
-def place_rows(t, rinv_ref, cinv_ref, from_ref, part_ref, out_ref):
+def place_rows(tile, t, rinv_ref, cinv_ref, from_ref, less, out_ref):
     groups = range(0, from_ref.shape[-2], 8)
     index = [jnp.maximum(cinv_ref[t, g : g + 8], 0) for g in groups]
     live = [(cinv_ref[t, g : g + 8] >= 0).astype(F32) for g in groups]
-    base = pl.program_id(0) * TB
+    base = tile * TB
 
     def body(o, _):
         s = rinv_ref[t, base + o]
@@ -269,27 +271,29 @@
         s = jnp.maximum(s, 0)
         for g, at, keep in zip(groups, index, live):
             x = jnp.take_along_axis(from_ref[s, g : g + 8], at, axis=1) * (keep * weight)
-            if part_ref is not None:
-                x += part_ref[o, g : g + 8]
-            out_ref[o, g : g + 8] = x
+            out_ref[o, g : g + 8] = x if less is None else x + less(o, g)
         return 0
 
     lax.fori_loop(0, TB, body, 0, unroll=16)
 
 
 def keep_kernel(at_ref, rinv_ref, kept_ref, cinv_ref, out_ref):
-    place_rows(0, rinv_ref, cinv_ref, kept_ref.at[0, 0, 0], None, out_ref.at[0])
-
-
-def finish_kernel(rinv_ref, got_ref, cinv_ref, part_ref, out_ref):
-    place_rows(1, rinv_ref, cinv_ref, got_ref.at[0], part_ref.at[0], out_ref.at[0, 0])
+    place_rows(pl.program_id(0), 0, rinv_ref, cinv_ref, kept_ref.at[0, 0, 0], None, out_ref.at[0, 0])
+
+
+def finish_kernel(start, rinv_ref, got_ref, cinv_ref, kept_ref, r_ref, out_ref):
+    def less(o, g):
+        return kept_ref[0, 0, o, g : g + 8] - r_ref.at[0][pl.ds(g * TB + o, 8, stride=TB), :]
+
+    tile = pl.program_id(0) + start
+    place_rows(tile, 1, rinv_ref, cinv_ref, got_ref.at[0], less, out_ref.at[0, 0])
 
 
 def update_kernel(
-    at_ref, kept_ref, g_ref, x_ref, y_ref, diag_ref, out_ref, wh_ref, wl_ref, xh_ref, xl_ref
+    at_ref, g_ref, x_ref, y_ref, diag_ref, out_ref, wh_ref, wl_ref, xh_ref, xl_ref
 ):
     step = pl.program_id(0)
-    tiles = kept_ref.shape[0]
+    tiles = out_ref.shape[0]
 
     @pl.when(step == 0)
     def _():
@@ -306,24 +310,27 @@
                 wl_ref[part, there] = low
     dims = (((1,), (1,)), ((), ()))
     dot = lambda a, b: lax.dot_general(a, b, dims, preferred_element_type=F32)
-    sub = lax.broadcasted_iota(jnp.int32, (TB, TB), 0)
-    lane = lax.broadcasted_iota(jnp.int32, (TB, TB), 1)
-    diag = jnp.where(sub == lane, diag_ref[pl.ds(step, 1), :], 0.0)
     for n in range(0, 8, 2):
         part = slice(n * TB, (n + 2) * TB)
         wh, wl = wh_ref[part, :], wl_ref[part, :]
         r = (dot(xl_ref[...], wh) + dot(xh_ref[...], wl)) + dot(xh_ref[...], wh)
         for i in range(2):
             for j in range(tiles):
-                meets = jnp.logical_and(at_ref[1] == n + i, step == j)
-                value = kept_ref[j, :, n + i, :] - r[j * TB : (j + 1) * TB, i * TB : (i + 1) * TB]
-                out_ref[j, :, n + i, :] = value + diag * jnp.where(meets, 1.0, 0.0)
+                out_ref[j, (n + i) * TB : (n + i + 1) * TB, :] = r[
+                    j * TB : (j + 1) * TB, i * TB : (i + 1) * TB
+                ]
+    sub = lax.broadcasted_iota(jnp.int32, (TB, TB), 0)
+    lane = lax.broadcasted_iota(jnp.int32, (TB, TB), 1)
+    here = pl.ds(pl.multiple_of(at_ref[1] * TB, TB), TB)
+    out_ref[step, here, :] = out_ref[step, here, :] - jnp.where(
+        sub == lane, diag_ref[pl.ds(step, 1), :], 0.0
+    )
 
     @pl.when(step == 0)
     def _():
         for v in range(2):
             for j in range(tiles):
-                out_ref[j, :, v, :] = y_ref[v, j * TB : (j + 1) * TB, :]
+                out_ref[j, v * TB : (v + 1) * TB, :] = -y_ref[v, j * TB : (j + 1) * TB, :]
 
 
 def inverse(relative):
@@ -344,9 +351,12 @@
 
     raw = jnp.transpose(block[:, :, :, :2, :], (0, 3, 1, 2, 4)).reshape(2, 2, rows, TB)
     got = lax.ppermute(raw, ("cube", "row"), trade)
+    early = tiles - 1
     bulk = lax.dynamic_index_in_dim(block, 1 - sibling, 0, keepdims=False)
-    bulk, got = lax.optimization_barrier((bulk, got))
-    arrived = lax.ppermute(bulk, ("cube", "row"), trade)
+    first, second, got = lax.optimization_barrier((bulk[:early], bulk[early:], got))
+    arrived = []
+    for part in (first, second):
+        arrived.append(lax.ppermute(part, ("cube", "row"), trade))
 
     maps = jnp.stack(
         [
@@ -455,11 +465,11 @@
     trailing_diag = jnp.where(here[:, None], diag, 0.0)
     crossed = (row // 2 != col // 2).astype(jnp.int32)
     at = jnp.stack([sibling, cube, 2 * crossed]).astype(jnp.int32)
-    by_row = pl.BlockSpec((1, TB, cols, TB), lambda i, *_: (i, 0, 0, 0))
+    whole = jax.ShapeDtypeStruct((1, tiles, TB, cols, TB), F32)
     all_maps = pl.BlockSpec((2, cols, TB), lambda i, *_: (0, 0, 0))
-    kept = pl.pallas_call(
+    result = pl.pallas_call(
         keep_kernel,
-        out_shape=jax.ShapeDtypeStruct((tiles, TB, cols, TB), F32),
+        out_shape=whole,
         grid_spec=pltpu.PrefetchScalarGridSpec(
             num_scalar_prefetch=2,
             grid=(tiles,),
@@ -469,24 +479,22 @@
                 ),
                 all_maps,
             ],
-            out_specs=by_row,
+            out_specs=pl.BlockSpec((1, 1, TB, cols, TB), lambda i, *_: (0, i, 0, 0, 0)),
         ),
     )(at, row_inverse, child_update, col_inverse)
-    by_col = pl.BlockSpec((tiles, TB, 8, TB), lambda i, *_: (0, 0, i, 0))
-    part = pl.pallas_call(
+    update = pl.pallas_call(
         update_kernel,
-        out_shape=jax.ShapeDtypeStruct((tiles, TB, cols, TB), F32),
+        out_shape=jax.ShapeDtypeStruct((tiles, cols * TB, TB), F32),
         grid_spec=pltpu.PrefetchScalarGridSpec(
             num_scalar_prefetch=1,
             grid=(cols // 8,),
             in_specs=[
-                by_col,
                 pl.BlockSpec((8, 4, 2, TB, TB), lambda i, *_: (0, 0, 0, i, 0)),
                 VMEM,
                 VMEM,
                 VMEM,
             ],
-            out_specs=by_col,
+            out_specs=pl.BlockSpec((tiles, 8 * TB, TB), lambda i, *_: (0, i, 0)),
             scratch_shapes=[
                 pltpu.VMEM((8 * TB, K), jnp.bfloat16),
                 pltpu.VMEM((8 * TB, K), jnp.bfloat16),
@@ -495,17 +503,26 @@
             ],
         ),
         cost_estimate=pl.CostEstimate(flops=26_000_000_000, bytes_accessed=32 << 20, transcendentals=0),
-    )(at, kept, others, x, y, trailing_diag)
-    return pl.pallas_call(
-        finish_kernel,
-        out_shape=jax.ShapeDtypeStruct((1, tiles, TB, cols, TB), F32),
-        grid_spec=pltpu.PrefetchScalarGridSpec(
-            num_scalar_prefetch=1,
-            grid=(tiles,),
-            in_specs=[by_row, all_maps, by_row],
-            out_specs=pl.BlockSpec((1, 1, TB, cols, TB), lambda i, *_: (0, i, 0, 0, 0)),
-        ),
-    )(row_inverse, arrived, col_inverse, part)
+    )(at, others, x, y, trailing_diag)
+    for start, part in zip((0, early), arrived):
+        block_at = lambda i, *_, start=start: (0, i + start, 0, 0, 0)
+        result = pl.pallas_call(
+            functools.partial(finish_kernel, start),
+            out_shape=whole,
+            grid_spec=pltpu.PrefetchScalarGridSpec(
+                num_scalar_prefetch=1,
+                grid=(part.shape[0],),
+                in_specs=[
+                    pl.BlockSpec((1, TB, cols, TB), lambda i, *_: (i, 0, 0, 0)),
+                    all_maps,
+                    pl.BlockSpec((1, 1, TB, cols, TB), block_at),
+                    pl.BlockSpec((1, cols * TB, TB), lambda i, *_, start=start: (i + start, 0, 0)),
+                ],
+                out_specs=pl.BlockSpec((1, 1, TB, cols, TB), block_at),
+            ),
+            input_output_aliases={3: 0},
+        )(row_inverse, part, col_inverse, result, update)
+    return result
 
 
 def solution(mesh):

time: 285 us -> 296 us (1.039)
  waiting for transfers between devices: 62.1 us -> 70.1 us
    ppermute x1 -> x2, waiting for transfers between devices: 24.5 us -> 34 us  [on_device(): arrived.append(lax.ppermute(part, ('cube', 'row'), trade))]
    slice x0 -> x2, local copies, waits for them, and re-layouts: none -> 9.29 us  [the longest x1 6.21 us: on_device(): bulk[:early]]
    squeeze x1 -> x0, local copies, waits for them, and re-layouts: 7.78 us -> none  [on_device(): bulk = lax.dynamic_index_in_dim(block, 1 - sibling, 0, keepdims=False)]
    pallas_call x3 -> x4, Pallas kernels: 56.1 us -> 55.9 us  [the longest x2 22.1 us: on_device(): pl.pallas_call(functools.partial(finish_kernel, start), out_shape=whole,...]
  transfers between devices with their start and end apart: 8 -> 9, of which waited for: 5 -> 6; matrix products, arithmetic and copies ran while one was open for 6% -> 6% of each run, Pallas kernels for 52% -> 52%
where the time goes in v4:
time: 296 us; the launch traced here: 294 us
  Pallas kernels  168 us (57%)
  waiting for transfers between devices  70.1 us (24%)
  local copies, waits for them, and re-layouts  19.1 us (6%)
  starting transfers between devices  16.2 us (5%)
  between operations  13.7 us (5%)
  other arithmetic  7.16 us (2%)
    pallas_call x1, Pallas kernels, on_device(): pl.pallas_call(factor_kernel, out_shape=[jax.ShapeDtypeStruct((2, rows, T...  70.1 us
    pallas_call x1, Pallas kernels, on_device(): pl.pallas_call(pivot_kernel, out_shape=jax.ShapeDtypeStruct((4, 8, 2, TB,...  35.2 us
    ppermute x2, waiting for transfers between devices, on_device(): arrived.append(lax.ppermute(part, ('cube', 'row'), trade))  34 us
    ppermute x4, waiting for transfers between devices, on_device(): lax.ppermute(even if m % 2 == 0 else odd, ('cube', 'row', 'col'), pairs)  25.6 us
    pallas_call x2, Pallas kernels, on_device(): pl.pallas_call(functools.partial(finish_kernel, start), out_shape=whole,...  22.1 us
    pallas_call x1, Pallas kernels, on_device(): pl.pallas_call(update_kernel, out_shape=jax.ShapeDtypeStruct((tiles, cols...  21.8 us
    ppermute x4, starting transfers between devices, on_device(): lax.ppermute(even if m % 2 == 0 else odd, ('cube', 'row', 'col'), pairs)  12.6 us
    pallas_call x1, Pallas kernels, on_device(): pl.pallas_call(keep_kernel, out_shape=whole, grid_spec=pltpu.PrefetchScal...  12 us
  transfers between devices with their start and end apart: 9, of which 6 were waited for; matrix products, arithmetic and copies ran while one was open for 6% of the time, Pallas kernels for 52%

profile of v4, /device:TPU:1, one launch (start us, length us, event | category | flops | bytes accessed | tf_op | source)
XLA Modules:
  0.0 294.2 jit_solution(11952574962103778110)
XLA Ops:
  6.5 0.0 copy-start
  6.5 0.0 copy-start.5
  6.5 0.0 all-gather.4.cloned.1.call-start
  6.5 2.5 slice_bitcast_fusion
  9.1 0.1 copy.21
  9.2 0.0 copy-start.2
  9.2 2.1 collective-permute-start
  11.3 0.0 copy-done
  11.4 0.0 copy-done.5
  11.4 0.1 constant_dynamic-slice_fusion.6
  11.5 0.1 pad_add_fusion
  11.7 0.1 reshape.119
  11.8 3.1 %dynamic-slice_bitcast_fusion.1 = f32[1,128,32,128]{3,2,1,0:T(8,128)} fusion(f32[1,2,4,128,32,128]{5,4,3,2,1,0:T(8,128)} %kept_ref.1, s32[]{:T(128)S(6)} %select_n.80, s32[]{:T(128)S(6)} %add.115), kind=kLoop, calls=%fused_computation.3 | loop fusion | bytes 4194312 | tf_op jit(solution)/shard_map/slice | solution.py:356
  14.9 0.1 broadcast_multiply_fusion
  15.0 0.1 broadcast_compare_fusion
  15.1 0.7 slice_subtract_fusion.cmap_ref
  15.8 0.7 broadcast_select_fusion.1.diag_ref
  16.5 0.7 fusion.rmap_ref
  17.1 6.2 %dynamic-slice_bitcast_fusion = f32[3,128,32,128]{3,2,1,0:T(8,128)} fusion(f32[1,2,4,128,32,128]{5,4,3,2,1,0:T(8,128)} %kept_ref.1, s32[]{:T(128)S(6)} %select_n.80), kind=kLoop, calls=%fused_computation | loop fusion | bytes 12582916 | tf_op jit(solution)/shard_map/slice | solution.py:356
  23.3 0.0 copy-done.2
  23.3 10.4 %collective-permute-done.got_ref = f32[2,2,512,128]{3,2,1,0:T(8,128)S(1)} collective-permute-done((f32[2,2,512,128]{3,2,1,0:T(8,128)S(1)}, f32[2,2,512,128]{3,2,1,0:T(8,128)S(1)}, u32[]{:S(2)}, u32[]{:S(2)}) %collective-permute-start) | collective-permute-done | bytes 1048608 | tf_op jit(solution)/shard_map/ppermute | solution.py:353
  33.8 0.0 copy-start.4
  33.8 1.0 copy-done.4
  34.8 6.7 %shard_map.38 = f32[2,2,512,128]{3,2,1,0:T(8,128)} custom-call(f32[2,2,512,128]{3,2,1,0:T(8,128)} %bitcast.55, f32[2,2,512,128]{3,2,1,0:T(8,128)} %copy-done.4, s32[2,2,4,128]{3,2,1,0:T(4,128)} %fusion.rmap_ref, s32[2,2,128]{2,1,0:T(2,128)} %slice_subtract_fusion.cmap_ref, f32[2,2,4,128]{3,2,1,0:T(4,128)} %broadcast_select_fusion.1.diag_ref), custom_call_target="tpu_custom_call" | custom-call | tf_op jit(solution)/shard_map/pallas_call | solution.py:398
  41.5 2.3 constant_dynamic-slice_fusion.1
  43.8 0.0 copy-start.6
  43.8 0.0 all-gather.4.cloned.1.call-update
  43.8 0.0 all-gather.6.cloned.1.call-start
  43.8 4.0 %collective-permute-start.6 = (f32[2,512,128]{2,1,0:T(8,128)S(1)}, f32[2,512,128]{2,1,0:T(8,128)S(1)}, u32[]{:S(2)}, u32[]{:S(2)}) collective-permute-start(f32[2,512,128]{2,1,0:T(8,128)S(1)} %get-tuple-element.18), channel_id=1, source_target_pairs={{0,76},{1,0},{2,4},{3,72},{4,77},{5,1},{6,5},{7,73},{8,70},{9,10},... | collective-permute-start | bytes 1572872 | tf_op jit(solution)/shard_map/ppermute | solution.py:420
  47.9 0.0 collective-permute-start.4
  47.9 4.9 %collective-permute-start.5 = (f32[2,512,128]{2,1,0:T(8,128)S(1)}, f32[2,512,128]{2,1,0:T(8,128)S(1)}, u32[]{:S(2)}, u32[]{:S(2)}) collective-permute-start(f32[2,512,128]{2,1,0:T(8,128)S(1)} %get-tuple-element.19), channel_id=1, source_target_pairs={{0,72},{1,76},{2,0},{3,4},{4,73},{5,77},{6,1},{7,5},{8,66},{9,70},... | collective-permute-start | bytes 1572872 | tf_op jit(solution)/shard_map/ppermute | solution.py:420
  52.8 3.6 %collective-permute-start.3 = (f32[2,512,128]{2,1,0:T(8,128)S(1)}, f32[2,512,128]{2,1,0:T(8,128)S(1)}, u32[]{:S(2)}, u32[]{:S(2)}) collective-permute-start(f32[2,512,128]{2,1,0:T(8,128)S(1)} %get-tuple-element.19), channel_id=1, source_target_pairs={{0,0},{1,4},{2,72},{3,76},{4,1},{5,5},{6,73},{7,77},{8,10},{9,14},... | collective-permute-start | bytes 1572872 | tf_op jit(solution)/shard_map/ppermute | solution.py:420
  56.4 3.2 %collective-permute-done.6 = f32[2,512,128]{2,1,0:T(8,128)S(1)} collective-permute-done((f32[2,512,128]{2,1,0:T(8,128)S(1)}, f32[2,512,128]{2,1,0:T(8,128)S(1)}, u32[]{:S(2)}, u32[]{:S(2)}) %collective-permute-start.6) | collective-permute-done | bytes 524320 | tf_op jit(solution)/shard_map/ppermute | solution.py:420
  59.6 0.0 collective-permute-done.4
  59.6 19.8 %collective-permute-done.5 = f32[2,512,128]{2,1,0:T(8,128)S(1)} collective-permute-done((f32[2,512,128]{2,1,0:T(8,128)S(1)}, f32[2,512,128]{2,1,0:T(8,128)S(1)}, u32[]{:S(2)}, u32[]{:S(2)}) %collective-permute-start.5) | collective-permute-done | bytes 524320 | tf_op jit(solution)/shard_map/ppermute | solution.py:420
  79.4 2.7 collective-permute-done.3
  82.0 1.5 pad_maximum_fusion
  83.5 0.0 all-gather.6.cloned.1.call-update
  83.6 0.0 copy-done.6
  83.6 0.2 select_reduce_fusion.1
  83.8 0.6 copy.32
  84.4 0.6 pad_add_fusion.1.at_ref
  85.0 0.1 subtract_bitcast_fusion
  85.1 1.2 select_reduce_fusion
  86.3 0.7 broadcast_select_fusion.cinv_ref
  86.9 12.0 %shard_map.37.kept_ref = f32[1,4,128,32,128]{4,3,2,1,0:T(8,128)} custom-call(s32[3]{0:T(128)} %pad_add_fusion.1.at_ref, s32[2,512]{1,0:T(2,128)} %bitcast.63, f32[1,2,4,128,32,128]{5,4,3,2,1,0:T(8,128)} %kept_ref.1, s32[2,32,128]{2,1,0:T(8,128)} %broadcast_select_fusion.cinv_ref), custom_call_target="tpu_custom_call" | custom-call | tf_op jit(solution)/shard_map/pallas_call | solution.py:470
  99.0 0.7 broadcast_select_fusion.2.diag_ref
  99.7 1.4 collective-permute-start.2
  101.0 1.6 slice_bitcast_fusion.1.piece_ref
  102.6 0.1 collective-permute-start.1
  102.7 35.2 %shard_map.39.s_ref = f32[4,8,2,128,128]{4,3,2,1,0:T(8,128)} custom-call(f32[2,128,128]{2,1,0:T(8,128)} %slice_bitcast_fusion.1.piece_ref), custom_call_target="tpu_custom_call" | custom-call | tf_op jit(solution)/shard_map/pallas_call | solution.py:432
  137.9 0.0 all-gather.4.cloned.1.call-done.a_ref
  138.0 70.1 %shard_map.40 = (f32[2,512,128]{2,1,0:T(8,128)}, f32[512,1024]{1,0:T(8,128)}) custom-call(s32[1]{0:T(128)} %bitcast.23.col_ref, f32[4,8,2,128,128]{4,3,2,1,0:T(8,128)} %shard_map.39.s_ref, f32[4,2,512,128]{3,2,1,0:T(8,128)} %all-gather.4.cloned.1.call-done.a_ref), custom_call_target="tpu_custom_call" | custom-call | flops 40000000000 | bytes 8388608 | tf_op jit(solution)/shard_map/pallas_call | solution.py:445
  208.1 0.0 all-gather.6.cloned.1.call-done
  208.1 21.8 %shard_map.41.r_ref = f32[4,4096,128]{2,1,0:T(8,128)} custom-call(s32[3]{0:T(128)} %pad_add_fusion.1.at_ref, f32[8,4,2,512,128]{4,3,2,1,0:T(8,128)} %bitcast.71, f32[512,1024]{1,0:T(8,128)} %get-tuple-element.13.x_ref, f32[2,512,128]{2,1,0:T(8,128)} %get-tuple-element.14.y_ref, f32[4,128]{1,0:T(4,128)} %broadcast_select_fusion.2.diag_ref), custom_call_target="tpu_custom_call" | custom-call | flops 25999998976 | bytes 33554432 | tf_op jit(solution)/shard_map/pallas_call | solution.py:485
  229.9 7.5 %collective-permute-done.2.got_ref = f32[3,128,32,128]{3,2,1,0:T(8,128)} collective-permute-done((f32[3,128,32,128]{3,2,1,0:T(8,128)}, f32[3,128,32,128]{3,2,1,0:T(8,128)}, u32[]{:S(2)}, u32[]{:S(2)}) %collective-permute-start.2) | collective-permute-done | bytes 6291488 | tf_op jit(solution)/shard_map/ppermute | solution.py:359
  237.4 15.0 %shard_map.42.kept_ref = f32[1,4,128,32,128]{4,3,2,1,0:T(8,128)} custom-call(s32[2,512]{1,0:T(2,128)} %bitcast.64, f32[3,128,32,128]{3,2,1,0:T(8,128)} %collective-permute-done.2.got_ref, s32[2,32,128]{2,1,0:T(8,128)} %broadcast_select_fusion.cinv_ref, f32[1,4,128,32,128]{4,3,2,1,0:T(8,128)} %shard_map.37.kept_ref, ...), custom_call_target="tpu_custom_call", output_to_operand_aliasing={{}: (3, {})} | custom-call | tf_op jit(solution)/shard_map/pallas_call | solution.py:509
  252.4 26.5 %collective-permute-done.1.got_ref = f32[1,128,32,128]{3,2,1,0:T(8,128)S(1)} collective-permute-done((f32[1,128,32,128]{3,2,1,0:T(8,128)}, f32[1,128,32,128]{3,2,1,0:T(8,128)S(1)}, u32[]{:S(2)}, u32[]{:S(2)}) %collective-permute-start.1) | collective-permute-done | bytes 2097184 | tf_op jit(solution)/shard_map/ppermute | solution.py:359
  278.9 0.0 copy-start.3
  278.9 1.3 copy-done.3
  280.2 0.0 copy-start.1
  280.2 7.1 %shard_map.43 = f32[1,4,128,32,128]{4,3,2,1,0:T(8,128)} custom-call(s32[2,512]{1,0:T(2,128)} %bitcast.65, f32[1,128,32,128]{3,2,1,0:T(8,128)} %copy-done.3, s32[2,32,128]{2,1,0:T(8,128)} %broadcast_select_fusion.cinv_ref, f32[1,4,128,32,128]{4,3,2,1,0:T(8,128)} %shard_map.42.kept_ref, f32[4,4096,128]{2,1,0:T(8,128)} %shard_map.41.r_ref), custom_call_target="tpu_custom_call", output_to_operand_aliasing={{}: (3, {})} | custom-call | tf_op jit(solution)/shard_map/pallas_call | solution.py:509
  287.3 0.0 copy-done.1
  (12 shorter events, 0.1 us)
Async XLA Ops:
  6.5 4.8 %copy-start = (f32[16384]{0:T(1024)S(1)}, f32[16384]{0:T(1024)}, u32[]{:S(2)}) copy-start(f32[16384]{0:T(1024)} %param.5) | copy-start | bytes 196612
  6.5 4.9 %copy-start.5 = (s32[2,16384]{1,0:T(2,128)S(1)}, s32[2,16384]{1,0:T(2,128)}, u32[]{:S(2)}) copy-start(s32[2,16384]{1,0:T(2,128)} %param.4) | copy-start | bytes 393220
  6.5 131.4 %all-gather.4.cloned.1.call-start = ((), (), s32[]{:S(2)}) async-start(), calls=%async_computation | async-start | bytes 2621440 | tf_op jit(solution)/shard_map/all_gather | solution.py:429
  9.2 14.1 %copy-start.2 = (f32[2,2,4,128,128]{4,3,2,1,0:T(8,128)}, f32[2,2,4,128,128]{4,3,2,1,0:T(8,128)S(1)}, u32[]{:S(2)}) copy-start(f32[2,2,4,128,128]{4,3,2,1,0:T(8,128)S(1)} %copy.21) | copy-start | bytes 3145732
  9.2 24.6 %collective-permute-start = (f32[2,2,512,128]{3,2,1,0:T(8,128)S(1)}, f32[2,2,512,128]{3,2,1,0:T(8,128)S(1)}, u32[]{:S(2)}, u32[]{:S(2)}) collective-permute-start(f32[2,2,512,128]{3,2,1,0:T(8,128)S(1)} %bitcast.54), channel_id=1, source_target_pairs={{0,64},{4,68},{8,72},{12,76},{16,80},{20,84},{24,88},{28,92},{32,9... | collective-permute-start | bytes 3145736 | tf_op jit(solution)/shard_map/ppermute | solution.py:353
  33.8 1.0 copy-start.4
  43.8 39.9 %copy-start.6 = (s32[2,2,4,128]{3,2,1,0:T(4,128)S(1)}, s32[2,2,4,128]{3,2,1,0:T(4,128)}, u32[]{:S(2)}) copy-start(s32[2,2,4,128]{3,2,1,0:T(4,128)} %fusion.rmap_ref) | copy-start | bytes 24580
  43.8 164.3 %all-gather.6.cloned.1.call-start = ((), (), s32[]{:S(2)}) async-start(), calls=%async_computation.1 | async-start | bytes 18874368 | tf_op jit(solution)/shard_map/all_gather | solution.py:427
  43.8 15.8 %collective-permute-start.6 = (f32[2,512,128]{2,1,0:T(8,128)S(1)}, f32[2,512,128]{2,1,0:T(8,128)S(1)}, u32[]{:S(2)}, u32[]{:S(2)}) collective-permute-start(f32[2,512,128]{2,1,0:T(8,128)S(1)} %get-tuple-element.18), channel_id=1, source_target_pairs={{0,76},{1,0},{2,4},{3,72},{4,77},{5,1},{6,5},{7,73},{8,70},{9,10},... | collective-permute-start | bytes 1572872 | tf_op jit(solution)/shard_map/ppermute | solution.py:420
  47.9 11.7 %collective-permute-start.4 = (f32[2,512,128]{2,1,0:T(8,128)S(1)}, f32[2,512,128]{2,1,0:T(8,128)S(1)}, u32[]{:S(2)}, u32[]{:S(2)}) collective-permute-start(f32[2,512,128]{2,1,0:T(8,128)S(1)} %get-tuple-element.18), channel_id=1, source_target_pairs={{0,4},{1,72},{2,76},{3,0},{4,5},{5,73},{6,77},{7,1},{8,14},{9,66},... | collective-permute-start | bytes 1572872 | tf_op jit(solution)/shard_map/ppermute | solution.py:420
  47.9 31.5 %collective-permute-start.5 = (f32[2,512,128]{2,1,0:T(8,128)S(1)}, f32[2,512,128]{2,1,0:T(8,128)S(1)}, u32[]{:S(2)}, u32[]{:S(2)}) collective-permute-start(f32[2,512,128]{2,1,0:T(8,128)S(1)} %get-tuple-element.19), channel_id=1, source_target_pairs={{0,72},{1,76},{2,0},{3,4},{4,73},{5,77},{6,1},{7,5},{8,66},{9,70},... | collective-permute-start | bytes 1572872 | tf_op jit(solution)/shard_map/ppermute | solution.py:420
  52.8 29.3 %collective-permute-start.3 = (f32[2,512,128]{2,1,0:T(8,128)S(1)}, f32[2,512,128]{2,1,0:T(8,128)S(1)}, u32[]{:S(2)}, u32[]{:S(2)}) collective-permute-start(f32[2,512,128]{2,1,0:T(8,128)S(1)} %get-tuple-element.19), channel_id=1, source_target_pairs={{0,0},{1,4},{2,72},{3,76},{4,1},{5,5},{6,73},{7,77},{8,10},{9,14},... | collective-permute-start | bytes 1572872 | tf_op jit(solution)/shard_map/ppermute | solution.py:420
  99.7 137.7 %collective-permute-start.2 = (f32[3,128,32,128]{3,2,1,0:T(8,128)}, f32[3,128,32,128]{3,2,1,0:T(8,128)}, u32[]{:S(2)}, u32[]{:S(2)}) collective-permute-start(f32[3,128,32,128]{3,2,1,0:T(8,128)} %dynamic-slice_bitcast_fusion), channel_id=1, source_target_pairs={{0,64},{4,68},{8,72},{12,76},{16,80},{20,84},{24,88},{28,92},{32,9... | collective-permute-start | bytes 18874376 | tf_op jit(solution)/shard_map/ppermute | solution.py:359
  102.6 176.3 %collective-permute-start.1 = (f32[1,128,32,128]{3,2,1,0:T(8,128)}, f32[1,128,32,128]{3,2,1,0:T(8,128)S(1)}, u32[]{:S(2)}, u32[]{:S(2)}) collective-permute-start(f32[1,128,32,128]{3,2,1,0:T(8,128)} %dynamic-slice_bitcast_fusion.1), channel_id=1, source_target_pairs={{0,64},{4,68},{8,72},{12,76},{16,80},{20,84},{24,88},{28,92},{32,9... | collective-permute-start | bytes 6291464 | tf_op jit(solution)/shard_map/ppermute | solution.py:359
  278.9 1.3 copy-start.3
  280.2 7.1 %copy-start.1 = (f32[16384]{0:T(1024)S(1)}, f32[16384]{0:T(1024)}, u32[]{:S(2)}) copy-start(f32[16384]{0:T(1024)} %param.5) | copy-start | bytes 196612
Sparse Core Ops, SparseCore 0:
  43.9 46.8 all-gather.3
  92.5 92.0 all-gather.5

commit v5 on v4

--- a/solution.py
+++ b/solution.py
@@ -29,7 +29,9 @@
     )
 
 
-def place_kernel(raw_ref, got_ref, rmap_ref, cmap_ref, diag_ref, out_ref):
+def place_kernel(
+    pick_ref, raw_ref, got_ref, rmap_ref, cmap_ref, diag_ref, own_ref, even_ref, odd_ref, piece_ref
+):
     sub = lax.broadcasted_iota(jnp.int32, (TB, TB), 0)
     lane = lax.broadcasted_iota(jnp.int32, (TB, TB), 1)
     tiles = rmap_ref.shape[2]
@@ -45,7 +47,17 @@
                 for t in range(2):
                     hot = (sub == rmap_ref[t, half, j : j + 1, :]).astype(F32)
                     total += nn(hot, cols[t][rows, :])
-                out_ref[half, v, rows, :] = total
+                if half == 0 and j == 0:
+                    piece_ref[v] = total
+                for out_ref, wanted in ((own_ref, pick_ref[0]), (even_ref, pick_ref[1])):
+
+                    @pl.when(wanted == half)
+                    def _():
+                        out_ref[v, rows, :] = total
+
+                @pl.when(pick_ref[1] != half)
+                def _():
+                    odd_ref[v, rows, :] = total
 
 
 def pivot_kernel(piece_ref, out_ref, send, recv, local):
@@ -194,16 +206,13 @@
                 b_rows[g] = b_rows[g] - db
 
 
-def factor_kernel(col_ref, s_ref, a_ref, y_ref, x_ref, m_ref, li_ref, d_ref):
-    blocks = K // TB
+def factor_kernel(s_ref, m_ref, li_ref, d_ref):
+    blocks, pair_width = K // TB, 2 * TB
     for c in range(4):
         for v in range(2):
             u = 4 * v + c
             for p in range(u, blocks):
                 m_ref[p * TB : (p + 1) * TB, u * TB : (u + 1) * TB] = s_ref[c, p, v]
-            m_ref[K:, u * TB : (u + 1) * TB] = a_ref[c, v]
-
-    pair_width = 2 * TB
 
     def step(k, _):
         here = pl.ds(pl.multiple_of(k * TB, TB), TB)
@@ -230,22 +239,52 @@
         return 0
 
     lax.fori_loop(0, blocks, step, 0)
+
+
+def solve_kernel(col_ref, l_ref, li_ref, own_ref, low_ref, high_ref, far_ref, y_ref, x_ref, m_ref):
+    blocks, pair_width = K // TB, 2 * TB
     col = col_ref[0]
+    for part, ref in enumerate((own_ref, high_ref, far_ref, low_ref)):
+        for v in range(2):
+            u = 4 * v + lax.rem(col + part, 4)
+            m_ref[:, pl.ds(pl.multiple_of(u * TB, TB), TB)] = ref[v]
+
+    def places(n):
+        at = n * pair_width
+        return (
+            pl.ds(pl.multiple_of(at, TB), TB),
+            pl.ds(pl.multiple_of(at + TB, TB), TB),
+            pl.ds(pl.multiple_of(at, pair_width), pair_width),
+        )
+
+    def forth(n, _):
+        first, last, pair = places(n)
+        m_ref[:, first] = nt(m_ref[:, first], li_ref[2 * n])
+        rest = m_ref[:, last] - nt(m_ref[:, first], l_ref[last, first])
+        m_ref[:, last] = nt(rest, li_ref[2 * n + 1])
+
+        def trail(i, _):
+            part = places(i)[2]
+            m_ref[:, part] = m_ref[:, part] - nt(m_ref[:, pair], l_ref[part, pair])
+            return 0
+
+        lax.fori_loop(n + 1, blocks // 2, trail, 0)
+        return 0
+
+    lax.fori_loop(0, blocks // 2, forth, 0)
     for v in range(2):
-        y_ref[v] = m_ref[K:, pl.ds(pl.multiple_of((4 * v + col) * TB, TB), TB)]
+        y_ref[v] = m_ref[:, pl.ds(pl.multiple_of((4 * v + col) * TB, TB), TB)]
 
     def back(i, _):
         n = blocks // 2 - 1 - i
-        first = pl.ds(pl.multiple_of(n * pair_width, TB), TB)
-        last = pl.ds(pl.multiple_of(n * pair_width + TB, TB), TB)
-        pair = pl.ds(pl.multiple_of(n * pair_width, pair_width), pair_width)
-        x_ref[:, last] = nn(m_ref[K:, last], li_ref[2 * n + 1])
-        rest = m_ref[K:, first] - nn(x_ref[:, last], m_ref[last, first])
+        first, last, pair = places(n)
+        x_ref[:, last] = nn(m_ref[:, last], li_ref[2 * n + 1])
+        rest = m_ref[:, first] - nn(x_ref[:, last], l_ref[last, first])
         x_ref[:, first] = nn(rest, li_ref[2 * n])
 
         def lead(j, _):
-            part = pl.ds(pl.multiple_of(j * pair_width, pair_width), pair_width)
-            m_ref[K:, part] = m_ref[K:, part] - nn(x_ref[:, pair], m_ref[pair, part])
+            part = places(j)[2]
+            m_ref[:, part] = m_ref[:, part] - nn(x_ref[:, pair], l_ref[pair, part])
             return 0
 
         lax.fori_loop(0, n, lead, 0)
@@ -281,21 +320,24 @@
     place_rows(pl.program_id(0), 0, rinv_ref, cinv_ref, kept_ref.at[0, 0, 0], None, out_ref.at[0, 0])
 
 
-def finish_kernel(start, rinv_ref, got_ref, cinv_ref, kept_ref, r_ref, out_ref):
+def finish_kernel(start, rinv_ref, got_ref, cinv_ref, kept_ref, ra_ref, rb_ref, out_ref):
+    cut = ra_ref.shape[1] // TB
+
     def less(o, g):
-        return kept_ref[0, 0, o, g : g + 8] - r_ref.at[0][pl.ds(g * TB + o, 8, stride=TB), :]
+        ref, at = (ra_ref, g) if g < cut else (rb_ref, g - cut)
+        return kept_ref[0, 0, o, g : g + 8] - ref.at[0][pl.ds(at * TB + o, 8, stride=TB), :]
 
     tile = pl.program_id(0) + start
     place_rows(tile, 1, rinv_ref, cinv_ref, got_ref.at[0], less, out_ref.at[0, 0])
 
 
 def update_kernel(
-    at_ref, g_ref, x_ref, y_ref, diag_ref, out_ref, wh_ref, wl_ref, xh_ref, xl_ref
+    start, at_ref, g_ref, x_ref, y_ref, diag_ref, out_ref, wh_ref, wl_ref, xh_ref, xl_ref
 ):
-    step = pl.program_id(0)
+    step = pl.program_id(0) + start
     tiles = out_ref.shape[0]
 
-    @pl.when(step == 0)
+    @pl.when(step == start)
     def _():
         xh_ref[...], xl_ref[...] = split(x_ref[...])
 
@@ -353,7 +395,8 @@
     got = lax.ppermute(raw, ("cube", "row"), trade)
     early = tiles - 1
     bulk = lax.dynamic_index_in_dim(block, 1 - sibling, 0, keepdims=False)
-    first, second, got = lax.optimization_barrier((bulk[:early], bulk[early:], got))
+    first, got = lax.optimization_barrier((bulk[:early], got))
+    second = bulk[early:]
     arrived = []
     for part in (first, second):
         arrived.append(lax.ppermute(part, ("cube", "row"), trade))
@@ -395,15 +438,17 @@
     meets = pair_tiles[:, None, :] == col_tiles[None, :2, None]
     panel_diag = jnp.where(meets[..., None], pair_diag[:, None], 0.0)
 
-    pieces = pl.pallas_call(
+    strip = jax.ShapeDtypeStruct((2, rows, TB), F32)
+    own, even, odd, piece = pl.pallas_call(
         place_kernel,
-        out_shape=jax.ShapeDtypeStruct((2, 2, rows, TB), F32),
-        in_specs=[VMEM] * 5,
-        out_specs=VMEM,
-    )(raw, got, pair_maps, col_maps[:, :2], panel_diag)
-
-    even = lax.dynamic_index_in_dim(pieces, col % 2, 0, keepdims=False)
-    odd = lax.dynamic_index_in_dim(pieces, 1 - col % 2, 0, keepdims=False)
+        out_shape=[strip, strip, strip, jax.ShapeDtypeStruct((2, TB, TB), F32)],
+        in_specs=[SMEM] + [VMEM] * 5,
+        out_specs=[VMEM] * 4,
+    )(
+        jnp.stack([sibling, col % 2]).astype(jnp.int32),
+        raw, got, pair_maps, col_maps[:, :2], panel_diag,
+    )
+
     quarters = []
     for m in range(4):
         pairs = []
@@ -418,17 +463,18 @@
                             target = ((s ^ far) * 4 + z) * 4 + (half ^ far) * 2 + h
                             pairs.append((source, target * 4 + half * 2 + core))
         quarters.append(lax.ppermute(even if m % 2 == 0 else odd, ("cube", "row", "col"), pairs))
-    turned = jnp.stack(quarters)
     groups = [
         [(s * 4 + z) * 4 + half * 2 + core for z in range(4) for core in range(2)]
         for s in range(2)
         for half in range(2)
     ]
-    others = lax.all_gather(turned, ("cube", "row"), axis=0, axis_index_groups=groups)
-
-    own_rows = lax.all_gather(
-        lax.dynamic_index_in_dim(pieces, sibling, 0, keepdims=False), "col", axis=0
-    )
+    others = []
+    for part in (slice(0, early * TB), slice(early * TB, rows)):
+        turned = jnp.stack([quarter[:, part] for quarter in quarters])
+        others.append(
+            lax.all_gather(turned, ("cube", "row"), axis=0, axis_index_groups=groups)
+        )
+
     pivot = pl.pallas_call(
         pivot_kernel,
         out_shape=jax.ShapeDtypeStruct((4, 8, 2, TB, TB), F32),
@@ -440,23 +486,30 @@
             pltpu.SemaphoreType.DMA,
         ],
         compiler_params=pltpu.CompilerParams(collective_id=0, has_side_effects=True),
-    )(pieces[0, :, :TB])
-
+    )(piece)
+
+    own, pivot = lax.optimization_barrier((own, pivot))
+    strips = []
+    for hop in (1, 3, 2):
+        strips.append(lax.ppermute(own, "col", [(c, (c + hop) % 4) for c in range(4)]))
+
+    lower, inverses = pl.pallas_call(
+        factor_kernel,
+        out_shape=[jax.ShapeDtypeStruct((K, K), F32), jax.ShapeDtypeStruct((K // TB, TB, TB), F32)],
+        in_specs=[VMEM],
+        out_specs=[VMEM, VMEM],
+        scratch_shapes=[pltpu.VMEM((TB, TB), F32)],
+    )(pivot)
     y, x = pl.pallas_call(
-        factor_kernel,
+        solve_kernel,
         out_shape=[
             jax.ShapeDtypeStruct((2, rows, TB), F32),
             jax.ShapeDtypeStruct((rows, K), F32),
         ],
-        in_specs=[SMEM, VMEM, VMEM],
+        in_specs=[SMEM] + [VMEM] * 6,
         out_specs=[VMEM, VMEM],
-        scratch_shapes=[
-            pltpu.VMEM((K + rows, K), F32),
-            pltpu.VMEM((K // TB, TB, TB), F32),
-            pltpu.VMEM((TB, TB), F32),
-        ],
-        cost_estimate=pl.CostEstimate(flops=40_000_000_000, bytes_accessed=8 << 20, transcendentals=0),
-    )(col.reshape(1), pivot, own_rows)
+        scratch_shapes=[pltpu.VMEM((rows, K), F32)],
+    )(col.reshape(1), lower, inverses, own, *strips)
 
     row_inverse = inverse(row_maps).reshape(2, rows)
     solved = jnp.arange(cols) < 2
@@ -482,28 +535,32 @@
             out_specs=pl.BlockSpec((1, 1, TB, cols, TB), lambda i, *_: (0, i, 0, 0, 0)),
         ),
     )(at, row_inverse, child_update, col_inverse)
-    update = pl.pallas_call(
-        update_kernel,
-        out_shape=jax.ShapeDtypeStruct((tiles, cols * TB, TB), F32),
-        grid_spec=pltpu.PrefetchScalarGridSpec(
-            num_scalar_prefetch=1,
-            grid=(cols // 8,),
-            in_specs=[
-                pl.BlockSpec((8, 4, 2, TB, TB), lambda i, *_: (0, 0, 0, i, 0)),
-                VMEM,
-                VMEM,
-                VMEM,
-            ],
-            out_specs=pl.BlockSpec((tiles, 8 * TB, TB), lambda i, *_: (0, i, 0)),
-            scratch_shapes=[
-                pltpu.VMEM((8 * TB, K), jnp.bfloat16),
-                pltpu.VMEM((8 * TB, K), jnp.bfloat16),
-                pltpu.VMEM((rows, K), jnp.bfloat16),
-                pltpu.VMEM((rows, K), jnp.bfloat16),
-            ],
-        ),
-        cost_estimate=pl.CostEstimate(flops=26_000_000_000, bytes_accessed=32 << 20, transcendentals=0),
-    )(at, others, x, y, trailing_diag)
+    updates = []
+    for start, gathered in zip((0, early), others):
+        steps = gathered.shape[3] // TB
+        updates.append(
+            pl.pallas_call(
+                functools.partial(update_kernel, start),
+                out_shape=jax.ShapeDtypeStruct((tiles, steps * 8 * TB, TB), F32),
+                grid_spec=pltpu.PrefetchScalarGridSpec(
+                    num_scalar_prefetch=1,
+                    grid=(steps,),
+                    in_specs=[
+                        pl.BlockSpec((8, 4, 2, TB, TB), lambda i, *_: (0, 0, 0, i, 0)),
+                        VMEM,
+                        VMEM,
+                        VMEM,
+                    ],
+                    out_specs=pl.BlockSpec((tiles, 8 * TB, TB), lambda i, *_: (0, i, 0)),
+                    scratch_shapes=[
+                        pltpu.VMEM((8 * TB, K), jnp.bfloat16),
+                        pltpu.VMEM((8 * TB, K), jnp.bfloat16),
+                        pltpu.VMEM((rows, K), jnp.bfloat16),
+                        pltpu.VMEM((rows, K), jnp.bfloat16),
+                    ],
+                ),
+            )(at, gathered, x, y, trailing_diag)
+        )
     for start, part in zip((0, early), arrived):
         block_at = lambda i, *_, start=start: (0, i + start, 0, 0, 0)
         result = pl.pallas_call(
@@ -516,12 +573,17 @@
                     pl.BlockSpec((1, TB, cols, TB), lambda i, *_: (i, 0, 0, 0)),
                     all_maps,
                     pl.BlockSpec((1, 1, TB, cols, TB), block_at),
-                    pl.BlockSpec((1, cols * TB, TB), lambda i, *_, start=start: (i + start, 0, 0)),
+                    *(
+                        pl.BlockSpec(
+                            (1,) + update.shape[1:], lambda i, *_, start=start: (i + start, 0, 0)
+                        )
+                        for update in updates
+                    ),
                 ],
                 out_specs=pl.BlockSpec((1, 1, TB, cols, TB), block_at),
             ),
             input_output_aliases={3: 0},
-        )(row_inverse, part, col_inverse, result, update)
+        )(row_inverse, part, col_inverse, result, *updates)
     return result
 
 

time: 296 us -> 281 us (0.949)
  waiting for transfers between devices: 70.1 us -> 31.3 us
  Pallas kernels: 168 us -> 189 us
  starting transfers between devices: 16.2 us -> 21.8 us
    ppermute x2, waiting for transfers between devices: 34 us -> 0.01 us  [on_device(): arrived.append(lax.ppermute(part, ('cube', 'row'), trade))]
    pallas_call x3 -> x5, Pallas kernels: 98.7 us -> 115 us  [the longest x1 55.9 us: on_device(): pl.pallas_call(factor_kernel, out_shape=[jax.ShapeDtypeStruct((K, K), F32...]
    ppermute x4, waiting for transfers between devices: 25.6 us -> 18.3 us  [on_device(): lax.ppermute(even if m % 2 == 0 else odd, ('cube', 'row', 'col'), pairs)]
    ppermute x0 -> x3, starting transfers between devices: none -> 5.42 us  [on_device(): lax.ppermute(own, 'col', [(c, (c + hop) % 4) for c in range(4)])]
    pallas_call x1, Pallas kernels: 35.2 us -> 40.5 us  [on_device(): pl.pallas_call(pivot_kernel, out_shape=jax.ShapeDtypeStruct((4, 8, 2, TB,...]
  transfers between devices with their start and end apart: 9 -> 12, of which waited for: 6 -> 4; matrix products, arithmetic and copies ran while one was open for 6% -> 6% of each run, Pallas kernels for 52% -> 61%
where the time goes in v5:
time: 281 us
  Pallas kernels  189 us (67%)
  waiting for transfers between devices  31.3 us (11%)
  starting transfers between devices  21.8 us (8%)
  local copies, waits for them, and re-layouts  16.2 us (6%)
  between operations  13.7 us (5%)
  other arithmetic  8.48 us (3%)
    pallas_call x1, Pallas kernels, on_device(): pl.pallas_call(factor_kernel, out_shape=[jax.ShapeDtypeStruct((K, K), F32...  55.9 us
    pallas_call x1, Pallas kernels, on_device(): pl.pallas_call(pivot_kernel, out_shape=jax.ShapeDtypeStruct((4, 8, 2, TB,...  40.5 us
    pallas_call x2, Pallas kernels, on_device(): pl.pallas_call(functools.partial(update_kernel, start), out_shape=jax.Sha...  26.6 us
    pallas_call x1, Pallas kernels, on_device(): pl.pallas_call(solve_kernel, out_shape=[jax.ShapeDtypeStruct((2, rows, TB...  22.4 us
    pallas_call x2, Pallas kernels, on_device(): pl.pallas_call(functools.partial(finish_kernel, start), out_shape=whole,...  21.3 us
    ppermute x4, waiting for transfers between devices, on_device(): lax.ppermute(even if m % 2 == 0 else odd, ('cube', 'row', 'col'), pairs)  18.3 us
    ppermute x1, waiting for transfers between devices, on_device(): got = lax.ppermute(raw, ('cube', 'row'), trade)  13 us
    ppermute x4, starting transfers between devices, on_device(): lax.ppermute(even if m % 2 == 0 else odd, ('cube', 'row', 'col'), pairs)  12.7 us
  transfers between devices with their start and end apart: 12, of which 4 were waited for; matrix products, arithmetic and copies ran while one was open for 6% of the time, Pallas kernels for 61%

profile of v5, /device:TPU:1, one launch (start us, length us, event | category | flops | bytes accessed | tf_op | source)
XLA Modules:
  0.0 280.7 jit_solution(14503653804515509112)
XLA Ops:
  6.5 0.0 copy-start
  6.5 0.0 all-gather.7.cloned.1.call-start
  6.5 2.5 slice_bitcast_fusion
  9.1 0.1 copy.22
  9.2 0.0 copy-start.2
  9.2 2.1 collective-permute-start.1
  11.3 0.0 copy-done.7
  11.4 0.1 constant_dynamic-slice_fusion.5
  11.5 0.1 pad_add_fusion
  11.6 0.1 reshape.118
  11.9 0.1 broadcast_multiply_fusion
  12.0 0.1 broadcast_compare_fusion
  12.1 0.7 pad_add_fusion.2.pick_ref
  12.7 0.7 slice_subtract_fusion.cmap_ref
  13.4 0.7 broadcast_select_fusion.1.diag_ref
  14.0 0.7 fusion.rmap_ref
  14.7 6.1 %dynamic-slice_bitcast_fusion = f32[3,128,32,128]{3,2,1,0:T(8,128)} fusion(f32[1,2,4,128,32,128]{5,4,3,2,1,0:T(8,128)} %kept_ref.1, s32[]{:T(128)S(6)} %select_n.70), kind=kLoop, calls=%fused_computation | loop fusion | bytes 12582916 | tf_op jit(solution)/shard_map/slice | solution.py:398
  20.8 13.0 %collective-permute-done.1.got_ref = f32[2,2,512,128]{3,2,1,0:T(8,128)S(1)} collective-permute-done((f32[2,2,512,128]{3,2,1,0:T(8,128)S(1)}, f32[2,2,512,128]{3,2,1,0:T(8,128)S(1)}, u32[]{:S(2)}, u32[]{:S(2)}) %collective-permute-start.1) | collective-permute-done | bytes 1048608 | tf_op jit(solution)/shard_map/ppermute | solution.py:395
  33.8 1.0 copy-done.4
  34.8 10.4 %shard_map.38 = (f32[2,512,128]{2,1,0:T(8,128)}, f32[2,512,128]{2,1,0:T(8,128)}, f32[2,512,128]{2,1,0:T(8,128)}, f32[2,128,128]{2,1,0:T(8,128)}) custom-call(s32[2]{0:T(128)} %pad_add_fusion.2.pick_ref, f32[2,2,512,128]{3,2,1,0:T(8,128)} %bitcast.65, f32[2,2,512,128]{3,2,1,0:T(8,128)} %copy-done.4, s32[2,2,4,128]{3,2,1,0:T(4,128)} %fusion.rmap_ref, ...), custom_call_target="tpu_custom_call" | custom-call | tf_op jit(solution)/shard_map/pallas_call | solution.py:442
  45.2 3.9 %collective-permute-start.6 = (f32[2,512,128]{2,1,0:T(8,128)}, f32[2,512,128]{2,1,0:T(8,128)S(1)}, u32[]{:S(2)}, u32[]{:S(2)}) collective-permute-start(f32[2,512,128]{2,1,0:T(8,128)} %get-tuple-element.20), channel_id=1, source_target_pairs={{0,76},{1,0},{2,4},{3,72},{4,77},{5,1},{6,5},{7,73},{8,70},{9,10},... | collective-permute-start | bytes 1572872 | tf_op jit(solution)/shard_map/ppermute | solution.py:465
  49.1 4.9 %collective-permute-start.5 = (f32[2,512,128]{2,1,0:T(8,128)}, f32[2,512,128]{2,1,0:T(8,128)S(1)}, u32[]{:S(2)}, u32[]{:S(2)}) collective-permute-start(f32[2,512,128]{2,1,0:T(8,128)} %get-tuple-element.19), channel_id=1, source_target_pairs={{0,72},{1,76},{2,0},{3,4},{4,73},{5,77},{6,1},{7,5},{8,66},{9,70},... | collective-permute-start | bytes 1572872 | tf_op jit(solution)/shard_map/ppermute | solution.py:465
  54.0 0.8 collective-permute-start.4
  54.8 3.2 %collective-permute-start.3 = (f32[2,512,128]{2,1,0:T(8,128)}, f32[2,512,128]{2,1,0:T(8,128)S(1)}, u32[]{:S(2)}, u32[]{:S(2)}) collective-permute-start(f32[2,512,128]{2,1,0:T(8,128)} %get-tuple-element.19), channel_id=1, source_target_pairs={{0,0},{1,4},{2,72},{3,76},{4,1},{5,5},{6,73},{7,77},{8,10},{9,14},... | collective-permute-start | bytes 1572872 | tf_op jit(solution)/shard_map/ppermute | solution.py:465
  57.9 3.2 %collective-permute-done.6 = f32[2,512,128]{2,1,0:T(8,128)S(1)} collective-permute-done((f32[2,512,128]{2,1,0:T(8,128)}, f32[2,512,128]{2,1,0:T(8,128)S(1)}, u32[]{:S(2)}, u32[]{:S(2)}) %collective-permute-start.6) | collective-permute-done | bytes 524320 | tf_op jit(solution)/shard_map/ppermute | solution.py:465
  61.1 10.8 %collective-permute-done.5 = f32[2,512,128]{2,1,0:T(8,128)S(1)} collective-permute-done((f32[2,512,128]{2,1,0:T(8,128)}, f32[2,512,128]{2,1,0:T(8,128)S(1)}, u32[]{:S(2)}, u32[]{:S(2)}) %collective-permute-start.5) | collective-permute-done | bytes 524320 | tf_op jit(solution)/shard_map/ppermute | solution.py:465
  72.0 0.0 collective-permute-done.4
  72.0 4.3 %collective-permute-done.3 = f32[2,512,128]{2,1,0:T(8,128)S(1)} collective-permute-done((f32[2,512,128]{2,1,0:T(8,128)}, f32[2,512,128]{2,1,0:T(8,128)S(1)}, u32[]{:S(2)}, u32[]{:S(2)}) %collective-permute-start.3) | collective-permute-done | bytes 524320 | tf_op jit(solution)/shard_map/ppermute | solution.py:465
  76.3 0.8 pad_maximum_fusion.1
  77.1 0.0 all-gather.7.cloned.1.call-update
  77.1 0.0 all-gather.5.cloned.1.call-start
  77.3 0.0 copy-start.8
  77.3 1.2 pad_maximum_fusion
  78.6 0.0 all-gather.5.cloned.1.call-update
  78.6 0.1 collective-permute-start.2
  78.7 3.1 %dynamic-slice_bitcast_fusion.1 = f32[1,128,32,128]{3,2,1,0:T(8,128)} fusion(f32[1,2,4,128,32,128]{5,4,3,2,1,0:T(8,128)} %kept_ref.1, s32[]{:T(128)S(6)} %select_n.70, s32[]{:T(128)S(6)} %add.104), kind=kLoop, calls=%fused_computation.3 | loop fusion | bytes 4194312 | tf_op jit(solution)/shard_map/slice | solution.py:399
  81.9 1.4 collective-permute-start
  83.3 0.2 select_reduce_fusion.1
  83.5 0.6 copy.32
  84.1 0.1 subtract_bitcast_fusion
  84.2 1.2 select_reduce_fusion
  85.4 0.7 broadcast_select_fusion.cinv_ref
  86.0 40.5 %shard_map.39.s_ref = f32[4,8,2,128,128]{4,3,2,1,0:T(8,128)} custom-call(f32[2,128,128]{2,1,0:T(8,128)} %get-tuple-element.22.piece_ref), custom_call_target="tpu_custom_call" | custom-call | tf_op jit(solution)/shard_map/pallas_call | solution.py:478
  126.6 0.0 copy-done.5
  126.6 3.1 %collective-permute-start.7 = (f32[2,512,128]{2,1,0:T(8,128)S(1)}, f32[2,512,128]{2,1,0:T(8,128)S(1)}, u32[]{:S(2)}, u32[]{:S(2)}) collective-permute-start(f32[2,512,128]{2,1,0:T(8,128)S(1)} %copy-done.5), channel_id=1, source_target_pairs={{0,1},{1,2},{2,3},{3,0},{4,5},{5,6},{6,7},{7,4},{8,9},{9,10},{10,1... | collective-permute-start | bytes 1572872 | tf_op jit(solution)/shard_map/ppermute | solution.py:494
  129.7 0.0 collective-permute-start.8
  129.7 2.3 collective-permute-start.9
  132.0 0.7 pad_add_fusion.1.at_ref
  132.7 12.1 %shard_map.37.kept_ref = f32[1,4,128,32,128]{4,3,2,1,0:T(8,128)} custom-call(s32[3]{0:T(128)} %pad_add_fusion.1.at_ref, s32[2,512]{1,0:T(2,128)} %bitcast.69, f32[1,2,4,128,32,128]{5,4,3,2,1,0:T(8,128)} %kept_ref.1, s32[2,32,128]{2,1,0:T(8,128)} %broadcast_select_fusion.cinv_ref), custom_call_target="tpu_custom_call" | custom-call | tf_op jit(solution)/shard_map/pallas_call | solution.py:523
  144.8 0.7 broadcast_select_fusion.2.diag_ref
  145.4 55.9 %shard_map.40 = (f32[1024,1024]{1,0:T(8,128)}, f32[8,128,128]{2,1,0:T(8,128)}) custom-call(f32[4,8,2,128,128]{4,3,2,1,0:T(8,128)} %shard_map.39.s_ref), custom_call_target="tpu_custom_call" | custom-call | tf_op jit(solution)/shard_map/pallas_call | solution.py:496
  201.3 0.0 collective-permute-done.7.low_ref
  201.3 0.0 collective-permute-done.8.high_ref
  201.3 0.0 collective-permute-done.9.far_ref
  201.3 0.8 copy-done.6
  202.2 22.4 %shard_map.41 = (f32[2,512,128]{2,1,0:T(8,128)}, f32[512,1024]{1,0:T(8,128)}) custom-call(s32[1]{0:T(128)} %bitcast.22.col_ref, f32[1024,1024]{1,0:T(8,128)} %get-tuple-element.24.l_ref, f32[8,128,128]{2,1,0:T(8,128)} %get-tuple-element.25.li_ref, f32[2,512,128]{2,1,0:T(8,128)} %get-tuple-element.26.own_ref, f32[2,512,128]{2,1,0:T(8,128)} %copy-done.6, ...), custom_call_target="tpu_custom_call" | custom-call | tf_op jit(solution)/shard_map/pallas_call | solution.py:503
  224.5 8.9 %shard_map.43.rb_ref = f32[4,1024,128]{2,1,0:T(8,128)} custom-call(s32[3]{0:T(128)} %pad_add_fusion.1.at_ref, f32[8,4,2,128,128]{4,3,2,1,0:T(8,128)} %bitcast.63, f32[512,1024]{1,0:T(8,128)} %get-tuple-element.27.x_ref, f32[2,512,128]{2,1,0:T(8,128)} %get-tuple-element.28.y_ref, f32[4,128]{1,0:T(4,128)} %broadcast_select_fusion.2.diag_ref), custom_call_target="tpu_custom_call" | custom-call | tf_op jit(solution)/shard_map/pallas_call | solution.py:542
  233.4 17.7 %shard_map.42.ra_ref = f32[4,3072,128]{2,1,0:T(8,128)} custom-call(s32[3]{0:T(128)} %pad_add_fusion.1.at_ref, f32[8,4,2,384,128]{4,3,2,1,0:T(8,128)} %bitcast.62, f32[512,1024]{1,0:T(8,128)} %get-tuple-element.27.x_ref, f32[2,512,128]{2,1,0:T(8,128)} %get-tuple-element.28.y_ref, f32[4,128]{1,0:T(4,128)} %broadcast_select_fusion.2.diag_ref), custom_call_target="tpu_custom_call" | custom-call | tf_op jit(solution)/shard_map/pallas_call | solution.py:542
  251.2 0.0 collective-permute-done.2.got_ref
  251.2 14.3 %shard_map.44.kept_ref = f32[1,4,128,32,128]{4,3,2,1,0:T(8,128)} custom-call(s32[2,512]{1,0:T(2,128)} %bitcast.70, f32[3,128,32,128]{3,2,1,0:T(8,128)} %collective-permute-done.2.got_ref, s32[2,32,128]{2,1,0:T(8,128)} %broadcast_select_fusion.cinv_ref, f32[1,4,128,32,128]{4,3,2,1,0:T(8,128)} %shard_map.37.kept_ref, ...), custom_call_target="tpu_custom_call", output_to_operand_aliasing={{}: (3, {})} | custom-call | tf_op jit(solution)/shard_map/pallas_call | solution.py:566
  265.5 0.0 collective-permute-done.got_ref
  265.5 1.3 copy-done.3
  266.8 7.0 %shard_map.45 = f32[1,4,128,32,128]{4,3,2,1,0:T(8,128)} custom-call(s32[2,512]{1,0:T(2,128)} %bitcast.71, f32[1,128,32,128]{3,2,1,0:T(8,128)} %copy-done.3, s32[2,32,128]{2,1,0:T(8,128)} %broadcast_select_fusion.cinv_ref, f32[1,4,128,32,128]{4,3,2,1,0:T(8,128)} %shard_map.44.kept_ref, ...), custom_call_target="tpu_custom_call", output_to_operand_aliasing={{}: (3, {})} | custom-call | tf_op jit(solution)/shard_map/pallas_call | solution.py:566
  273.8 0.0 copy-done.1
  (31 shorter events, 0.3 us)
Async XLA Ops:
  6.5 5.3 %copy-start = (f32[16384]{0:T(1024)S(1)}, f32[16384]{0:T(1024)}, u32[]{:S(2)}) copy-start(f32[16384]{0:T(1024)} %param.5) | copy-start | bytes 196612
  6.5 4.8 %copy-start.7 = (s32[2,16384]{1,0:T(2,128)S(1)}, s32[2,16384]{1,0:T(2,128)}, u32[]{:S(2)}) copy-start(s32[2,16384]{1,0:T(2,128)} %param.4) | copy-start | bytes 393220
  6.5 218.0 %all-gather.7.cloned.1.call-start = ((), (), s32[]{:S(2)}) async-start(), calls=%async_computation.1 | async-start | bytes 4718592 | tf_op jit(solution)/shard_map/all_gather | solution.py:475
  9.2 11.6 %copy-start.2 = (f32[2,2,4,128,128]{4,3,2,1,0:T(8,128)}, f32[2,2,4,128,128]{4,3,2,1,0:T(8,128)S(1)}, u32[]{:S(2)}) copy-start(f32[2,2,4,128,128]{4,3,2,1,0:T(8,128)S(1)} %copy.22) | copy-start | bytes 3145732
  9.2 24.6 %collective-permute-start.1 = (f32[2,2,512,128]{3,2,1,0:T(8,128)S(1)}, f32[2,2,512,128]{3,2,1,0:T(8,128)S(1)}, u32[]{:S(2)}, u32[]{:S(2)}) collective-permute-start(f32[2,2,512,128]{3,2,1,0:T(8,128)S(1)} %bitcast.64), channel_id=1, source_target_pairs={{0,64},{4,68},{8,72},{12,76},{16,80},{20,84},{24,88},{28,92},{32,9... | collective-permute-start | bytes 3145736 | tf_op jit(solution)/shard_map/ppermute | solution.py:395
  33.8 1.0 copy-start.4
  45.2 15.9 %collective-permute-start.6 = (f32[2,512,128]{2,1,0:T(8,128)}, f32[2,512,128]{2,1,0:T(8,128)S(1)}, u32[]{:S(2)}, u32[]{:S(2)}) collective-permute-start(f32[2,512,128]{2,1,0:T(8,128)} %get-tuple-element.20), channel_id=1, source_target_pairs={{0,76},{1,0},{2,4},{3,72},{4,77},{5,1},{6,5},{7,73},{8,70},{9,10},... | collective-permute-start | bytes 1572872 | tf_op jit(solution)/shard_map/ppermute | solution.py:465
  49.1 22.9 %collective-permute-start.5 = (f32[2,512,128]{2,1,0:T(8,128)}, f32[2,512,128]{2,1,0:T(8,128)S(1)}, u32[]{:S(2)}, u32[]{:S(2)}) collective-permute-start(f32[2,512,128]{2,1,0:T(8,128)} %get-tuple-element.19), channel_id=1, source_target_pairs={{0,72},{1,76},{2,0},{3,4},{4,73},{5,77},{6,1},{7,5},{8,66},{9,70},... | collective-permute-start | bytes 1572872 | tf_op jit(solution)/shard_map/ppermute | solution.py:465
  54.0 18.0 %collective-permute-start.4 = (f32[2,512,128]{2,1,0:T(8,128)}, f32[2,512,128]{2,1,0:T(8,128)S(1)}, u32[]{:S(2)}, u32[]{:S(2)}) collective-permute-start(f32[2,512,128]{2,1,0:T(8,128)} %get-tuple-element.20), channel_id=1, source_target_pairs={{0,4},{1,72},{2,76},{3,0},{4,5},{5,73},{6,77},{7,1},{8,14},{9,66},... | collective-permute-start | bytes 1572872 | tf_op jit(solution)/shard_map/ppermute | solution.py:465
  54.8 21.5 %collective-permute-start.3 = (f32[2,512,128]{2,1,0:T(8,128)}, f32[2,512,128]{2,1,0:T(8,128)S(1)}, u32[]{:S(2)}, u32[]{:S(2)}) collective-permute-start(f32[2,512,128]{2,1,0:T(8,128)} %get-tuple-element.19), channel_id=1, source_target_pairs={{0,0},{1,4},{2,72},{3,76},{4,1},{5,5},{6,73},{7,77},{8,10},{9,14},... | collective-permute-start | bytes 1572872 | tf_op jit(solution)/shard_map/ppermute | solution.py:465
  77.1 156.3 %all-gather.5.cloned.1.call-start = ((), (), s32[]{:S(2)}) async-start(), calls=%async_computation | async-start | bytes 14155776 | tf_op jit(solution)/shard_map/all_gather | solution.py:475
  77.3 6.0 %copy-start.8 = (s32[2,2,4,128]{3,2,1,0:T(4,128)S(1)}, s32[2,2,4,128]{3,2,1,0:T(4,128)}, u32[]{:S(2)}) copy-start(s32[2,2,4,128]{3,2,1,0:T(4,128)} %fusion.rmap_ref) | copy-start | bytes 24580
  78.6 172.6 %collective-permute-start.2 = (f32[3,128,32,128]{3,2,1,0:T(8,128)}, f32[3,128,32,128]{3,2,1,0:T(8,128)}, u32[]{:S(2)}, u32[]{:S(2)}) collective-permute-start(f32[3,128,32,128]{3,2,1,0:T(8,128)} %dynamic-slice_bitcast_fusion), channel_id=1, source_target_pairs={{0,64},{4,68},{8,72},{12,76},{16,80},{20,84},{24,88},{28,92},{32,9... | collective-permute-start | bytes 18874376 | tf_op jit(solution)/shard_map/ppermute | solution.py:402
  78.7 47.9 %copy-start.5 = (f32[2,512,128]{2,1,0:T(8,128)S(1)}, f32[2,512,128]{2,1,0:T(8,128)}, u32[]{:S(2)}) copy-start(f32[2,512,128]{2,1,0:T(8,128)} %get-tuple-element.26.own_ref) | copy-start | bytes 1572868
  81.9 183.6 %collective-permute-start = (f32[1,128,32,128]{3,2,1,0:T(8,128)}, f32[1,128,32,128]{3,2,1,0:T(8,128)S(1)}, u32[]{:S(2)}, u32[]{:S(2)}) collective-permute-start(f32[1,128,32,128]{3,2,1,0:T(8,128)} %dynamic-slice_bitcast_fusion.1), channel_id=1, source_target_pairs={{0,64},{4,68},{8,72},{12,76},{16,80},{20,84},{24,88},{28,92},{32,9... | collective-permute-start | bytes 6291464 | tf_op jit(solution)/shard_map/ppermute | solution.py:402
  126.6 74.7 %collective-permute-start.7 = (f32[2,512,128]{2,1,0:T(8,128)S(1)}, f32[2,512,128]{2,1,0:T(8,128)S(1)}, u32[]{:S(2)}, u32[]{:S(2)}) collective-permute-start(f32[2,512,128]{2,1,0:T(8,128)S(1)} %copy-done.5), channel_id=1, source_target_pairs={{0,1},{1,2},{2,3},{3,0},{4,5},{5,6},{6,7},{7,4},{8,9},{9,10},{10,1... | collective-permute-start | bytes 1572872 | tf_op jit(solution)/shard_map/ppermute | solution.py:494
  129.7 71.6 %collective-permute-start.8 = (f32[2,512,128]{2,1,0:T(8,128)S(1)}, f32[2,512,128]{2,1,0:T(8,128)}, u32[]{:S(2)}, u32[]{:S(2)}) collective-permute-start(f32[2,512,128]{2,1,0:T(8,128)S(1)} %copy-done.5), channel_id=1, source_target_pairs={{0,3},{1,0},{2,1},{3,2},{4,7},{5,4},{6,5},{7,6},{8,11},{9,8},{10,9... | collective-permute-start | bytes 1572872 | tf_op jit(solution)/shard_map/ppermute | solution.py:494
  129.7 71.6 %collective-permute-start.9 = (f32[2,512,128]{2,1,0:T(8,128)S(1)}, f32[2,512,128]{2,1,0:T(8,128)}, u32[]{:S(2)}, u32[]{:S(2)}) collective-permute-start(f32[2,512,128]{2,1,0:T(8,128)S(1)} %copy-done.5), channel_id=1, source_target_pairs={{0,2},{1,3},{2,0},{3,1},{4,6},{5,7},{6,4},{7,5},{8,10},{9,11},{10,... | collective-permute-start | bytes 1572872 | tf_op jit(solution)/shard_map/ppermute | solution.py:494
  201.3 0.9 copy-start.6
  265.5 1.3 copy-start.3
  266.8 7.0 %copy-start.1 = (f32[16384]{0:T(1024)S(1)}, f32[16384]{0:T(1024)}, u32[]{:S(2)}) copy-start(f32[16384]{0:T(1024)} %param.5) | copy-start | bytes 196612
Sparse Core Ops, SparseCore 0:
  77.3 40.4 all-gather.6
  119.4 66.9 all-gather.4

commit v6 on v5

--- a/solution.py
+++ b/solution.py
@@ -14,6 +14,7 @@
 F32 = jnp.float32
 MESH = pl.DeviceIdType.MESH
 VMEM = pl.BlockSpec(memory_space=pltpu.VMEM)
+ANY = pl.BlockSpec(memory_space=pl.ANY)
 SMEM = pl.BlockSpec(memory_space=pltpu.SMEM)
 
 
@@ -30,7 +31,7 @@
 
 
 def place_kernel(
-    pick_ref, raw_ref, got_ref, rmap_ref, cmap_ref, diag_ref, own_ref, even_ref, odd_ref, piece_ref
+    pick_ref, raw_ref, got_ref, rmap_ref, cmap_ref, diag_ref, own_ref, even_ref, odd_ref, piece_ref, hold_ref
 ):
     sub = lax.broadcasted_iota(jnp.int32, (TB, TB), 0)
     lane = lax.broadcasted_iota(jnp.int32, (TB, TB), 1)
@@ -49,21 +50,18 @@
                     total += nn(hot, cols[t][rows, :])
                 if half == 0 and j == 0:
                     piece_ref[v] = total
-                for out_ref, wanted in ((own_ref, pick_ref[0]), (even_ref, pick_ref[1])):
-
-                    @pl.when(wanted == half)
-                    def _():
-                        out_ref[v, rows, :] = total
-
-                @pl.when(pick_ref[1] != half)
-                def _():
-                    odd_ref[v, rows, :] = total
-
-
-def pivot_kernel(piece_ref, out_ref, send, recv, local):
+                hold_ref[jnp.where(pick_ref[0] == half, 0, 3), v, rows, :] = total
+                hold_ref[jnp.where(pick_ref[1] == half, 1, 2), v, rows, :] = total
+    for n, out_ref in enumerate((own_ref, even_ref, odd_ref)):
+        out_ref[...] = hold_ref[n]
+
+
+def pivot_kernel(
+    piece_ref, even_ref, odd_ref, out_ref, turned_ref, send, recv, local, send_turned, recv_turned
+):
     cube, row, col = lax.axis_index("cube"), lax.axis_index("row"), lax.axis_index("col")
     z = lax.rem(cube, 4)
-    core = lax.rem(row, 2)
+    core, half = lax.rem(row, 2), row // 2
     at = lambda cu, ro, co: {"cube": cu, "row": ro, "col": co}
     mates = [at((cube - z) + lax.rem(z + d, 4), row, col) for d in (1, 2, 3)]
     across = at(lax.rem(cube + 4, 8), lax.rem(row + 2, 4), col)
@@ -73,7 +71,49 @@
     barrier = pltpu.get_barrier_semaphore()
     for peer in mates + [across] + sides + [other]:
         pl.semaphore_signal(barrier, inc=1, device_id=peer, device_id_type=MESH)
-    pl.semaphore_wait(barrier, 7)
+    side = cube // 4
+    alone = row == col
+
+    def to_kind(kind):
+        far, h = kind // 2, lax.rem(kind, 2)
+        x = lax.rem(side + far, 2) * 4 + z
+        return at(x, lax.rem(half + far, 2) * 2 + h, row)
+
+    crossed = lax.rem(half + col // 2, 2)
+    sender = lambda y: at(
+        lax.rem(side + crossed, 2) * 4 + z, col, y
+    )
+    for y in range(4):
+
+        @pl.when(jnp.logical_not(jnp.logical_and(alone, col == y)))
+        def _():
+            pl.semaphore_signal(barrier, inc=1, device_id=sender(y), device_id_type=MESH)
+
+    @pl.when(alone)
+    def _():
+        pl.semaphore_wait(barrier, 10)
+
+    @pl.when(jnp.logical_not(alone))
+    def _():
+        pl.semaphore_wait(barrier, 11)
+
+    def quarter(m):
+        return pltpu.make_async_remote_copy(
+            src_ref=(odd_ref if m % 2 else even_ref),
+            dst_ref=turned_ref.at[m],
+            send_sem=send_turned.at[m],
+            recv_sem=recv_turned.at[m],
+            device_id=to_kind(lax.rem(m + col, 4)),
+            device_id_type=MESH,
+        )
+
+    def stays(m):
+        return jnp.logical_and(alone, lax.rem(m + col, 4) == core)
+
+    def keep_quarter(m):
+        return pltpu.make_async_copy(
+            odd_ref if m % 2 else even_ref, turned_ref.at[m], send_turned.at[m]
+        )
 
     def copy(c, p, slot, peer, width):
         part = out_ref.at[c, p, pl.ds(0, width)]
@@ -118,6 +158,16 @@
         copy(col, p, 11 + n, sides[0], zz + 1).start()
         copy(col, p, 13 + n, sides[1], zz + 1).start()
         copy(col, p, 15 + n, other, zz + 1).start()
+    for m in range(4):
+
+        @pl.when(stays(m))
+        def _():
+            keep_quarter(m).start()
+
+        @pl.when(jnp.logical_not(stays(m)))
+        def _():
+            quarter(m).start()
+
     for i, who in enumerate((row, opposite)):
         for zz in range(2):
             p = zz * 4 + who
@@ -156,6 +206,16 @@
 
         for i in (3, 5, 7, 9, 11, 13, 15, 17, 19, 21, 23, 25, 27, 29, 31):
             copy(col, row, i + zz, other, zz + 1).wait_send()
+
+    for m in range(4):
+
+        @pl.when(stays(m))
+        def _():
+            keep_quarter(m).wait()
+
+        @pl.when(jnp.logical_not(stays(m)))
+        def _():
+            quarter(m).wait()
 
 
 def leaf(d_ref, li_ref):
@@ -316,28 +376,37 @@
     lax.fori_loop(0, TB, body, 0, unroll=16)
 
 
-def keep_kernel(at_ref, rinv_ref, kept_ref, cinv_ref, out_ref):
-    place_rows(pl.program_id(0), 0, rinv_ref, cinv_ref, kept_ref.at[0, 0, 0], None, out_ref.at[0, 0])
-
-
-def finish_kernel(start, rinv_ref, got_ref, cinv_ref, kept_ref, ra_ref, rb_ref, out_ref):
-    cut = ra_ref.shape[1] // TB
-
+def keep_kernel(
+    at_ref, rinv_ref, kept_ref, sent_ref, cinv_ref, out_ref, early_ref, late_ref
+):
+    step, steps = pl.program_id(0), pl.num_programs(0)
+
+    @pl.when(step < steps - 1)
+    def _():
+        early_ref[0] = sent_ref[0, 0, 0]
+
+    @pl.when(step == steps - 1)
+    def _():
+        late_ref[0] = sent_ref[0, 0, 0]
+
+    place_rows(step, 0, rinv_ref, cinv_ref, kept_ref.at[0, 0, 0], None, out_ref.at[0, 0])
+
+
+def finish_kernel(start, rinv_ref, got_ref, cinv_ref, kept_ref, r_ref, out_ref):
     def less(o, g):
-        ref, at = (ra_ref, g) if g < cut else (rb_ref, g - cut)
-        return kept_ref[0, 0, o, g : g + 8] - ref.at[0][pl.ds(at * TB + o, 8, stride=TB), :]
+        return kept_ref[0, 0, o, g : g + 8] - r_ref.at[0][pl.ds(g * TB + o, 8, stride=TB), :]
 
     tile = pl.program_id(0) + start
     place_rows(tile, 1, rinv_ref, cinv_ref, got_ref.at[0], less, out_ref.at[0, 0])
 
 
 def update_kernel(
-    start, at_ref, g_ref, x_ref, y_ref, diag_ref, out_ref, wh_ref, wl_ref, xh_ref, xl_ref
+    at_ref, g_ref, x_ref, y_ref, diag_ref, out_ref, wh_ref, wl_ref, xh_ref, xl_ref
 ):
-    step = pl.program_id(0) + start
+    step = pl.program_id(0)
     tiles = out_ref.shape[0]
 
-    @pl.when(step == start)
+    @pl.when(step == 0)
     def _():
         xh_ref[...], xl_ref[...] = split(x_ref[...])
 
@@ -394,13 +463,6 @@
     raw = jnp.transpose(block[:, :, :, :2, :], (0, 3, 1, 2, 4)).reshape(2, 2, rows, TB)
     got = lax.ppermute(raw, ("cube", "row"), trade)
     early = tiles - 1
-    bulk = lax.dynamic_index_in_dim(block, 1 - sibling, 0, keepdims=False)
-    first, got = lax.optimization_barrier((bulk[:early], got))
-    second = bulk[early:]
-    arrived = []
-    for part in (first, second):
-        arrived.append(lax.ppermute(part, ("cube", "row"), trade))
-
     maps = jnp.stack(
         [
             lax.dynamic_index_in_dim(child_map, sibling, 0, keepdims=False),
@@ -438,56 +500,80 @@
     meets = pair_tiles[:, None, :] == col_tiles[None, :2, None]
     panel_diag = jnp.where(meets[..., None], pair_diag[:, None], 0.0)
 
+    row_inverse = inverse(row_maps).reshape(2, rows)
+    solved = jnp.arange(cols) < 2
+    col_inverse = jnp.where(solved[None, :, None], -1, inverse(col_maps))
+    here = jnp.logical_and(row == col, jnp.logical_or(jnp.arange(tiles) > 0, cube >= 2))
+    trailing_diag = jnp.where(here[:, None], diag, 0.0)
+    crossed = (row // 2 != col // 2).astype(jnp.int32)
+    at = jnp.stack([sibling, cube, 2 * crossed]).astype(jnp.int32)
+    whole = jax.ShapeDtypeStruct((1, tiles, TB, cols, TB), F32)
+    all_maps = pl.BlockSpec((2, cols, TB), lambda i, *_: (0, 0, 0))
+    result, first, second = pl.pallas_call(
+        keep_kernel,
+        out_shape=[
+            whole,
+            jax.ShapeDtypeStruct((early, TB, cols, TB), F32),
+            jax.ShapeDtypeStruct((tiles - early, TB, cols, TB), F32),
+        ],
+        grid_spec=pltpu.PrefetchScalarGridSpec(
+            num_scalar_prefetch=2,
+            grid=(tiles,),
+            in_specs=[
+                pl.BlockSpec(
+                    (1, 1, 1, TB, cols, TB), lambda i, at, _: (0, at[0], i, 0, 0, 0)
+                ),
+                pl.BlockSpec((1, 1, 1, TB, cols, TB), lambda i, at, _: (0, 1 - at[0], i, 0, 0, 0)),
+                all_maps,
+            ],
+            out_specs=[
+                pl.BlockSpec((1, 1, TB, cols, TB), lambda i, *_: (0, i, 0, 0, 0)),
+                pl.BlockSpec((1, TB, cols, TB), lambda i, *_: (jnp.minimum(i, early - 1), 0, 0, 0)),
+                pl.BlockSpec((1, TB, cols, TB), lambda i, *_: (0, 0, 0, 0)),
+            ],
+        ),
+    )(at, row_inverse, child_update, child_update, col_inverse)
+    first, second, got = lax.optimization_barrier((first, second, got))
+    arrived = []
+    for part in (first, second):
+        arrived.append(lax.ppermute(part, ("cube", "row"), trade))
+
     strip = jax.ShapeDtypeStruct((2, rows, TB), F32)
     own, even, odd, piece = pl.pallas_call(
         place_kernel,
         out_shape=[strip, strip, strip, jax.ShapeDtypeStruct((2, TB, TB), F32)],
         in_specs=[SMEM] + [VMEM] * 5,
         out_specs=[VMEM] * 4,
+        scratch_shapes=[pltpu.VMEM((4, 2, rows, TB), F32)],
     )(
         jnp.stack([sibling, col % 2]).astype(jnp.int32),
         raw, got, pair_maps, col_maps[:, :2], panel_diag,
     )
 
-    quarters = []
-    for m in range(4):
-        pairs = []
-        for s in range(2):
-            for z in range(4):
-                for half in range(2):
-                    for core in range(2):
-                        for y in range(4):
-                            kind = (m + y) % 4
-                            far, h = kind // 2, kind % 2
-                            source = ((s * 4 + z) * 4 + half * 2 + core) * 4 + y
-                            target = ((s ^ far) * 4 + z) * 4 + (half ^ far) * 2 + h
-                            pairs.append((source, target * 4 + half * 2 + core))
-        quarters.append(lax.ppermute(even if m % 2 == 0 else odd, ("cube", "row", "col"), pairs))
+    pivot, turned = pl.pallas_call(
+        pivot_kernel,
+        out_shape=[
+            jax.ShapeDtypeStruct((4, 8, 2, TB, TB), F32),
+            jax.ShapeDtypeStruct((4, 2, rows, TB), F32),
+        ],
+        in_specs=[VMEM, ANY, ANY],
+        out_specs=[VMEM, ANY],
+        scratch_shapes=[
+            pltpu.SemaphoreType.DMA((33,)),
+            pltpu.SemaphoreType.DMA((4, 8)),
+            pltpu.SemaphoreType.DMA,
+            pltpu.SemaphoreType.DMA((4,)),
+            pltpu.SemaphoreType.DMA((4,)),
+        ],
+        compiler_params=pltpu.CompilerParams(collective_id=0, has_side_effects=True),
+    )(piece, even, odd)
+
     groups = [
         [(s * 4 + z) * 4 + half * 2 + core for z in range(4) for core in range(2)]
         for s in range(2)
         for half in range(2)
     ]
-    others = []
-    for part in (slice(0, early * TB), slice(early * TB, rows)):
-        turned = jnp.stack([quarter[:, part] for quarter in quarters])
-        others.append(
-            lax.all_gather(turned, ("cube", "row"), axis=0, axis_index_groups=groups)
-        )
-
-    pivot = pl.pallas_call(
-        pivot_kernel,
-        out_shape=jax.ShapeDtypeStruct((4, 8, 2, TB, TB), F32),
-        in_specs=[VMEM],
-        out_specs=VMEM,
-        scratch_shapes=[
-            pltpu.SemaphoreType.DMA((33,)),
-            pltpu.SemaphoreType.DMA((4, 8)),
-            pltpu.SemaphoreType.DMA,
-        ],
-        compiler_params=pltpu.CompilerParams(collective_id=0, has_side_effects=True),
-    )(piece)
-
+    others = lax.all_gather(turned, ("cube", "row"), axis=0, axis_index_groups=groups)
     own, pivot = lax.optimization_barrier((own, pivot))
     strips = []
     for hop in (1, 3, 2):
@@ -511,56 +597,27 @@
         scratch_shapes=[pltpu.VMEM((rows, K), F32)],
     )(col.reshape(1), lower, inverses, own, *strips)
 
-    row_inverse = inverse(row_maps).reshape(2, rows)
-    solved = jnp.arange(cols) < 2
-    col_inverse = jnp.where(solved[None, :, None], -1, inverse(col_maps))
-    here = jnp.logical_and(row == col, jnp.logical_or(jnp.arange(tiles) > 0, cube >= 2))
-    trailing_diag = jnp.where(here[:, None], diag, 0.0)
-    crossed = (row // 2 != col // 2).astype(jnp.int32)
-    at = jnp.stack([sibling, cube, 2 * crossed]).astype(jnp.int32)
-    whole = jax.ShapeDtypeStruct((1, tiles, TB, cols, TB), F32)
-    all_maps = pl.BlockSpec((2, cols, TB), lambda i, *_: (0, 0, 0))
-    result = pl.pallas_call(
-        keep_kernel,
-        out_shape=whole,
+    update = pl.pallas_call(
+        update_kernel,
+        out_shape=jax.ShapeDtypeStruct((tiles, cols * TB, TB), F32),
         grid_spec=pltpu.PrefetchScalarGridSpec(
-            num_scalar_prefetch=2,
-            grid=(tiles,),
+            num_scalar_prefetch=1,
+            grid=(cols // 8,),
             in_specs=[
-                pl.BlockSpec(
-                    (1, 1, 1, TB, cols, TB), lambda i, at, _: (0, at[0], i, 0, 0, 0)
-                ),
-                all_maps,
+                pl.BlockSpec((8, 4, 2, TB, TB), lambda i, *_: (0, 0, 0, i, 0)),
+                VMEM,
+                VMEM,
+                VMEM,
             ],
-            out_specs=pl.BlockSpec((1, 1, TB, cols, TB), lambda i, *_: (0, i, 0, 0, 0)),
+            out_specs=pl.BlockSpec((tiles, 8 * TB, TB), lambda i, *_: (0, i, 0)),
+            scratch_shapes=[
+                pltpu.VMEM((8 * TB, K), jnp.bfloat16),
+                pltpu.VMEM((8 * TB, K), jnp.bfloat16),
+                pltpu.VMEM((rows, K), jnp.bfloat16),
+                pltpu.VMEM((rows, K), jnp.bfloat16),
+            ],
         ),
-    )(at, row_inverse, child_update, col_inverse)
-    updates = []
-    for start, gathered in zip((0, early), others):
-        steps = gathered.shape[3] // TB
-        updates.append(
-            pl.pallas_call(
-                functools.partial(update_kernel, start),
-                out_shape=jax.ShapeDtypeStruct((tiles, steps * 8 * TB, TB), F32),
-                grid_spec=pltpu.PrefetchScalarGridSpec(
-                    num_scalar_prefetch=1,
-                    grid=(steps,),
-                    in_specs=[
-                        pl.BlockSpec((8, 4, 2, TB, TB), lambda i, *_: (0, 0, 0, i, 0)),
-                        VMEM,
-                        VMEM,
-                        VMEM,
-                    ],
-                    out_specs=pl.BlockSpec((tiles, 8 * TB, TB), lambda i, *_: (0, i, 0)),
-                    scratch_shapes=[
-                        pltpu.VMEM((8 * TB, K), jnp.bfloat16),
-                        pltpu.VMEM((8 * TB, K), jnp.bfloat16),
-                        pltpu.VMEM((rows, K), jnp.bfloat16),
-                        pltpu.VMEM((rows, K), jnp.bfloat16),
-                    ],
-                ),
-            )(at, gathered, x, y, trailing_diag)
-        )
+    )(at, others, x, y, trailing_diag)
     for start, part in zip((0, early), arrived):
         block_at = lambda i, *_, start=start: (0, i + start, 0, 0, 0)
         result = pl.pallas_call(
@@ -573,17 +630,12 @@
                     pl.BlockSpec((1, TB, cols, TB), lambda i, *_: (i, 0, 0, 0)),
                     all_maps,
                     pl.BlockSpec((1, 1, TB, cols, TB), block_at),
-                    *(
-                        pl.BlockSpec(
-                            (1,) + update.shape[1:], lambda i, *_, start=start: (i + start, 0, 0)
-                        )
-                        for update in updates
-                    ),
+                    pl.BlockSpec((1, cols * TB, TB), lambda i, *_, start=start: (i + start, 0, 0)),
                 ],
                 out_specs=pl.BlockSpec((1, 1, TB, cols, TB), block_at),
             ),
             input_output_aliases={3: 0},
-        )(row_inverse, part, col_inverse, result, *updates)
+        )(row_inverse, part, col_inverse, result, update)
     return result
 
 

time: 281 us -> 296 us (1.053)
  waiting for transfers between devices: 31.3 us -> 61.2 us
  starting transfers between devices: 21.8 us -> 5.75 us
  Pallas kernels: 189 us -> 202 us
  local copies, waits for them, and re-layouts: 16.2 us -> 6.89 us
    ppermute x2, waiting for transfers between devices: 0.01 us -> 61.1 us  [on_device(): arrived.append(lax.ppermute(part, ('cube', 'row'), trade))]
    ppermute x4 -> x0, waiting for transfers between devices: 18.3 us -> none  [on_device(): lax.ppermute(even if m % 2 == 0 else odd, ('cube', 'row', 'col'), pairs)]
    pallas_call x4 -> x3, Pallas kernels: 79.2 us -> 94.4 us  [the longest x1 55 us: on_device(): pl.pallas_call(pivot_kernel, out_shape=[jax.ShapeDtypeStruct((4, 8, 2, TB...]
    ppermute x1, waiting for transfers between devices: 13 us -> 0.01 us  [on_device(): got = lax.ppermute(raw, ('cube', 'row'), trade)]
    ppermute x4 -> x0, starting transfers between devices: 12.7 us -> none  [on_device(): lax.ppermute(even if m % 2 == 0 else odd, ('cube', 'row', 'col'), pairs)]
    slice x2 -> x0, local copies, waits for them, and re-layouts: 9.23 us -> none  [the longest x1 6.09 us: on_device(): first, got = lax.optimization_barrier((bulk[:early], got))]
    ppermute x3, starting transfers between devices: 5.42 us -> 2.1 us  [on_device(): lax.ppermute(own, 'col', [(c, (c + hop) % 4) for c in range(4)])]
    pallas_call x1, Pallas kernels: 10.4 us -> 7.12 us  [on_device(): pl.pallas_call(place_kernel, out_shape=[strip, strip, strip, jax.ShapeDty...]
  transfers between devices with their start and end apart: 12 -> 7, of which waited for: 4 -> 2; matrix products, arithmetic and copies ran while one was open for 6% -> 2% of each run, Pallas kernels for 61% -> 45%
where the time goes in v6:
time: 296 us; the launch traced here: 295 us
  Pallas kernels  202 us (68%)
  waiting for transfers between devices  61.2 us (21%)
  between operations  13.6 us (5%)
  local copies, waits for them, and re-layouts  6.89 us (2%)
  starting transfers between devices  5.75 us (2%)
  other arithmetic  5.7 us (2%)
    ppermute x2, waiting for transfers between devices, on_device(): arrived.append(lax.ppermute(part, ('cube', 'row'), trade))  61.1 us
    pallas_call x1, Pallas kernels, on_device(): pl.pallas_call(factor_kernel, out_shape=[jax.ShapeDtypeStruct((K, K), F32...  56.2 us
    pallas_call x1, Pallas kernels, on_device(): pl.pallas_call(pivot_kernel, out_shape=[jax.ShapeDtypeStruct((4, 8, 2, TB...  55 us
    pallas_call x1, Pallas kernels, on_device(): pl.pallas_call(solve_kernel, out_shape=[jax.ShapeDtypeStruct((2, rows, TB...  22.5 us
    pallas_call x2, Pallas kernels, on_device(): pl.pallas_call(functools.partial(finish_kernel, start), out_shape=whole,...  22 us
    pallas_call x1, Pallas kernels, on_device(): pl.pallas_call(update_kernel, out_shape=jax.ShapeDtypeStruct((tiles, cols...  22 us
    pallas_call x1, Pallas kernels, on_device(): pl.pallas_call(keep_kernel, out_shape=[whole, jax.ShapeDtypeStruct((early...  17.4 us
    pallas_call x1, Pallas kernels, on_device(): pl.pallas_call(place_kernel, out_shape=[strip, strip, strip, jax.ShapeDty...  7.12 us
  transfers between devices with their start and end apart: 7, of which 2 were waited for; matrix products, arithmetic and copies ran while one was open for 2% of the time, Pallas kernels for 45%

profile of v6, /device:TPU:1, one launch (start us, length us, event | category | flops | bytes accessed | tf_op | source)
XLA Modules:
  0.0 295.5 jit_solution(9880240190575852004)
XLA Ops:
  6.5 0.0 copy-start
  6.5 0.0 copy-start.7
  6.5 0.0 all-gather.3.cloned.1.call-start
  6.5 2.5 slice_bitcast_fusion
  9.1 0.1 copy.22
  9.2 0.0 copy-start.2
  9.2 2.1 collective-permute-start
  11.4 0.0 copy-done.7
  11.4 0.1 constant_dynamic-slice_fusion.5
  11.5 0.1 pad_add_fusion
  11.7 0.1 reshape.114
  11.8 0.1 subtract_bitcast_fusion
  11.9 1.2 select_reduce_fusion
  13.1 0.0 copy-done
  13.2 0.1 broadcast_multiply_fusion
  13.2 0.1 fusion.rmap_ref
  13.3 0.0 copy-start.8
  13.3 0.2 select_reduce_fusion.1
  13.5 0.6 pad_add_fusion.1.at_ref
  14.1 0.6 copy.32
  14.7 0.7 broadcast_select_fusion.cinv_ref
  15.4 17.4 %shard_map.37 = (f32[1,4,128,32,128]{4,3,2,1,0:T(8,128)}, f32[3,128,32,128]{3,2,1,0:T(8,128)}, f32[1,128,32,128]{3,2,1,0:T(8,128)}) custom-call(s32[3]{0:T(128)} %pad_add_fusion.1.at_ref, s32[2,512]{1,0:T(2,128)} %bitcast.47, f32[1,2,4,128,32,128]{5,4,3,2,1,0:T(8,128)} %sent_ref.1, f32[1,2,4,128,32,128]{5,4,3,2,1,0:T(8,128)} %sent_ref.1, ...), custom_call_target="tpu_custom_call" | custom-call | tf_op jit(solution)/shard_map/pallas_call | solution.py:512
  32.8 0.0 copy-done.2
  32.8 0.0 copy-done.8
  32.8 0.6 pad_add_fusion.2.pick_ref
  33.4 0.1 broadcast_compare_fusion
  33.5 0.7 slice_subtract_fusion.cmap_ref
  34.1 0.7 broadcast_select_fusion.1.diag_ref
  34.8 0.0 collective-permute-done.got_ref
  34.8 0.0 copy-start.4
  34.8 1.0 copy-done.4
  35.8 7.1 %shard_map.38 = (f32[2,512,128]{2,1,0:T(8,128)}, f32[2,512,128]{2,1,0:T(8,128)}, f32[2,512,128]{2,1,0:T(8,128)}, f32[2,128,128]{2,1,0:T(8,128)}) custom-call(s32[2]{0:T(128)} %pad_add_fusion.2.pick_ref, f32[2,2,512,128]{3,2,1,0:T(8,128)} %bitcast.43, f32[2,2,512,128]{3,2,1,0:T(8,128)} %copy-done.4, s32[2,2,4,128]{3,2,1,0:T(4,128)} %copy-done.8, ...), custom_call_target="tpu_custom_call" | custom-call | tf_op jit(solution)/shard_map/pallas_call | solution.py:542
  42.9 55.0 %shard_map.39 = (f32[4,8,2,128,128]{4,3,2,1,0:T(8,128)}, f32[4,2,512,128]{3,2,1,0:T(8,128)}) custom-call(f32[2,128,128]{2,1,0:T(8,128)} %get-tuple-element.29.piece_ref, f32[2,512,128]{2,1,0:T(8,128)} %get-tuple-element.30.even_ref, f32[2,512,128]{2,1,0:T(8,128)} %get-tuple-element.31.odd_ref), custom_call_target="tpu_custom_call" | custom-call | tf_op jit(solution)/shard_map/pallas_call | solution.py:553
  97.9 0.0 all-gather.3.cloned.1.call-update
  98.0 0.1 collective-permute-start.2
  98.1 1.5 collective-permute-start.1
  99.5 0.6 collective-permute-start.5
  100.1 0.0 collective-permute-start.4
  100.1 1.5 collective-permute-start.3
  101.6 0.7 broadcast_select_fusion.2.diag_ref
  102.3 56.2 %shard_map.40 = (f32[1024,1024]{1,0:T(8,128)}, f32[8,128,128]{2,1,0:T(8,128)}) custom-call(f32[4,8,2,128,128]{4,3,2,1,0:T(8,128)} %get-tuple-element.35.s_ref), custom_call_target="tpu_custom_call" | custom-call | tf_op jit(solution)/shard_map/pallas_call | solution.py:582
  158.5 0.0 collective-permute-done.5.far_ref
  158.5 0.0 copy-start.5
  158.5 0.0 collective-permute-done.4.high_ref
  158.6 0.0 copy-start.6
  158.6 0.0 collective-permute-done.3.low_ref
  158.6 0.8 copy-done.5
  159.3 0.2 copy-done.6
  159.6 22.5 %shard_map.41 = (f32[2,512,128]{2,1,0:T(8,128)}, f32[512,1024]{1,0:T(8,128)}) custom-call(s32[1]{0:T(128)} %bitcast.16.col_ref, f32[1024,1024]{1,0:T(8,128)} %get-tuple-element.36.l_ref, f32[8,128,128]{2,1,0:T(8,128)} %get-tuple-element.37.li_ref, f32[2,512,128]{2,1,0:T(8,128)} %get-tuple-element.38.own_ref, f32[2,512,128]{2,1,0:T(8,128)} %collective-permute-done.3.low_ref, ...), custom_call_target="tpu_custom_call" | custom-call | tf_op jit(solution)/shard_map/pallas_call | solution.py:589
  182.1 0.0 all-gather.3.cloned.1.call-done
  182.1 22.0 %shard_map.42.r_ref = f32[4,4096,128]{2,1,0:T(8,128)} custom-call(s32[3]{0:T(128)} %pad_add_fusion.1.at_ref, f32[8,4,2,512,128]{4,3,2,1,0:T(8,128)} %bitcast.41, f32[512,1024]{1,0:T(8,128)} %get-tuple-element.39.x_ref, f32[2,512,128]{2,1,0:T(8,128)} %get-tuple-element.40.y_ref, f32[4,128]{1,0:T(4,128)} %broadcast_select_fusion.2.diag_ref), custom_call_target="tpu_custom_call" | custom-call | tf_op jit(solution)/shard_map/pallas_call | solution.py:600
  204.1 31.2 %collective-permute-done.2.got_ref = f32[3,128,32,128]{3,2,1,0:T(8,128)} collective-permute-done((f32[3,128,32,128]{3,2,1,0:T(8,128)}, f32[3,128,32,128]{3,2,1,0:T(8,128)}, u32[]{:S(2)}, u32[]{:S(2)}) %collective-permute-start.2) | collective-permute-done | bytes 6291488 | tf_op jit(solution)/shard_map/ppermute | solution.py:539
  235.3 14.9 %shard_map.43.kept_ref = f32[1,4,128,32,128]{4,3,2,1,0:T(8,128)} custom-call(s32[2,512]{1,0:T(2,128)} %bitcast.48, f32[3,128,32,128]{3,2,1,0:T(8,128)} %collective-permute-done.2.got_ref, s32[2,32,128]{2,1,0:T(8,128)} %broadcast_select_fusion.cinv_ref, f32[1,4,128,32,128]{4,3,2,1,0:T(8,128)} %get-tuple-element.27.kept_ref, ...), custom_call_target="tpu_custom_call", output_to_operand_aliasing={{}: (3, {})} | custom-call | tf_op jit(solution)/shard_map/pallas_call | solution.py:623
  250.3 29.9 %collective-permute-done.1.got_ref = f32[1,128,32,128]{3,2,1,0:T(8,128)S(1)} collective-permute-done((f32[1,128,32,128]{3,2,1,0:T(8,128)}, f32[1,128,32,128]{3,2,1,0:T(8,128)S(1)}, u32[]{:S(2)}, u32[]{:S(2)}) %collective-permute-start.1) | collective-permute-done | bytes 2097184 | tf_op jit(solution)/shard_map/ppermute | solution.py:539
  280.2 0.0 copy-start.3
  280.2 1.3 copy-done.3
  281.5 0.0 copy-start.1
  281.5 7.1 %shard_map.44 = f32[1,4,128,32,128]{4,3,2,1,0:T(8,128)} custom-call(s32[2,512]{1,0:T(2,128)} %bitcast.49, f32[1,128,32,128]{3,2,1,0:T(8,128)} %copy-done.3, s32[2,32,128]{2,1,0:T(8,128)} %broadcast_select_fusion.cinv_ref, f32[1,4,128,32,128]{4,3,2,1,0:T(8,128)} %shard_map.43.kept_ref, f32[4,4096,128]{2,1,0:T(8,128)} %shard_map.42.r_ref), custom_call_target="tpu_custom_call", output_to_operand_aliasing={{}: (3, {})} | custom-call | tf_op jit(solution)/shard_map/pallas_call | solution.py:623
  288.6 0.0 copy-done.1
  (12 shorter events, 0.1 us)
Async XLA Ops:
  6.5 6.6 %copy-start = (f32[16384]{0:T(1024)S(1)}, f32[16384]{0:T(1024)}, u32[]{:S(2)}) copy-start(f32[16384]{0:T(1024)} %param.5) | copy-start | bytes 196612
  6.5 4.8 %copy-start.7 = (s32[2,16384]{1,0:T(2,128)S(1)}, s32[2,16384]{1,0:T(2,128)}, u32[]{:S(2)}) copy-start(s32[2,16384]{1,0:T(2,128)} %param.4) | copy-start | bytes 393220
  6.5 175.6 %all-gather.3.cloned.1.call-start = ((), (), s32[]{:S(2)}) async-start(), calls=%async_computation | async-start | bytes 18874368 | tf_op jit(solution)/shard_map/all_gather | solution.py:576
  9.2 23.6 %copy-start.2 = (f32[2,2,4,128,128]{4,3,2,1,0:T(8,128)}, f32[2,2,4,128,128]{4,3,2,1,0:T(8,128)S(1)}, u32[]{:S(2)}) copy-start(f32[2,2,4,128,128]{4,3,2,1,0:T(8,128)S(1)} %copy.22) | copy-start | bytes 3145732
  9.2 25.6 %collective-permute-start = (f32[2,2,512,128]{3,2,1,0:T(8,128)S(1)}, f32[2,2,512,128]{3,2,1,0:T(8,128)S(1)}, u32[]{:S(2)}, u32[]{:S(2)}) collective-permute-start(f32[2,2,512,128]{3,2,1,0:T(8,128)S(1)} %bitcast.42), channel_id=1, source_target_pairs={{0,64},{4,68},{8,72},{12,76},{16,80},{20,84},{24,88},{28,92},{32,9... | collective-permute-start | bytes 3145736 | tf_op jit(solution)/shard_map/ppermute | solution.py:464
  13.3 19.5 %copy-start.8 = (s32[2,2,4,128]{3,2,1,0:T(4,128)}, s32[2,2,4,128]{3,2,1,0:T(4,128)S(1)}, u32[]{:S(2)}) copy-start(s32[2,2,4,128]{3,2,1,0:T(4,128)S(1)} %fusion.rmap_ref) | copy-start | bytes 24580
  34.8 1.0 copy-start.4
  98.0 137.4 %collective-permute-start.2 = (f32[3,128,32,128]{3,2,1,0:T(8,128)}, f32[3,128,32,128]{3,2,1,0:T(8,128)}, u32[]{:S(2)}, u32[]{:S(2)}) collective-permute-start(f32[3,128,32,128]{3,2,1,0:T(8,128)} %get-tuple-element.26), channel_id=1, source_target_pairs={{0,64},{4,68},{8,72},{12,76},{16,80},{20,84},{24,88},{28,92},{32,9... | collective-permute-start | bytes 18874376 | tf_op jit(solution)/shard_map/ppermute | solution.py:539
  98.1 182.1 %collective-permute-start.1 = (f32[1,128,32,128]{3,2,1,0:T(8,128)}, f32[1,128,32,128]{3,2,1,0:T(8,128)S(1)}, u32[]{:S(2)}, u32[]{:S(2)}) collective-permute-start(f32[1,128,32,128]{3,2,1,0:T(8,128)} %get-tuple-element.25), channel_id=1, source_target_pairs={{0,64},{4,68},{8,72},{12,76},{16,80},{20,84},{24,88},{28,92},{32,9... | collective-permute-start | bytes 6291464 | tf_op jit(solution)/shard_map/ppermute | solution.py:539
  99.5 59.0 %collective-permute-start.5 = (f32[2,512,128]{2,1,0:T(8,128)}, f32[2,512,128]{2,1,0:T(8,128)S(1)}, u32[]{:S(2)}, u32[]{:S(2)}) collective-permute-start(f32[2,512,128]{2,1,0:T(8,128)} %get-tuple-element.38.own_ref), channel_id=1, source_target_pairs={{0,2},{1,3},{2,0},{3,1},{4,6},{5,7},{6,4},{7,5},{8,10},{9,11},{10,... | collective-permute-start | bytes 1572872 | tf_op jit(solution)/shard_map/ppermute | solution.py:580
  100.1 58.4 %collective-permute-start.4 = (f32[2,512,128]{2,1,0:T(8,128)}, f32[2,512,128]{2,1,0:T(8,128)S(1)}, u32[]{:S(2)}, u32[]{:S(2)}) collective-permute-start(f32[2,512,128]{2,1,0:T(8,128)} %get-tuple-element.38.own_ref), channel_id=1, source_target_pairs={{0,3},{1,0},{2,1},{3,2},{4,7},{5,4},{6,5},{7,6},{8,11},{9,8},{10,9... | collective-permute-start | bytes 1572872 | tf_op jit(solution)/shard_map/ppermute | solution.py:580
  100.1 58.4 %collective-permute-start.3 = (f32[2,512,128]{2,1,0:T(8,128)}, f32[2,512,128]{2,1,0:T(8,128)}, u32[]{:S(2)}, u32[]{:S(2)}) collective-permute-start(f32[2,512,128]{2,1,0:T(8,128)} %get-tuple-element.38.own_ref), channel_id=1, source_target_pairs={{0,1},{1,2},{2,3},{3,0},{4,5},{5,6},{6,7},{7,4},{8,9},{9,10},{10,1... | collective-permute-start | bytes 1572872 | tf_op jit(solution)/shard_map/ppermute | solution.py:580
  158.5 0.8 copy-start.5
  158.6 1.0 copy-start.6
  280.2 1.3 copy-start.3
  281.5 7.1 %copy-start.1 = (f32[16384]{0:T(1024)S(1)}, f32[16384]{0:T(1024)}, u32[]{:S(2)}) copy-start(f32[16384]{0:T(1024)} %param.5) | copy-start | bytes 196612
Sparse Core Ops, SparseCore 0:
  98.1 80.9 all-gather.2

commit v7 on v6

--- a/solution.py
+++ b/solution.py
@@ -57,7 +57,8 @@
 
 
 def pivot_kernel(
-    piece_ref, even_ref, odd_ref, out_ref, turned_ref, send, recv, local, send_turned, recv_turned
+    piece_ref, even_ref, odd_ref, out_ref, turned_ref, send, recv, local, send_turned, recv_turned,
+    relay_ref, send_relay, recv_relay,
 ):
     cube, row, col = lax.axis_index("cube"), lax.axis_index("row"), lax.axis_index("col")
     z = lax.rem(cube, 4)
@@ -83,11 +84,25 @@
     sender = lambda y: at(
         lax.rem(side + crossed, 2) * 4 + z, col, y
     )
-    for y in range(4):
-
-        @pl.when(jnp.logical_not(jnp.logical_and(alone, col == y)))
+    twice = lax.rem(col + 4 - row, 4) == 2
+    served = lax.rem(col + 1 + 2 * lax.rem(col + 1, 2), 4)
+    served_crossed = lax.rem(half + served // 2, 2)
+    served_slot = lax.rem(2 * served_crossed + core + 8 - served - 2, 4)
+    for d in (0, 1, 3):
+        y = lax.rem(col + d, 4)
+
+        @pl.when(jnp.logical_not(jnp.logical_and(alone, d == 0)))
         def _():
             pl.semaphore_signal(barrier, inc=1, device_id=sender(y), device_id_type=MESH)
+
+    pl.semaphore_signal(
+        barrier,
+        inc=1,
+        device_id=at(
+            lax.rem(side + served_crossed, 2) * 4 + z, served, lax.rem(served + 2, 4)
+        ),
+        device_id_type=MESH,
+    )
 
     @pl.when(alone)
     def _():
@@ -106,6 +121,26 @@
             device_id=to_kind(lax.rem(m + col, 4)),
             device_id_type=MESH,
         )
+
+    def to_relay(m):
+        target = to_kind(lax.rem(m + col, 4))
+        return pltpu.make_async_remote_copy(
+            src_ref=(odd_ref if m % 2 else even_ref),
+            dst_ref=relay_ref,
+            send_sem=send_turned.at[m],
+            recv_sem=recv_relay,
+            device_id=at(target["cube"], target["row"], lax.rem(row + 3 - 2 * lax.rem(row, 2), 4)),
+            device_id_type=MESH,
+        )
+
+    onward = pltpu.make_async_remote_copy(
+        src_ref=relay_ref,
+        dst_ref=turned_ref.at[served_slot],
+        send_sem=send_relay,
+        recv_sem=recv_turned.at[served_slot],
+        device_id=at(cube, row, served),
+        device_id_type=MESH,
+    )
 
     def stays(m):
         return jnp.logical_and(alone, lax.rem(m + col, 4) == core)
@@ -164,7 +199,11 @@
         def _():
             keep_quarter(m).start()
 
-        @pl.when(jnp.logical_not(stays(m)))
+        @pl.when(twice)
+        def _():
+            to_relay(m).start()
+
+        @pl.when(jnp.logical_not(jnp.logical_or(stays(m), twice)))
         def _():
             quarter(m).start()
 
@@ -186,6 +225,8 @@
             def _():
                 copy(up, p, 21 + n, sides[1], zz + 1).start()
 
+    to_relay(0).wait_recv()
+    onward.start()
     far = lax.rem(col + 2, 4)
     for i, who in enumerate((row, opposite)):
         for zz in range(2):
@@ -216,6 +257,8 @@
         @pl.when(jnp.logical_not(stays(m)))
         def _():
             quarter(m).wait()
+
+    onward.wait_send()
 
 
 def leaf(d_ref, li_ref):
@@ -358,8 +401,8 @@
     return high, (x - high.astype(F32)).astype(jnp.bfloat16)
 
 
-def place_rows(tile, t, rinv_ref, cinv_ref, from_ref, less, out_ref):
-    groups = range(0, from_ref.shape[-2], 8)
+def place_rows(tile, t, rinv_ref, cinv_ref, load, less, out_ref):
+    groups = range(0, out_ref.shape[-2], 8)
     index = [jnp.maximum(cinv_ref[t, g : g + 8], 0) for g in groups]
     live = [(cinv_ref[t, g : g + 8] >= 0).astype(F32) for g in groups]
     base = tile * TB
@@ -369,7 +412,7 @@
         weight = jnp.where(s >= 0, 1.0, 0.0)
         s = jnp.maximum(s, 0)
         for g, at, keep in zip(groups, index, live):
-            x = jnp.take_along_axis(from_ref[s, g : g + 8], at, axis=1) * (keep * weight)
+            x = jnp.take_along_axis(load(s, g), at, axis=1) * (keep * weight)
             out_ref[o, g : g + 8] = x if less is None else x + less(o, g)
         return 0
 
@@ -377,27 +420,47 @@
 
 
 def keep_kernel(
-    at_ref, rinv_ref, kept_ref, sent_ref, cinv_ref, out_ref, early_ref, late_ref
+    at_ref, rinv_ref, kept_ref, sent_ref, cinv_ref, out_ref, early_ref, late_ref, thin_ref
 ):
     step, steps = pl.program_id(0), pl.num_programs(0)
 
     @pl.when(step < steps - 1)
     def _():
-        early_ref[0] = sent_ref[0, 0, 0]
+        early_ref[0] = sent_ref[0, 0, 0, :, 8:, :]
 
     @pl.when(step == steps - 1)
     def _():
-        late_ref[0] = sent_ref[0, 0, 0]
-
-    place_rows(step, 0, rinv_ref, cinv_ref, kept_ref.at[0, 0, 0], None, out_ref.at[0, 0])
-
-
-def finish_kernel(start, rinv_ref, got_ref, cinv_ref, kept_ref, r_ref, out_ref):
+        late_ref[0] = sent_ref[0, 0, 0, :, 8:, :]
+
+    for v in range(2, 8):
+        thin_ref[v - 2] = sent_ref[0, 0, 0, :, v, :]
+
+    def load(s, g):
+        return kept_ref[0, 0, 0, s, g : g + 8]
+
+    place_rows(step, 0, rinv_ref, cinv_ref, load, None, out_ref.at[0, 0])
+
+
+def finish_kernel(
+    start, rinv_ref, got_ref, thin_ref, cinv_ref, kept_ref, r_ref, out_ref, first_ref
+):
+    @pl.when(pl.program_id(0) == 0)
+    def _():
+        first_ref[: 2 * TB, :] = jnp.zeros((2 * TB, TB), F32)
+
+    for v in range(2, 8):
+        first_ref[v * TB : (v + 1) * TB, :] = thin_ref[v - 2]
+
+    def load(s, g):
+        if g == 0:
+            return first_ref[pl.ds(s, 8, stride=TB), :]
+        return got_ref[0, s, g - 8 : g]
+
     def less(o, g):
         return kept_ref[0, 0, o, g : g + 8] - r_ref.at[0][pl.ds(g * TB + o, 8, stride=TB), :]
 
     tile = pl.program_id(0) + start
-    place_rows(tile, 1, rinv_ref, cinv_ref, got_ref.at[0], less, out_ref.at[0, 0])
+    place_rows(tile, 1, rinv_ref, cinv_ref, load, less, out_ref.at[0, 0])
 
 
 def update_kernel(
@@ -509,12 +572,13 @@
     at = jnp.stack([sibling, cube, 2 * crossed]).astype(jnp.int32)
     whole = jax.ShapeDtypeStruct((1, tiles, TB, cols, TB), F32)
     all_maps = pl.BlockSpec((2, cols, TB), lambda i, *_: (0, 0, 0))
-    result, first, second = pl.pallas_call(
+    result, first, second, thin = pl.pallas_call(
         keep_kernel,
         out_shape=[
             whole,
-            jax.ShapeDtypeStruct((early, TB, cols, TB), F32),
-            jax.ShapeDtypeStruct((tiles - early, TB, cols, TB), F32),
+            jax.ShapeDtypeStruct((early, TB, cols - 8, TB), F32),
+            jax.ShapeDtypeStruct((tiles - early, TB, cols - 8, TB), F32),
+            jax.ShapeDtypeStruct((6, rows, TB), F32),
         ],
         grid_spec=pltpu.PrefetchScalarGridSpec(
             num_scalar_prefetch=2,
@@ -528,14 +592,17 @@
             ],
             out_specs=[
                 pl.BlockSpec((1, 1, TB, cols, TB), lambda i, *_: (0, i, 0, 0, 0)),
-                pl.BlockSpec((1, TB, cols, TB), lambda i, *_: (jnp.minimum(i, early - 1), 0, 0, 0)),
-                pl.BlockSpec((1, TB, cols, TB), lambda i, *_: (0, 0, 0, 0)),
+                pl.BlockSpec(
+                    (1, TB, cols - 8, TB), lambda i, *_: (jnp.minimum(i, early - 1), 0, 0, 0)
+                ),
+                pl.BlockSpec((1, TB, cols - 8, TB), lambda i, *_: (0, 0, 0, 0)),
+                pl.BlockSpec((6, TB, TB), lambda i, *_: (0, i, 0)),
             ],
         ),
     )(at, row_inverse, child_update, child_update, col_inverse)
-    first, second, got = lax.optimization_barrier((first, second, got))
+    first, second, thin, got = lax.optimization_barrier((first, second, thin, got))
     arrived = []
-    for part in (first, second):
+    for part in (thin, first, second):
         arrived.append(lax.ppermute(part, ("cube", "row"), trade))
 
     strip = jax.ShapeDtypeStruct((2, rows, TB), F32)
@@ -564,6 +631,9 @@
             pltpu.SemaphoreType.DMA,
             pltpu.SemaphoreType.DMA((4,)),
             pltpu.SemaphoreType.DMA((4,)),
+            pltpu.VMEM((2, rows, TB), F32),
+            pltpu.SemaphoreType.DMA,
+            pltpu.SemaphoreType.DMA,
         ],
         compiler_params=pltpu.CompilerParams(collective_id=0, has_side_effects=True),
     )(piece, even, odd)
@@ -618,6 +688,7 @@
             ],
         ),
     )(at, others, x, y, trailing_diag)
+    thin, *arrived = arrived
     for start, part in zip((0, early), arrived):
         block_at = lambda i, *_, start=start: (0, i + start, 0, 0, 0)
         result = pl.pallas_call(
@@ -627,15 +698,17 @@
                 num_scalar_prefetch=1,
                 grid=(part.shape[0],),
                 in_specs=[
-                    pl.BlockSpec((1, TB, cols, TB), lambda i, *_: (i, 0, 0, 0)),
+                    pl.BlockSpec((1, TB, cols - 8, TB), lambda i, *_: (i, 0, 0, 0)),
+                    pl.BlockSpec((6, TB, TB), lambda i, *_, start=start: (0, i + start, 0)),
                     all_maps,
                     pl.BlockSpec((1, 1, TB, cols, TB), block_at),
                     pl.BlockSpec((1, cols * TB, TB), lambda i, *_, start=start: (i + start, 0, 0)),
                 ],
                 out_specs=pl.BlockSpec((1, 1, TB, cols, TB), block_at),
+                scratch_shapes=[pltpu.VMEM((8 * TB, TB), F32)],
             ),
-            input_output_aliases={3: 0},
-        )(row_inverse, part, col_inverse, result, update)
+            input_output_aliases={4: 0},
+        )(row_inverse, part, thin, col_inverse, result, update)
     return result
 
 

time: 296 us -> 282 us (0.953)
  waiting for transfers between devices: 61.2 us -> 43.7 us
  starting transfers between devices: 5.75 us -> 11 us
    ppermute x2 -> x3, waiting for transfers between devices: 61.1 us -> 33.9 us  [on_device(): arrived.append(lax.ppermute(part, ('cube', 'row'), trade))]
    ppermute x3, waiting for transfers between devices: 0.01 us -> 9.75 us  [on_device(): lax.ppermute(own, 'col', [(c, (c + hop) % 4) for c in range(4)])]
    ppermute x3, starting transfers between devices: 2.1 us -> 7.3 us  [on_device(): lax.ppermute(own, 'col', [(c, (c + hop) % 4) for c in range(4)])]
  transfers between devices with their start and end apart: 7 -> 8, of which waited for: 2 -> 3; matrix products, arithmetic and copies ran while one was open for 2% -> 2% of each run, Pallas kernels for 45% -> 47%
where the time goes in v7:
time: 282 us; the launch traced here: 281 us
  Pallas kernels  200 us (71%)
  waiting for transfers between devices  43.7 us (15%)
  between operations  13.6 us (5%)
  starting transfers between devices  11 us (4%)
  local copies, waits for them, and re-layouts  6.91 us (2%)
  other arithmetic  5.63 us (2%)
    pallas_call x1, Pallas kernels, on_device(): pl.pallas_call(factor_kernel, out_shape=[jax.ShapeDtypeStruct((K, K), F32...  55.8 us
    pallas_call x1, Pallas kernels, on_device(): pl.pallas_call(pivot_kernel, out_shape=[jax.ShapeDtypeStruct((4, 8, 2, TB...  55.1 us
    ppermute x3, waiting for transfers between devices, on_device(): arrived.append(lax.ppermute(part, ('cube', 'row'), trade))  33.9 us
    pallas_call x1, Pallas kernels, on_device(): pl.pallas_call(solve_kernel, out_shape=[jax.ShapeDtypeStruct((2, rows, TB...  22.6 us
    pallas_call x1, Pallas kernels, on_device(): pl.pallas_call(update_kernel, out_shape=jax.ShapeDtypeStruct((tiles, cols...  22 us
    pallas_call x2, Pallas kernels, on_device(): pl.pallas_call(functools.partial(finish_kernel, start), out_shape=whole,...  20.5 us
    pallas_call x1, Pallas kernels, on_device(): pl.pallas_call(keep_kernel, out_shape=[whole, jax.ShapeDtypeStruct((early...  17.1 us
    ppermute x3, waiting for transfers between devices, on_device(): lax.ppermute(own, 'col', [(c, (c + hop) % 4) for c in range(4)])  9.75 us
  transfers between devices with their start and end apart: 8, of which 3 were waited for; matrix products, arithmetic and copies ran while one was open for 2% of the time, Pallas kernels for 47%

profile of v7, /device:TPU:1, one launch (start us, length us, event | category | flops | bytes accessed | tf_op | source)
XLA Modules:
  0.0 281.2 jit_solution(10771588145984388441)
XLA Ops:
  6.5 0.0 copy-start
  6.5 0.0 copy-start.6
  6.5 0.0 all-gather.3.cloned.1.call-start
  6.5 2.5 slice_bitcast_fusion
  9.1 0.1 copy.22
  9.2 0.0 copy-start.3
  9.2 2.1 collective-permute-start
  11.4 0.0 copy-done.6
  11.4 0.1 constant_dynamic-slice_fusion.5
  11.5 0.1 pad_add_fusion
  11.7 0.1 reshape.114
  11.9 0.1 subtract_bitcast_fusion
  11.9 1.2 select_reduce_fusion
  13.1 0.0 copy-done
  13.2 0.1 broadcast_multiply_fusion
  13.2 0.1 fusion.rmap_ref
  13.3 0.0 copy-start.7
  13.3 0.2 select_reduce_fusion.1
  13.5 0.6 pad_add_fusion.1.at_ref
  14.1 0.6 copy.32
  14.7 0.7 broadcast_select_fusion.cinv_ref
  15.4 17.1 %shard_map.37 = (f32[1,4,128,32,128]{4,3,2,1,0:T(8,128)}, f32[3,128,24,128]{3,2,1,0:T(8,128)}, f32[1,128,24,128]{3,2,1,0:T(8,128)}, f32[6,512,128]{2,1,0:T(8,128)}) custom-call(s32[3]{0:T(128)} %pad_add_fusion.1.at_ref, s32[2,512]{1,0:T(2,128)} %bitcast.47, f32[1,2,4,128,32,128]{5,4,3,2,1,0:T(8,128)} %sent_ref.1, f32[1,2,4,128,32,128]{5,4,3,2,1,0:T(8,128)} %sent_ref.1, ...), custom_call_target="tpu_custom_call" | custom-call | tf_op jit(solution)/shard_map/pallas_call | solution.py:575
  32.5 0.0 copy-done.3
  32.5 0.0 copy-done.7
  32.5 0.6 pad_add_fusion.2.pick_ref
  33.1 0.1 broadcast_compare_fusion
  33.2 0.6 slice_subtract_fusion.cmap_ref
  33.8 0.7 broadcast_select_fusion.1.diag_ref
  34.5 0.0 collective-permute-done.got_ref
  34.5 0.0 copy-start.5
  34.5 1.0 copy-done.5
  35.5 7.1 %shard_map.38 = (f32[2,512,128]{2,1,0:T(8,128)}, f32[2,512,128]{2,1,0:T(8,128)}, f32[2,512,128]{2,1,0:T(8,128)}, f32[2,128,128]{2,1,0:T(8,128)}) custom-call(s32[2]{0:T(128)} %pad_add_fusion.2.pick_ref, f32[2,2,512,128]{3,2,1,0:T(8,128)} %bitcast.43, f32[2,2,512,128]{3,2,1,0:T(8,128)} %copy-done.5, s32[2,2,4,128]{3,2,1,0:T(4,128)} %copy-done.7, ...), custom_call_target="tpu_custom_call" | custom-call | tf_op jit(solution)/shard_map/pallas_call | solution.py:609
  42.6 55.1 %shard_map.39 = (f32[4,8,2,128,128]{4,3,2,1,0:T(8,128)}, f32[4,2,512,128]{3,2,1,0:T(8,128)}) custom-call(f32[2,128,128]{2,1,0:T(8,128)} %get-tuple-element.33.piece_ref, f32[2,512,128]{2,1,0:T(8,128)} %get-tuple-element.34.even_ref, f32[2,512,128]{2,1,0:T(8,128)} %get-tuple-element.35.odd_ref), custom_call_target="tpu_custom_call" | custom-call | tf_op jit(solution)/shard_map/pallas_call | solution.py:620
  97.8 0.0 all-gather.3.cloned.1.call-update
  97.8 0.1 collective-permute-start.3
  97.9 1.5 collective-permute-start.2
  99.3 0.1 collective-permute-start.1
  99.4 1.2 collective-permute-start.6
  100.6 2.5 collective-permute-start.5
  103.1 9.7 %collective-permute-done.6.far_ref = f32[2,512,128]{2,1,0:T(8,128)} collective-permute-done((f32[2,512,128]{2,1,0:T(8,128)}, f32[2,512,128]{2,1,0:T(8,128)}, u32[]{:S(2)}, u32[]{:S(2)}) %collective-permute-start.6) | collective-permute-done | bytes 524320 | tf_op jit(solution)/shard_map/ppermute | solution.py:650
  112.8 3.6 %collective-permute-start.4 = (f32[2,512,128]{2,1,0:T(8,128)}, f32[2,512,128]{2,1,0:T(8,128)}, u32[]{:S(2)}, u32[]{:S(2)}) collective-permute-start(f32[2,512,128]{2,1,0:T(8,128)} %get-tuple-element.42.own_ref), channel_id=1, source_target_pairs={{0,1},{1,2},{2,3},{3,0},{4,5},{5,6},{6,7},{7,4},{8,9},{9,10},{10,1... | collective-permute-start | bytes 1572872 | tf_op jit(solution)/shard_map/ppermute | solution.py:650
  116.5 0.7 broadcast_select_fusion.2.diag_ref
  117.1 55.8 %shard_map.40 = (f32[1024,1024]{1,0:T(8,128)}, f32[8,128,128]{2,1,0:T(8,128)}) custom-call(f32[4,8,2,128,128]{4,3,2,1,0:T(8,128)} %get-tuple-element.39.s_ref), custom_call_target="tpu_custom_call" | custom-call | tf_op jit(solution)/shard_map/pallas_call | solution.py:652
  173.0 0.0 collective-permute-done.5.high_ref
  173.0 0.0 collective-permute-done.4.low_ref
  173.0 22.6 %shard_map.41 = (f32[2,512,128]{2,1,0:T(8,128)}, f32[512,1024]{1,0:T(8,128)}) custom-call(s32[1]{0:T(128)} %bitcast.16.col_ref, f32[1024,1024]{1,0:T(8,128)} %get-tuple-element.40.l_ref, f32[8,128,128]{2,1,0:T(8,128)} %get-tuple-element.41.li_ref, f32[2,512,128]{2,1,0:T(8,128)} %get-tuple-element.42.own_ref, f32[2,512,128]{2,1,0:T(8,128)} %collective-permute-done.4.low_ref, ...), custom_call_target="tpu_custom_call" | custom-call | tf_op jit(solution)/shard_map/pallas_call | solution.py:659
  195.6 0.0 all-gather.3.cloned.1.call-done
  195.6 22.0 %shard_map.42.r_ref = f32[4,4096,128]{2,1,0:T(8,128)} custom-call(s32[3]{0:T(128)} %pad_add_fusion.1.at_ref, f32[8,4,2,512,128]{4,3,2,1,0:T(8,128)} %bitcast.41, f32[512,1024]{1,0:T(8,128)} %get-tuple-element.43.x_ref, f32[2,512,128]{2,1,0:T(8,128)} %get-tuple-element.44.y_ref, f32[4,128]{1,0:T(4,128)} %broadcast_select_fusion.2.diag_ref), custom_call_target="tpu_custom_call" | custom-call | tf_op jit(solution)/shard_map/pallas_call | solution.py:670
  217.6 18.0 %collective-permute-done.2.thin_ref = f32[6,512,128]{2,1,0:T(8,128)S(1)} collective-permute-done((f32[6,512,128]{2,1,0:T(8,128)}, f32[6,512,128]{2,1,0:T(8,128)S(1)}, u32[]{:S(2)}, u32[]{:S(2)}) %collective-permute-start.2) | collective-permute-done | bytes 1572896 | tf_op jit(solution)/shard_map/ppermute | solution.py:606
  235.6 0.0 copy-start.2
  235.6 0.0 collective-permute-done.3.got_ref
  235.6 1.1 copy-done.2
  236.7 13.4 %shard_map.43.kept_ref = f32[1,4,128,32,128]{4,3,2,1,0:T(8,128)} custom-call(s32[2,512]{1,0:T(2,128)} %bitcast.48, f32[3,128,24,128]{3,2,1,0:T(8,128)} %collective-permute-done.3.got_ref, f32[6,512,128]{2,1,0:T(8,128)} %copy-done.2, s32[2,32,128]{2,1,0:T(8,128)} %broadcast_select_fusion.cinv_ref, ...), custom_call_target="tpu_custom_call", output_to_operand_aliasing={{}: (4, {})} | custom-call | tf_op jit(solution)/shard_map/pallas_call | solution.py:694
  250.1 15.9 %collective-permute-done.1.got_ref = f32[1,128,24,128]{3,2,1,0:T(8,128)S(1)} collective-permute-done((f32[1,128,24,128]{3,2,1,0:T(8,128)}, f32[1,128,24,128]{3,2,1,0:T(8,128)S(1)}, u32[]{:S(2)}, u32[]{:S(2)}) %collective-permute-start.1) | collective-permute-done | bytes 1572896 | tf_op jit(solution)/shard_map/ppermute | solution.py:606
  266.0 0.0 copy-start.4
  266.0 1.2 copy-done.4
  267.2 0.0 copy-start.1
  267.2 7.1 %shard_map.44 = f32[1,4,128,32,128]{4,3,2,1,0:T(8,128)} custom-call(s32[2,512]{1,0:T(2,128)} %bitcast.49, f32[1,128,24,128]{3,2,1,0:T(8,128)} %copy-done.4, f32[6,512,128]{2,1,0:T(8,128)} %copy-done.2, s32[2,32,128]{2,1,0:T(8,128)} %broadcast_select_fusion.cinv_ref, f32[1,4,128,32,128]{4,3,2,1,0:T(8,128)} %shard_map.43.kept_ref, ...), custom_call_target="tpu_custom_call", output_to_operand_aliasing={{}: (4, {})} | custom-call | tf_op jit(solution)/shard_map/pallas_call | solution.py:694
  274.3 0.0 copy-done.1
  (12 shorter events, 0.1 us)
Async XLA Ops:
  6.5 6.6 %copy-start = (f32[16384]{0:T(1024)S(1)}, f32[16384]{0:T(1024)}, u32[]{:S(2)}) copy-start(f32[16384]{0:T(1024)} %param.5) | copy-start | bytes 196612
  6.5 4.8 %copy-start.6 = (s32[2,16384]{1,0:T(2,128)S(1)}, s32[2,16384]{1,0:T(2,128)}, u32[]{:S(2)}) copy-start(s32[2,16384]{1,0:T(2,128)} %param.4) | copy-start | bytes 393220
  6.5 189.0 %all-gather.3.cloned.1.call-start = ((), (), s32[]{:S(2)}) async-start(), calls=%async_computation | async-start | bytes 18874368 | tf_op jit(solution)/shard_map/all_gather | solution.py:646
  9.2 23.3 %copy-start.3 = (f32[2,2,4,128,128]{4,3,2,1,0:T(8,128)}, f32[2,2,4,128,128]{4,3,2,1,0:T(8,128)S(1)}, u32[]{:S(2)}) copy-start(f32[2,2,4,128,128]{4,3,2,1,0:T(8,128)S(1)} %copy.22) | copy-start | bytes 3145732
  9.2 25.3 %collective-permute-start = (f32[2,2,512,128]{3,2,1,0:T(8,128)S(1)}, f32[2,2,512,128]{3,2,1,0:T(8,128)S(1)}, u32[]{:S(2)}, u32[]{:S(2)}) collective-permute-start(f32[2,2,512,128]{3,2,1,0:T(8,128)S(1)} %bitcast.42), channel_id=1, source_target_pairs={{0,64},{4,68},{8,72},{12,76},{16,80},{20,84},{24,88},{28,92},{32,9... | collective-permute-start | bytes 3145736 | tf_op jit(solution)/shard_map/ppermute | solution.py:527
  13.3 19.2 %copy-start.7 = (s32[2,2,4,128]{3,2,1,0:T(4,128)}, s32[2,2,4,128]{3,2,1,0:T(4,128)S(1)}, u32[]{:S(2)}) copy-start(s32[2,2,4,128]{3,2,1,0:T(4,128)S(1)} %fusion.rmap_ref) | copy-start | bytes 24580
  34.5 1.0 copy-start.5
  97.8 137.8 %collective-permute-start.3 = (f32[3,128,24,128]{3,2,1,0:T(8,128)}, f32[3,128,24,128]{3,2,1,0:T(8,128)}, u32[]{:S(2)}, u32[]{:S(2)}) collective-permute-start(f32[3,128,24,128]{3,2,1,0:T(8,128)} %get-tuple-element.30), channel_id=1, source_target_pairs={{0,64},{4,68},{8,72},{12,76},{16,80},{20,84},{24,88},{28,92},{32,9... | collective-permute-start | bytes 14155784 | tf_op jit(solution)/shard_map/ppermute | solution.py:606
  97.9 137.7 %collective-permute-start.2 = (f32[6,512,128]{2,1,0:T(8,128)}, f32[6,512,128]{2,1,0:T(8,128)S(1)}, u32[]{:S(2)}, u32[]{:S(2)}) collective-permute-start(f32[6,512,128]{2,1,0:T(8,128)} %get-tuple-element.29), channel_id=1, source_target_pairs={{0,64},{4,68},{8,72},{12,76},{16,80},{20,84},{24,88},{28,92},{32,9... | collective-permute-start | bytes 4718600 | tf_op jit(solution)/shard_map/ppermute | solution.py:606
  99.3 166.7 %collective-permute-start.1 = (f32[1,128,24,128]{3,2,1,0:T(8,128)}, f32[1,128,24,128]{3,2,1,0:T(8,128)S(1)}, u32[]{:S(2)}, u32[]{:S(2)}) collective-permute-start(f32[1,128,24,128]{3,2,1,0:T(8,128)} %get-tuple-element.28), channel_id=1, source_target_pairs={{0,64},{4,68},{8,72},{12,76},{16,80},{20,84},{24,88},{28,92},{32,9... | collective-permute-start | bytes 4718600 | tf_op jit(solution)/shard_map/ppermute | solution.py:606
  99.4 13.4 %collective-permute-start.6 = (f32[2,512,128]{2,1,0:T(8,128)}, f32[2,512,128]{2,1,0:T(8,128)}, u32[]{:S(2)}, u32[]{:S(2)}) collective-permute-start(f32[2,512,128]{2,1,0:T(8,128)} %get-tuple-element.42.own_ref), channel_id=1, source_target_pairs={{0,2},{1,3},{2,0},{3,1},{4,6},{5,7},{6,4},{7,5},{8,10},{9,11},{10,... | collective-permute-start | bytes 1572872 | tf_op jit(solution)/shard_map/ppermute | solution.py:650
  100.6 72.4 %collective-permute-start.5 = (f32[2,512,128]{2,1,0:T(8,128)}, f32[2,512,128]{2,1,0:T(8,128)}, u32[]{:S(2)}, u32[]{:S(2)}) collective-permute-start(f32[2,512,128]{2,1,0:T(8,128)} %get-tuple-element.42.own_ref), channel_id=1, source_target_pairs={{0,3},{1,0},{2,1},{3,2},{4,7},{5,4},{6,5},{7,6},{8,11},{9,8},{10,9... | collective-permute-start | bytes 1572872 | tf_op jit(solution)/shard_map/ppermute | solution.py:650
  112.8 60.1 %collective-permute-start.4 = (f32[2,512,128]{2,1,0:T(8,128)}, f32[2,512,128]{2,1,0:T(8,128)}, u32[]{:S(2)}, u32[]{:S(2)}) collective-permute-start(f32[2,512,128]{2,1,0:T(8,128)} %get-tuple-element.42.own_ref), channel_id=1, source_target_pairs={{0,1},{1,2},{2,3},{3,0},{4,5},{5,6},{6,7},{7,4},{8,9},{9,10},{10,1... | collective-permute-start | bytes 1572872 | tf_op jit(solution)/shard_map/ppermute | solution.py:650
  235.6 1.1 copy-start.2
  266.0 1.2 copy-start.4
  267.2 7.1 %copy-start.1 = (f32[16384]{0:T(1024)S(1)}, f32[16384]{0:T(1024)}, u32[]{:S(2)}) copy-start(f32[16384]{0:T(1024)} %param.5) | copy-start | bytes 196612
Sparse Core Ops, SparseCore 0:
  97.9 83.0 all-gather.2

commit v8 on v6

--- a/solution.py
+++ b/solution.py
@@ -1,5 +1,3 @@
-import functools
-
 import jax
 import jax.numpy as jnp
 from jax import lax
@@ -358,8 +356,8 @@
     return high, (x - high.astype(F32)).astype(jnp.bfloat16)
 
 
-def place_rows(tile, t, rinv_ref, cinv_ref, from_ref, less, out_ref):
-    groups = range(0, from_ref.shape[-2], 8)
+def place_rows(tile, t, rinv_ref, cinv_ref, load, less, out_ref):
+    groups = range(0, out_ref.shape[-2], 8)
     index = [jnp.maximum(cinv_ref[t, g : g + 8], 0) for g in groups]
     live = [(cinv_ref[t, g : g + 8] >= 0).astype(F32) for g in groups]
     base = tile * TB
@@ -369,7 +367,7 @@
         weight = jnp.where(s >= 0, 1.0, 0.0)
         s = jnp.maximum(s, 0)
         for g, at, keep in zip(groups, index, live):
-            x = jnp.take_along_axis(from_ref[s, g : g + 8], at, axis=1) * (keep * weight)
+            x = jnp.take_along_axis(load(s, g), at, axis=1) * (keep * weight)
             out_ref[o, g : g + 8] = x if less is None else x + less(o, g)
         return 0
 
@@ -377,27 +375,37 @@
 
 
 def keep_kernel(
-    at_ref, rinv_ref, kept_ref, sent_ref, cinv_ref, out_ref, early_ref, late_ref
+    at_ref, rinv_ref, kept_ref, sent_ref, cinv_ref, out_ref, main_ref, thin_ref
 ):
-    step, steps = pl.program_id(0), pl.num_programs(0)
-
-    @pl.when(step < steps - 1)
+    main_ref[0] = sent_ref[0, 0, 0, :, 8:, :]
+    for v in range(2, 8):
+        thin_ref[v - 2] = sent_ref[0, 0, 0, :, v, :]
+
+    def load(s, g):
+        return kept_ref[0, 0, 0, s, g : g + 8]
+
+    place_rows(pl.program_id(0), 0, rinv_ref, cinv_ref, load, None, out_ref.at[0, 0])
+
+
+def finish_kernel(
+    rinv_ref, got_ref, thin_ref, cinv_ref, kept_ref, r_ref, out_ref, first_ref
+):
+    @pl.when(pl.program_id(0) == 0)
     def _():
-        early_ref[0] = sent_ref[0, 0, 0]
-
-    @pl.when(step == steps - 1)
-    def _():
-        late_ref[0] = sent_ref[0, 0, 0]
-
-    place_rows(step, 0, rinv_ref, cinv_ref, kept_ref.at[0, 0, 0], None, out_ref.at[0, 0])
-
-
-def finish_kernel(start, rinv_ref, got_ref, cinv_ref, kept_ref, r_ref, out_ref):
+        first_ref[: 2 * TB, :] = jnp.zeros((2 * TB, TB), F32)
+
+    for v in range(2, 8):
+        first_ref[v * TB : (v + 1) * TB, :] = thin_ref[v - 2]
+
+    def load(s, g):
+        if g == 0:
+            return first_ref[pl.ds(s, 8, stride=TB), :]
+        return got_ref[0, s, g - 8 : g]
+
     def less(o, g):
         return kept_ref[0, 0, o, g : g + 8] - r_ref.at[0][pl.ds(g * TB + o, 8, stride=TB), :]
 
-    tile = pl.program_id(0) + start
-    place_rows(tile, 1, rinv_ref, cinv_ref, got_ref.at[0], less, out_ref.at[0, 0])
+    place_rows(pl.program_id(0), 1, rinv_ref, cinv_ref, load, less, out_ref.at[0, 0])
 
 
 def update_kernel(
@@ -462,7 +470,6 @@
 
     raw = jnp.transpose(block[:, :, :, :2, :], (0, 3, 1, 2, 4)).reshape(2, 2, rows, TB)
     got = lax.ppermute(raw, ("cube", "row"), trade)
-    early = tiles - 1
     maps = jnp.stack(
         [
             lax.dynamic_index_in_dim(child_map, sibling, 0, keepdims=False),
@@ -509,12 +516,12 @@
     at = jnp.stack([sibling, cube, 2 * crossed]).astype(jnp.int32)
     whole = jax.ShapeDtypeStruct((1, tiles, TB, cols, TB), F32)
     all_maps = pl.BlockSpec((2, cols, TB), lambda i, *_: (0, 0, 0))
-    result, first, second = pl.pallas_call(
+    result, main, thin = pl.pallas_call(
         keep_kernel,
         out_shape=[
             whole,
-            jax.ShapeDtypeStruct((early, TB, cols, TB), F32),
-            jax.ShapeDtypeStruct((tiles - early, TB, cols, TB), F32),
+            jax.ShapeDtypeStruct((tiles, TB, cols - 8, TB), F32),
+            jax.ShapeDtypeStruct((6, rows, TB), F32),
         ],
         grid_spec=pltpu.PrefetchScalarGridSpec(
             num_scalar_prefetch=2,
@@ -528,14 +535,14 @@
             ],
             out_specs=[
                 pl.BlockSpec((1, 1, TB, cols, TB), lambda i, *_: (0, i, 0, 0, 0)),
-                pl.BlockSpec((1, TB, cols, TB), lambda i, *_: (jnp.minimum(i, early - 1), 0, 0, 0)),
-                pl.BlockSpec((1, TB, cols, TB), lambda i, *_: (0, 0, 0, 0)),
+                pl.BlockSpec((1, TB, cols - 8, TB), lambda i, *_: (i, 0, 0, 0)),
+                pl.BlockSpec((6, TB, TB), lambda i, *_: (0, i, 0)),
             ],
         ),
     )(at, row_inverse, child_update, child_update, col_inverse)
-    first, second, got = lax.optimization_barrier((first, second, got))
+    main, thin, got = lax.optimization_barrier((main, thin, got))
     arrived = []
-    for part in (first, second):
+    for part in (thin, main):
         arrived.append(lax.ppermute(part, ("cube", "row"), trade))
 
     strip = jax.ShapeDtypeStruct((2, rows, TB), F32)
@@ -618,25 +625,24 @@
             ],
         ),
     )(at, others, x, y, trailing_diag)
-    for start, part in zip((0, early), arrived):
-        block_at = lambda i, *_, start=start: (0, i + start, 0, 0, 0)
-        result = pl.pallas_call(
-            functools.partial(finish_kernel, start),
-            out_shape=whole,
-            grid_spec=pltpu.PrefetchScalarGridSpec(
-                num_scalar_prefetch=1,
-                grid=(part.shape[0],),
-                in_specs=[
-                    pl.BlockSpec((1, TB, cols, TB), lambda i, *_: (i, 0, 0, 0)),
-                    all_maps,
-                    pl.BlockSpec((1, 1, TB, cols, TB), block_at),
-                    pl.BlockSpec((1, cols * TB, TB), lambda i, *_, start=start: (i + start, 0, 0)),
-                ],
-                out_specs=pl.BlockSpec((1, 1, TB, cols, TB), block_at),
-            ),
-            input_output_aliases={3: 0},
-        )(row_inverse, part, col_inverse, result, update)
-    return result
+    own_block = pl.BlockSpec((1, 1, TB, cols, TB), lambda i, *_: (0, i, 0, 0, 0))
+    return pl.pallas_call(
+        finish_kernel,
+        out_shape=whole,
+        grid_spec=pltpu.PrefetchScalarGridSpec(
+            num_scalar_prefetch=1,
+            grid=(tiles,),
+            in_specs=[
+                pl.BlockSpec((1, TB, cols - 8, TB), lambda i, *_: (i, 0, 0, 0)),
+                pl.BlockSpec((6, TB, TB), lambda i, *_: (0, i, 0)),
+                all_maps,
+                own_block,
+                pl.BlockSpec((1, cols * TB, TB), lambda i, *_: (i, 0, 0)),
+            ],
+            out_specs=own_block,
+            scratch_shapes=[pltpu.VMEM((8 * TB, TB), F32)],
+        ),
+    )(row_inverse, arrived[1], arrived[0], col_inverse, result, update)
 
 
 def solution(mesh):

time: 296 us -> 293 us (0.990)
  Pallas kernels: 202 us -> 196 us
  waiting for transfers between devices: 61.2 us -> 64.8 us
    pallas_call x3 -> x2, Pallas kernels: 39.4 us -> 32.3 us  [the longest x1 16.6 us: on_device(): pl.pallas_call(keep_kernel, out_shape=[whole, jax.ShapeDtypeStruct((tiles...]
    ppermute x2, waiting for transfers between devices: 61.1 us -> 64.8 us  [on_device(): arrived.append(lax.ppermute(part, ('cube', 'row'), trade))]
  transfers between devices with their start and end apart: 7 -> 7, of which waited for: 2 -> 1; matrix products, arithmetic and copies ran while one was open for 2% -> 2% of each run, Pallas kernels for 45% -> 40%
where the time goes in v8:
time: 293 us
  Pallas kernels  196 us (67%)
  waiting for transfers between devices  64.8 us (22%)
  between operations  13.6 us (5%)
  local copies, waits for them, and re-layouts  6.91 us (2%)
  starting transfers between devices  5.7 us (2%)
  other arithmetic  5.56 us (2%)
    ppermute x2, waiting for transfers between devices, on_device(): arrived.append(lax.ppermute(part, ('cube', 'row'), trade))  64.8 us
    pallas_call x1, Pallas kernels, on_device(): pl.pallas_call(factor_kernel, out_shape=[jax.ShapeDtypeStruct((K, K), F32...  56.2 us
    pallas_call x1, Pallas kernels, on_device(): pl.pallas_call(pivot_kernel, out_shape=[jax.ShapeDtypeStruct((4, 8, 2, TB...  55.8 us
    pallas_call x1, Pallas kernels, on_device(): pl.pallas_call(solve_kernel, out_shape=[jax.ShapeDtypeStruct((2, rows, TB...  22.6 us
    pallas_call x1, Pallas kernels, on_device(): pl.pallas_call(update_kernel, out_shape=jax.ShapeDtypeStruct((tiles, cols...  22 us
    pallas_call x1, Pallas kernels, on_device(): pl.pallas_call(keep_kernel, out_shape=[whole, jax.ShapeDtypeStruct((tiles...  16.6 us
    pallas_call x1, Pallas kernels, on_device(): pl.pallas_call(finish_kernel, out_shape=whole, grid_spec=pltpu.PrefetchSc...  15.6 us
    pallas_call x1, Pallas kernels, on_device(): pl.pallas_call(place_kernel, out_shape=[strip, strip, strip, jax.ShapeDty...  7.05 us
  transfers between devices with their start and end apart: 7, of which 1 were waited for; matrix products, arithmetic and copies ran while one was open for 2% of the time, Pallas kernels for 40%

profile of v8, /device:TPU:1, one launch (start us, length us, event | category | flops | bytes accessed | tf_op | source)
XLA Modules:
  0.0 292.6 jit_solution(1303533125319378456)
XLA Ops:
  6.5 0.0 copy-start
  6.5 0.0 copy-start.8
  6.5 0.0 all-gather.3.cloned.1.call-start
  6.5 2.5 slice_bitcast_fusion
  9.1 0.1 copy.20
  9.2 0.0 copy-start.2
  9.2 2.1 collective-permute-start
  11.4 0.0 copy-done.8
  11.4 0.1 constant_dynamic-slice_fusion.5
  11.5 0.1 pad_add_fusion
  11.7 0.1 reshape.114
  11.8 0.1 subtract_bitcast_fusion
  11.9 1.2 select_reduce_fusion
  13.1 0.0 copy-done
  13.2 0.1 broadcast_multiply_fusion
  13.2 0.1 fusion.rmap_ref
  13.3 0.0 copy-start.9
  13.3 0.2 select_reduce_fusion.1
  13.5 0.6 pad_add_fusion.1.at_ref
  14.2 0.6 copy.30
  14.7 0.7 broadcast_select_fusion.cinv_ref
  15.4 16.6 %shard_map.37 = (f32[1,4,128,32,128]{4,3,2,1,0:T(8,128)}, f32[4,128,24,128]{3,2,1,0:T(8,128)}, f32[6,512,128]{2,1,0:T(8,128)}) custom-call(s32[3]{0:T(128)} %pad_add_fusion.1.at_ref, s32[2,512]{1,0:T(2,128)} %bitcast.47, f32[1,2,4,128,32,128]{5,4,3,2,1,0:T(8,128)} %sent_ref.1, f32[1,2,4,128,32,128]{5,4,3,2,1,0:T(8,128)} %sent_ref.1, ...), custom_call_target="tpu_custom_call" | custom-call | tf_op jit(solution)/shard_map/pallas_call | solution.py:519
  32.1 0.0 copy-done.2
  32.1 0.0 copy-done.9
  32.1 0.6 pad_add_fusion.2.pick_ref
  32.6 0.1 broadcast_compare_fusion
  32.7 0.6 slice_subtract_fusion.cmap_ref
  33.3 0.7 broadcast_select_fusion.1.diag_ref
  34.0 0.0 collective-permute-done.got_ref
  34.0 0.0 copy-start.4
  34.0 1.0 copy-done.4
  35.0 7.1 %shard_map.38 = (f32[2,512,128]{2,1,0:T(8,128)}, f32[2,512,128]{2,1,0:T(8,128)}, f32[2,512,128]{2,1,0:T(8,128)}, f32[2,128,128]{2,1,0:T(8,128)}) custom-call(s32[2]{0:T(128)} %pad_add_fusion.2.pick_ref, f32[2,2,512,128]{3,2,1,0:T(8,128)} %bitcast.43, f32[2,2,512,128]{3,2,1,0:T(8,128)} %copy-done.4, s32[2,2,4,128]{3,2,1,0:T(4,128)} %copy-done.9, ...), custom_call_target="tpu_custom_call" | custom-call | tf_op jit(solution)/shard_map/pallas_call | solution.py:549
  42.1 55.8 %shard_map.39 = (f32[4,8,2,128,128]{4,3,2,1,0:T(8,128)}, f32[4,2,512,128]{3,2,1,0:T(8,128)}) custom-call(f32[2,128,128]{2,1,0:T(8,128)} %get-tuple-element.29.piece_ref, f32[2,512,128]{2,1,0:T(8,128)} %get-tuple-element.30.even_ref, f32[2,512,128]{2,1,0:T(8,128)} %get-tuple-element.31.odd_ref), custom_call_target="tpu_custom_call" | custom-call | tf_op jit(solution)/shard_map/pallas_call | solution.py:560
  97.9 0.0 all-gather.3.cloned.1.call-update
  97.9 0.1 collective-permute-start.1
  98.0 1.5 collective-permute-start.2
  99.5 0.6 collective-permute-start.5
  100.1 0.0 collective-permute-start.4
  100.1 1.5 collective-permute-start.3
  101.6 0.6 broadcast_select_fusion.2.diag_ref
  102.2 56.2 %shard_map.40 = (f32[1024,1024]{1,0:T(8,128)}, f32[8,128,128]{2,1,0:T(8,128)}) custom-call(f32[4,8,2,128,128]{4,3,2,1,0:T(8,128)} %get-tuple-element.35.s_ref), custom_call_target="tpu_custom_call" | custom-call | tf_op jit(solution)/shard_map/pallas_call | solution.py:589
  158.4 0.0 collective-permute-done.5.far_ref
  158.4 0.0 copy-start.5
  158.4 0.0 collective-permute-done.4.high_ref
  158.4 0.0 copy-start.6
  158.4 0.0 collective-permute-done.3.low_ref
  158.4 0.0 copy-start.7
  158.4 0.8 copy-done.5
  159.2 0.2 copy-done.6
  159.4 0.1 copy-done.7
  159.5 22.6 %shard_map.41 = (f32[2,512,128]{2,1,0:T(8,128)}, f32[512,1024]{1,0:T(8,128)}) custom-call(s32[1]{0:T(128)} %bitcast.16.col_ref, f32[1024,1024]{1,0:T(8,128)} %get-tuple-element.36.l_ref, f32[8,128,128]{2,1,0:T(8,128)} %get-tuple-element.37.li_ref, f32[2,512,128]{2,1,0:T(8,128)} %get-tuple-element.38.own_ref, f32[2,512,128]{2,1,0:T(8,128)} %copy-done.7, ...), custom_call_target="tpu_custom_call" | custom-call | tf_op jit(solution)/shard_map/pallas_call | solution.py:596
  182.1 0.0 all-gather.3.cloned.1.call-done
  182.1 22.0 %shard_map.42.r_ref = f32[4,4096,128]{2,1,0:T(8,128)} custom-call(s32[3]{0:T(128)} %pad_add_fusion.1.at_ref, f32[8,4,2,512,128]{4,3,2,1,0:T(8,128)} %bitcast.41, f32[512,1024]{1,0:T(8,128)} %get-tuple-element.39.x_ref, f32[2,512,128]{2,1,0:T(8,128)} %get-tuple-element.40.y_ref, f32[4,128]{1,0:T(4,128)} %broadcast_select_fusion.2.diag_ref), custom_call_target="tpu_custom_call" | custom-call | tf_op jit(solution)/shard_map/pallas_call | solution.py:607
  204.1 64.8 %collective-permute-done.2.thin_ref = f32[6,512,128]{2,1,0:T(8,128)S(1)} collective-permute-done((f32[6,512,128]{2,1,0:T(8,128)}, f32[6,512,128]{2,1,0:T(8,128)S(1)}, u32[]{:S(2)}, u32[]{:S(2)}) %collective-permute-start.2) | collective-permute-done | bytes 1572896 | tf_op jit(solution)/shard_map/ppermute | solution.py:546
  268.9 0.0 copy-start.3
  268.9 0.0 collective-permute-done.1.got_ref
  268.9 1.2 copy-done.3
  270.1 0.0 copy-start.1
  270.1 15.6 %shard_map.43 = f32[1,4,128,32,128]{4,3,2,1,0:T(8,128)} custom-call(s32[2,512]{1,0:T(2,128)} %bitcast.48, f32[4,128,24,128]{3,2,1,0:T(8,128)} %collective-permute-done.1.got_ref, f32[6,512,128]{2,1,0:T(8,128)} %copy-done.3, s32[2,32,128]{2,1,0:T(8,128)} %broadcast_select_fusion.cinv_ref, f32[1,4,128,32,128]{4,3,2,1,0:T(8,128)} %get-tuple-element.27.kept_ref, ...), custom_call_target="tpu_custom_call" | custom-call | tf_op jit(solution)/shard_map/pallas_call | solution.py:629
  285.7 0.0 copy-done.1
  (12 shorter events, 0.1 us)
Async XLA Ops:
  6.5 6.6 %copy-start = (f32[16384]{0:T(1024)S(1)}, f32[16384]{0:T(1024)}, u32[]{:S(2)}) copy-start(f32[16384]{0:T(1024)} %param.5) | copy-start | bytes 196612
  6.5 4.8 %copy-start.8 = (s32[2,16384]{1,0:T(2,128)S(1)}, s32[2,16384]{1,0:T(2,128)}, u32[]{:S(2)}) copy-start(s32[2,16384]{1,0:T(2,128)} %param.4) | copy-start | bytes 393220
  6.5 175.6 %all-gather.3.cloned.1.call-start = ((), (), s32[]{:S(2)}) async-start(), calls=%async_computation | async-start | bytes 18874368 | tf_op jit(solution)/shard_map/all_gather | solution.py:583
  9.2 22.9 %copy-start.2 = (f32[2,2,4,128,128]{4,3,2,1,0:T(8,128)}, f32[2,2,4,128,128]{4,3,2,1,0:T(8,128)S(1)}, u32[]{:S(2)}) copy-start(f32[2,2,4,128,128]{4,3,2,1,0:T(8,128)S(1)} %copy.20) | copy-start | bytes 3145732
  9.2 24.8 %collective-permute-start = (f32[2,2,512,128]{3,2,1,0:T(8,128)S(1)}, f32[2,2,512,128]{3,2,1,0:T(8,128)S(1)}, u32[]{:S(2)}, u32[]{:S(2)}) collective-permute-start(f32[2,2,512,128]{3,2,1,0:T(8,128)S(1)} %bitcast.42), channel_id=1, source_target_pairs={{0,64},{4,68},{8,72},{12,76},{16,80},{20,84},{24,88},{28,92},{32,9... | collective-permute-start | bytes 3145736 | tf_op jit(solution)/shard_map/ppermute | solution.py:472
  13.3 18.8 %copy-start.9 = (s32[2,2,4,128]{3,2,1,0:T(4,128)}, s32[2,2,4,128]{3,2,1,0:T(4,128)S(1)}, u32[]{:S(2)}) copy-start(s32[2,2,4,128]{3,2,1,0:T(4,128)S(1)} %fusion.rmap_ref) | copy-start | bytes 24580
  34.0 1.0 copy-start.4
  97.9 171.0 %collective-permute-start.1 = (f32[4,128,24,128]{3,2,1,0:T(8,128)}, f32[4,128,24,128]{3,2,1,0:T(8,128)}, u32[]{:S(2)}, u32[]{:S(2)}) collective-permute-start(f32[4,128,24,128]{3,2,1,0:T(8,128)} %get-tuple-element.25), channel_id=1, source_target_pairs={{0,64},{4,68},{8,72},{12,76},{16,80},{20,84},{24,88},{28,92},{32,9... | collective-permute-start | bytes 18874376 | tf_op jit(solution)/shard_map/ppermute | solution.py:546
  98.0 170.9 %collective-permute-start.2 = (f32[6,512,128]{2,1,0:T(8,128)}, f32[6,512,128]{2,1,0:T(8,128)S(1)}, u32[]{:S(2)}, u32[]{:S(2)}) collective-permute-start(f32[6,512,128]{2,1,0:T(8,128)} %get-tuple-element.26), channel_id=1, source_target_pairs={{0,64},{4,68},{8,72},{12,76},{16,80},{20,84},{24,88},{28,92},{32,9... | collective-permute-start | bytes 4718600 | tf_op jit(solution)/shard_map/ppermute | solution.py:546
  99.5 58.9 %collective-permute-start.5 = (f32[2,512,128]{2,1,0:T(8,128)}, f32[2,512,128]{2,1,0:T(8,128)S(1)}, u32[]{:S(2)}, u32[]{:S(2)}) collective-permute-start(f32[2,512,128]{2,1,0:T(8,128)} %get-tuple-element.38.own_ref), channel_id=1, source_target_pairs={{0,2},{1,3},{2,0},{3,1},{4,6},{5,7},{6,4},{7,5},{8,10},{9,11},{10,... | collective-permute-start | bytes 1572872 | tf_op jit(solution)/shard_map/ppermute | solution.py:587
  100.1 58.3 %collective-permute-start.4 = (f32[2,512,128]{2,1,0:T(8,128)}, f32[2,512,128]{2,1,0:T(8,128)S(1)}, u32[]{:S(2)}, u32[]{:S(2)}) collective-permute-start(f32[2,512,128]{2,1,0:T(8,128)} %get-tuple-element.38.own_ref), channel_id=1, source_target_pairs={{0,3},{1,0},{2,1},{3,2},{4,7},{5,4},{6,5},{7,6},{8,11},{9,8},{10,9... | collective-permute-start | bytes 1572872 | tf_op jit(solution)/shard_map/ppermute | solution.py:587
  100.1 58.4 %collective-permute-start.3 = (f32[2,512,128]{2,1,0:T(8,128)}, f32[2,512,128]{2,1,0:T(8,128)S(1)}, u32[]{:S(2)}, u32[]{:S(2)}) collective-permute-start(f32[2,512,128]{2,1,0:T(8,128)} %get-tuple-element.38.own_ref), channel_id=1, source_target_pairs={{0,1},{1,2},{2,3},{3,0},{4,5},{5,6},{6,7},{7,4},{8,9},{9,10},{10,1... | collective-permute-start | bytes 1572872 | tf_op jit(solution)/shard_map/ppermute | solution.py:587
  158.4 0.8 copy-start.5
  158.4 1.0 copy-start.6
  158.4 1.1 copy-start.7
  268.9 1.2 copy-start.3
  270.1 15.6 %copy-start.1 = (f32[16384]{0:T(1024)S(1)}, f32[16384]{0:T(1024)}, u32[]{:S(2)}) copy-start(f32[16384]{0:T(1024)} %param.5) | copy-start | bytes 196612
Sparse Core Ops, SparseCore 0:
  98.1 80.8 all-gather.2

commit v9 on v8

--- a/solution.py
+++ b/solution.py
@@ -136,6 +136,16 @@
             for i, peer in enumerate(mates):
                 copy(col, mine, i, peer, zz + 1).start()
 
+    for m in range(4):
+
+        @pl.when(stays(m))
+        def _():
+            keep_quarter(m).start()
+
+        @pl.when(jnp.logical_not(stays(m)))
+        def _():
+            quarter(m).start()
+
     for zz in range(2):
         p = zz * 4 + row
         n = zz
@@ -156,16 +166,6 @@
         copy(col, p, 11 + n, sides[0], zz + 1).start()
         copy(col, p, 13 + n, sides[1], zz + 1).start()
         copy(col, p, 15 + n, other, zz + 1).start()
-    for m in range(4):
-
-        @pl.when(stays(m))
-        def _():
-            keep_quarter(m).start()
-
-        @pl.when(jnp.logical_not(stays(m)))
-        def _():
-            quarter(m).start()
-
     for i, who in enumerate((row, opposite)):
         for zz in range(2):
             p = zz * 4 + who
@@ -356,14 +356,14 @@
     return high, (x - high.astype(F32)).astype(jnp.bfloat16)
 
 
-def place_rows(tile, t, rinv_ref, cinv_ref, load, less, out_ref):
+def place_rows(tile, first, t, rinv_ref, cinv_ref, load, less, out_ref):
     groups = range(0, out_ref.shape[-2], 8)
     index = [jnp.maximum(cinv_ref[t, g : g + 8], 0) for g in groups]
     live = [(cinv_ref[t, g : g + 8] >= 0).astype(F32) for g in groups]
-    base = tile * TB
+    count = out_ref.shape[0]
 
     def body(o, _):
-        s = rinv_ref[t, base + o]
+        s = rinv_ref[t, tile * TB + first + o]
         weight = jnp.where(s >= 0, 1.0, 0.0)
         s = jnp.maximum(s, 0)
         for g, at, keep in zip(groups, index, live):
@@ -371,7 +371,7 @@
             out_ref[o, g : g + 8] = x if less is None else x + less(o, g)
         return 0
 
-    lax.fori_loop(0, TB, body, 0, unroll=16)
+    lax.fori_loop(0, count, body, 0, unroll=16)
 
 
 def keep_kernel(
@@ -384,7 +384,7 @@
     def load(s, g):
         return kept_ref[0, 0, 0, s, g : g + 8]
 
-    place_rows(pl.program_id(0), 0, rinv_ref, cinv_ref, load, None, out_ref.at[0, 0])
+    place_rows(pl.program_id(0), 0, 0, rinv_ref, cinv_ref, load, None, out_ref.at[0, 0])
 
 
 def finish_kernel(
@@ -394,6 +394,7 @@
     def _():
         first_ref[: 2 * TB, :] = jnp.zeros((2 * TB, TB), F32)
 
+    tile, first = pl.program_id(0) // 2, lax.rem(pl.program_id(0), 2) * (TB // 2)
     for v in range(2, 8):
         first_ref[v * TB : (v + 1) * TB, :] = thin_ref[v - 2]
 
@@ -403,9 +404,9 @@
         return got_ref[0, s, g - 8 : g]
 
     def less(o, g):
-        return kept_ref[0, 0, o, g : g + 8] - r_ref.at[0][pl.ds(g * TB + o, 8, stride=TB), :]
-
-    place_rows(pl.program_id(0), 1, rinv_ref, cinv_ref, load, less, out_ref.at[0, 0])
+        return kept_ref[0, 0, o, g : g + 8] - r_ref.at[0][pl.ds(g * TB + first + o, 8, stride=TB), :]
+
+    place_rows(tile, first, 1, rinv_ref, cinv_ref, load, less, out_ref.at[0, 0])
 
 
 def update_kernel(
@@ -625,19 +626,19 @@
             ],
         ),
     )(at, others, x, y, trailing_diag)
-    own_block = pl.BlockSpec((1, 1, TB, cols, TB), lambda i, *_: (0, i, 0, 0, 0))
+    own_block = pl.BlockSpec((1, 1, TB // 2, cols, TB), lambda i, *_: (0, i // 2, i % 2, 0, 0))
     return pl.pallas_call(
         finish_kernel,
         out_shape=whole,
         grid_spec=pltpu.PrefetchScalarGridSpec(
             num_scalar_prefetch=1,
-            grid=(tiles,),
+            grid=(2 * tiles,),
             in_specs=[
-                pl.BlockSpec((1, TB, cols - 8, TB), lambda i, *_: (i, 0, 0, 0)),
-                pl.BlockSpec((6, TB, TB), lambda i, *_: (0, i, 0)),
+                pl.BlockSpec((1, TB, cols - 8, TB), lambda i, *_: (i // 2, 0, 0, 0)),
+                pl.BlockSpec((6, TB, TB), lambda i, *_: (0, i // 2, 0)),
                 all_maps,
                 own_block,
-                pl.BlockSpec((1, cols * TB, TB), lambda i, *_: (i, 0, 0)),
+                pl.BlockSpec((1, cols * TB, TB), lambda i, *_: (i // 2, 0, 0)),
             ],
             out_specs=own_block,
             scratch_shapes=[pltpu.VMEM((8 * TB, TB), F32)],

time: 293 us -> 291 us (level)
  Pallas kernels: 196 us -> 193 us
    pallas_call x1, Pallas kernels: 55.8 us -> 49.7 us  [on_device(): pl.pallas_call(pivot_kernel, out_shape=[jax.ShapeDtypeStruct((4, 8, 2, TB...]
    pallas_call x1, Pallas kernels: 15.6 us -> 19.6 us  [on_device(): pl.pallas_call(finish_kernel, out_shape=whole, grid_spec=pltpu.PrefetchSc...]
where the time goes in v9:
time: 291 us; the launch traced here: 290 us
  Pallas kernels  193 us (66%)
  waiting for transfers between devices  64.5 us (22%)
  between operations  13.6 us (5%)
  local copies, waits for them, and re-layouts  6.92 us (2%)
  starting transfers between devices  6.77 us (2%)
  other arithmetic  5.56 us (2%)
    ppermute x2, waiting for transfers between devices, on_device(): arrived.append(lax.ppermute(part, ('cube', 'row'), trade))  64.5 us
    pallas_call x1, Pallas kernels, on_device(): pl.pallas_call(factor_kernel, out_shape=[jax.ShapeDtypeStruct((K, K), F32...  55.7 us
    pallas_call x1, Pallas kernels, on_device(): pl.pallas_call(pivot_kernel, out_shape=[jax.ShapeDtypeStruct((4, 8, 2, TB...  49.7 us
    pallas_call x1, Pallas kernels, on_device(): pl.pallas_call(solve_kernel, out_shape=[jax.ShapeDtypeStruct((2, rows, TB...  22.4 us
    pallas_call x1, Pallas kernels, on_device(): pl.pallas_call(update_kernel, out_shape=jax.ShapeDtypeStruct((tiles, cols...  22 us
    pallas_call x1, Pallas kernels, on_device(): pl.pallas_call(finish_kernel, out_shape=whole, grid_spec=pltpu.PrefetchSc...  19.6 us
    pallas_call x1, Pallas kernels, on_device(): pl.pallas_call(keep_kernel, out_shape=[whole, jax.ShapeDtypeStruct((tiles...  16.6 us
    pallas_call x1, Pallas kernels, on_device(): pl.pallas_call(place_kernel, out_shape=[strip, strip, strip, jax.ShapeDty...  7.05 us
  transfers between devices with their start and end apart: 7, of which 1 were waited for; matrix products, arithmetic and copies ran while one was open for 2% of the time, Pallas kernels for 40%

profile of v9, /device:TPU:1, one launch (start us, length us, event | category | flops | bytes accessed | tf_op | source)
XLA Modules:
  0.0 290.3 jit_solution(11847202600530161177)
XLA Ops:
  6.5 0.0 copy-start
  6.5 0.0 copy-start.8
  6.5 0.0 all-gather.3.cloned.1.call-start
  6.5 2.5 slice_bitcast_fusion
  9.1 0.1 copy.20
  9.2 0.0 copy-start.2
  9.2 2.1 collective-permute-start
  11.4 0.0 copy-done.8
  11.4 0.1 constant_dynamic-slice_fusion.5
  11.5 0.1 pad_add_fusion
  11.7 0.1 reshape.114
  11.8 0.1 subtract_bitcast_fusion
  11.9 1.2 select_reduce_fusion
  13.1 0.0 copy-done
  13.2 0.1 broadcast_multiply_fusion
  13.2 0.1 fusion.rmap_ref
  13.3 0.0 copy-start.9
  13.3 0.2 select_reduce_fusion.1
  13.5 0.6 pad_add_fusion.1.at_ref
  14.2 0.6 copy.30
  14.7 0.7 broadcast_select_fusion.cinv_ref
  15.4 16.6 %shard_map.37 = (f32[1,4,128,32,128]{4,3,2,1,0:T(8,128)}, f32[4,128,24,128]{3,2,1,0:T(8,128)}, f32[6,512,128]{2,1,0:T(8,128)}) custom-call(s32[3]{0:T(128)} %pad_add_fusion.1.at_ref, s32[2,512]{1,0:T(2,128)} %bitcast.47, f32[1,2,4,128,32,128]{5,4,3,2,1,0:T(8,128)} %sent_ref.1, f32[1,2,4,128,32,128]{5,4,3,2,1,0:T(8,128)} %sent_ref.1, ...), custom_call_target="tpu_custom_call" | custom-call | tf_op jit(solution)/shard_map/pallas_call | solution.py:520
  32.0 0.0 copy-done.2
  32.1 0.0 copy-done.9
  32.1 0.6 pad_add_fusion.2.pick_ref
  32.6 0.1 broadcast_compare_fusion
  32.7 0.6 slice_subtract_fusion.cmap_ref
  33.3 0.7 broadcast_select_fusion.1.diag_ref
  34.0 0.0 collective-permute-done.got_ref
  34.0 0.0 copy-start.4
  34.0 1.0 copy-done.4
  35.0 7.0 %shard_map.38 = (f32[2,512,128]{2,1,0:T(8,128)}, f32[2,512,128]{2,1,0:T(8,128)}, f32[2,512,128]{2,1,0:T(8,128)}, f32[2,128,128]{2,1,0:T(8,128)}) custom-call(s32[2]{0:T(128)} %pad_add_fusion.2.pick_ref, f32[2,2,512,128]{3,2,1,0:T(8,128)} %bitcast.43, f32[2,2,512,128]{3,2,1,0:T(8,128)} %copy-done.4, s32[2,2,4,128]{3,2,1,0:T(4,128)} %copy-done.9, ...), custom_call_target="tpu_custom_call" | custom-call | tf_op jit(solution)/shard_map/pallas_call | solution.py:550
  42.1 49.7 %shard_map.39 = (f32[4,8,2,128,128]{4,3,2,1,0:T(8,128)}, f32[4,2,512,128]{3,2,1,0:T(8,128)}) custom-call(f32[2,128,128]{2,1,0:T(8,128)} %get-tuple-element.29.piece_ref, f32[2,512,128]{2,1,0:T(8,128)} %get-tuple-element.30.even_ref, f32[2,512,128]{2,1,0:T(8,128)} %get-tuple-element.31.odd_ref), custom_call_target="tpu_custom_call" | custom-call | tf_op jit(solution)/shard_map/pallas_call | solution.py:561
  91.7 0.0 all-gather.3.cloned.1.call-update
  91.8 1.1 collective-permute-start.1
  92.9 0.4 collective-permute-start.2
  93.3 1.6 collective-permute-start.5
  94.9 1.2 collective-permute-start.4
  96.2 0.3 collective-permute-start.3
  96.4 0.6 broadcast_select_fusion.2.diag_ref
  97.0 55.7 %shard_map.40 = (f32[1024,1024]{1,0:T(8,128)}, f32[8,128,128]{2,1,0:T(8,128)}) custom-call(f32[4,8,2,128,128]{4,3,2,1,0:T(8,128)} %get-tuple-element.35.s_ref), custom_call_target="tpu_custom_call" | custom-call | tf_op jit(solution)/shard_map/pallas_call | solution.py:590
  152.7 0.0 collective-permute-done.5.far_ref
  152.7 0.0 copy-start.5
  152.7 0.0 collective-permute-done.4.high_ref
  152.7 0.0 copy-start.6
  152.8 0.0 collective-permute-done.3.low_ref
  152.8 0.0 copy-start.7
  152.8 0.8 copy-done.5
  153.6 0.2 copy-done.6
  153.7 0.1 copy-done.7
  153.9 22.4 %shard_map.41 = (f32[2,512,128]{2,1,0:T(8,128)}, f32[512,1024]{1,0:T(8,128)}) custom-call(s32[1]{0:T(128)} %bitcast.16.col_ref, f32[1024,1024]{1,0:T(8,128)} %get-tuple-element.36.l_ref, f32[8,128,128]{2,1,0:T(8,128)} %get-tuple-element.37.li_ref, f32[2,512,128]{2,1,0:T(8,128)} %get-tuple-element.38.own_ref, f32[2,512,128]{2,1,0:T(8,128)} %copy-done.7, ...), custom_call_target="tpu_custom_call" | custom-call | tf_op jit(solution)/shard_map/pallas_call | solution.py:597
  176.3 0.0 all-gather.3.cloned.1.call-done
  176.3 22.0 %shard_map.42.r_ref = f32[4,4096,128]{2,1,0:T(8,128)} custom-call(s32[3]{0:T(128)} %pad_add_fusion.1.at_ref, f32[8,4,2,512,128]{4,3,2,1,0:T(8,128)} %bitcast.41, f32[512,1024]{1,0:T(8,128)} %get-tuple-element.39.x_ref, f32[2,512,128]{2,1,0:T(8,128)} %get-tuple-element.40.y_ref, f32[4,128]{1,0:T(4,128)} %broadcast_select_fusion.2.diag_ref), custom_call_target="tpu_custom_call" | custom-call | tf_op jit(solution)/shard_map/pallas_call | solution.py:608
  198.3 64.5 %collective-permute-done.2.thin_ref = f32[6,512,128]{2,1,0:T(8,128)S(1)} collective-permute-done((f32[6,512,128]{2,1,0:T(8,128)}, f32[6,512,128]{2,1,0:T(8,128)S(1)}, u32[]{:S(2)}, u32[]{:S(2)}) %collective-permute-start.2) | collective-permute-done | bytes 1572896 | tf_op jit(solution)/shard_map/ppermute | solution.py:547
  262.7 0.0 copy-start.3
  262.7 0.0 collective-permute-done.1.got_ref
  262.7 1.2 copy-done.3
  263.9 0.0 copy-start.1
  263.9 19.6 %shard_map.43 = f32[1,4,128,32,128]{4,3,2,1,0:T(8,128)} custom-call(s32[2,512]{1,0:T(2,128)} %bitcast.48, f32[4,128,24,128]{3,2,1,0:T(8,128)} %collective-permute-done.1.got_ref, f32[6,512,128]{2,1,0:T(8,128)} %copy-done.3, s32[2,32,128]{2,1,0:T(8,128)} %broadcast_select_fusion.cinv_ref, f32[1,4,128,32,128]{4,3,2,1,0:T(8,128)} %get-tuple-element.27.kept_ref, ...), custom_call_target="tpu_custom_call" | custom-call | tf_op jit(solution)/shard_map/pallas_call | solution.py:630
  283.5 0.0 copy-done.1
  (12 shorter events, 0.1 us)
Async XLA Ops:
  6.5 6.6 %copy-start = (f32[16384]{0:T(1024)S(1)}, f32[16384]{0:T(1024)}, u32[]{:S(2)}) copy-start(f32[16384]{0:T(1024)} %param.5) | copy-start | bytes 196612
  6.5 4.8 %copy-start.8 = (s32[2,16384]{1,0:T(2,128)S(1)}, s32[2,16384]{1,0:T(2,128)}, u32[]{:S(2)}) copy-start(s32[2,16384]{1,0:T(2,128)} %param.4) | copy-start | bytes 393220
  6.5 169.8 %all-gather.3.cloned.1.call-start = ((), (), s32[]{:S(2)}) async-start(), calls=%async_computation | async-start | bytes 18874368 | tf_op jit(solution)/shard_map/all_gather | solution.py:584
  9.2 22.9 %copy-start.2 = (f32[2,2,4,128,128]{4,3,2,1,0:T(8,128)}, f32[2,2,4,128,128]{4,3,2,1,0:T(8,128)S(1)}, u32[]{:S(2)}) copy-start(f32[2,2,4,128,128]{4,3,2,1,0:T(8,128)S(1)} %copy.20) | copy-start | bytes 3145732
  9.2 24.8 %collective-permute-start = (f32[2,2,512,128]{3,2,1,0:T(8,128)S(1)}, f32[2,2,512,128]{3,2,1,0:T(8,128)S(1)}, u32[]{:S(2)}, u32[]{:S(2)}) collective-permute-start(f32[2,2,512,128]{3,2,1,0:T(8,128)S(1)} %bitcast.42), channel_id=1, source_target_pairs={{0,64},{4,68},{8,72},{12,76},{16,80},{20,84},{24,88},{28,92},{32,9... | collective-permute-start | bytes 3145736 | tf_op jit(solution)/shard_map/ppermute | solution.py:473
  13.3 18.7 %copy-start.9 = (s32[2,2,4,128]{3,2,1,0:T(4,128)}, s32[2,2,4,128]{3,2,1,0:T(4,128)S(1)}, u32[]{:S(2)}) copy-start(s32[2,2,4,128]{3,2,1,0:T(4,128)S(1)} %fusion.rmap_ref) | copy-start | bytes 24580
  34.0 1.0 copy-start.4
  91.8 171.0 %collective-permute-start.1 = (f32[4,128,24,128]{3,2,1,0:T(8,128)}, f32[4,128,24,128]{3,2,1,0:T(8,128)}, u32[]{:S(2)}, u32[]{:S(2)}) collective-permute-start(f32[4,128,24,128]{3,2,1,0:T(8,128)} %get-tuple-element.25), channel_id=1, source_target_pairs={{0,64},{4,68},{8,72},{12,76},{16,80},{20,84},{24,88},{28,92},{32,9... | collective-permute-start | bytes 18874376 | tf_op jit(solution)/shard_map/ppermute | solution.py:547
  92.9 169.9 %collective-permute-start.2 = (f32[6,512,128]{2,1,0:T(8,128)}, f32[6,512,128]{2,1,0:T(8,128)S(1)}, u32[]{:S(2)}, u32[]{:S(2)}) collective-permute-start(f32[6,512,128]{2,1,0:T(8,128)} %get-tuple-element.26), channel_id=1, source_target_pairs={{0,64},{4,68},{8,72},{12,76},{16,80},{20,84},{24,88},{28,92},{32,9... | collective-permute-start | bytes 4718600 | tf_op jit(solution)/shard_map/ppermute | solution.py:547
  93.3 59.4 %collective-permute-start.5 = (f32[2,512,128]{2,1,0:T(8,128)}, f32[2,512,128]{2,1,0:T(8,128)S(1)}, u32[]{:S(2)}, u32[]{:S(2)}) collective-permute-start(f32[2,512,128]{2,1,0:T(8,128)} %get-tuple-element.38.own_ref), channel_id=1, source_target_pairs={{0,2},{1,3},{2,0},{3,1},{4,6},{5,7},{6,4},{7,5},{8,10},{9,11},{10,... | collective-permute-start | bytes 1572872 | tf_op jit(solution)/shard_map/ppermute | solution.py:588
  94.9 57.8 %collective-permute-start.4 = (f32[2,512,128]{2,1,0:T(8,128)}, f32[2,512,128]{2,1,0:T(8,128)S(1)}, u32[]{:S(2)}, u32[]{:S(2)}) collective-permute-start(f32[2,512,128]{2,1,0:T(8,128)} %get-tuple-element.38.own_ref), channel_id=1, source_target_pairs={{0,3},{1,0},{2,1},{3,2},{4,7},{5,4},{6,5},{7,6},{8,11},{9,8},{10,9... | collective-permute-start | bytes 1572872 | tf_op jit(solution)/shard_map/ppermute | solution.py:588
  96.2 56.6 %collective-permute-start.3 = (f32[2,512,128]{2,1,0:T(8,128)}, f32[2,512,128]{2,1,0:T(8,128)S(1)}, u32[]{:S(2)}, u32[]{:S(2)}) collective-permute-start(f32[2,512,128]{2,1,0:T(8,128)} %get-tuple-element.38.own_ref), channel_id=1, source_target_pairs={{0,1},{1,2},{2,3},{3,0},{4,5},{5,6},{6,7},{7,4},{8,9},{9,10},{10,1... | collective-permute-start | bytes 1572872 | tf_op jit(solution)/shard_map/ppermute | solution.py:588
  152.7 0.8 copy-start.5
  152.7 1.0 copy-start.6
  152.8 1.1 copy-start.7
  262.7 1.2 copy-start.3
  263.9 19.6 %copy-start.1 = (f32[16384]{0:T(1024)S(1)}, f32[16384]{0:T(1024)}, u32[]{:S(2)}) copy-start(f32[16384]{0:T(1024)} %param.5) | copy-start | bytes 196612
Sparse Core Ops, SparseCore 0:
  91.9 84.2 all-gather.2
